TPU v7x, 256 devices: a whole 4x4x8 slice. The times are simulated.
256 devices in a mesh: snap: 32 (over z_hi, x, y), vert: 8 (over z_lo, core).
Axes of the slice: x: 4, y: 4, z: 8 (z_hi: 2, z_lo: 4; z = z_hi * 4 + z_lo), core: 2. Of those that a mesh axis runs over, the one named last changes fastest.
Arguments:
- features: bfloat16 [64, 8192, 128], P('snap', 'vert'), may hold values from -6 to 6
- tile_cols: int32 [64, 64, 8], P('snap', 'vert'), may hold values from 0 to 63
- tile_weights: int32 [64, 64, 8, 128, 128], P('snap', 'vert'), may hold values from 0 to 3
- graph_gain: float32 [2, 128], replicated, may hold values from 0.5 to 1.5
- graph_up: bfloat16 [2, 128, 512], replicated, may hold values from -0.5 to 0.5
- graph_down: bfloat16 [2, 512, 128], replicated, may hold values from -0.25 to 0.25
- lag_mix: float32 [2, 8, 128], replicated, may hold values from -2 to 2
- time_gain: float32 [2, 128], replicated, may hold values from 0.5 to 1.5
- time_up: bfloat16 [2, 128, 1024], replicated, may hold values from -0.5 to 0.5
- time_down: bfloat16 [2, 1024, 128], replicated, may hold values from -0.1875 to 0.1875
Outputs:
- result: bfloat16 [64, 8192, 128], P('snap', 'vert')
All inputs are finite; a program needn't handle non-finite values.
Results may differ from a plain program's by a relative error of at most 0.0085.
Values may be sent and summed in bfloat16 or wider, within the bound.
No kernel may reach another device: no remote copies, remote signals or barrier semaphores. Data moves between devices by JAX's collectives and lax.ppermute only.
A program may use at most 64 MiB of HBM per device.

v0:
```python
import jax
import jax.numpy as jnp
from jax import lax
from jax.sharding import PartitionSpec as P

eps = 1e-06


def rms_scale(activation, gain_row):
    return (
        activation
        * lax.rsqrt(jnp.mean(activation * activation, axis=-1, keepdims=True) + eps)
        * gain_row
    )


def mlp_branch(residual, mixed_rows, gain_row, up_weight, down_weight):
    feature_width = residual.shape[-1]
    normed = rms_scale(mixed_rows, gain_row).astype(jnp.bfloat16).reshape(-1, feature_width)
    hidden = jax.nn.gelu(jnp.dot(normed, up_weight, preferred_element_type=jnp.float32)).astype(
        jnp.bfloat16
    )
    branch = jnp.dot(hidden, down_weight, preferred_element_type=jnp.float32).reshape(
        residual.shape
    )
    return (residual.astype(jnp.float32) + branch).astype(jnp.bfloat16)


def lagged(sequence, lag_rows, before, out_count):
    widened = sequence.astype(jnp.float32)
    running = jnp.zeros((out_count,) + sequence.shape[1:], jnp.float32)
    for lag_step in range(lag_rows.shape[0]):
        running = running + lag_rows[lag_step] * lax.slice_in_dim(
            widened, before - lag_step, before - lag_step + out_count, axis=0
        )
    return running


def aggregate(snapshot, columns, blocks):
    tile_size = blocks.shape[-1]
    feature_width = snapshot.shape[-1]
    stacked = snapshot.reshape(-1, tile_size, feature_width)
    picked = stacked[columns]
    product = jnp.einsum("rkij,rkjf->rif", blocks, picked, preferred_element_type=jnp.float32)
    return product.reshape(-1, feature_width)


def on_device(
    features,
    tile_cols,
    tile_weights,
    graph_gain,
    graph_up,
    graph_down,
    lag_mix,
    time_gain,
    time_up,
    time_down,
):
    blocks = tile_weights.astype(jnp.bfloat16)
    state = features
    owners = lax.axis_size("snap")
    snap_dev, vert_dev, feature_width = features.shape
    lag_count = lag_mix.shape[1]
    for layer_index in range(graph_up.shape[0]):
        gathered = lax.all_gather(state, "vert", axis=1, tiled=True)
        summed = jax.vmap(aggregate)(gathered, tile_cols, blocks)
        graph_out = mlp_branch(
            state, summed, graph_gain[layer_index], graph_up[layer_index], graph_down[layer_index]
        )
        grouped = graph_out.reshape(snap_dev, owners, vert_dev // owners, feature_width)
        owned_rows = lax.all_to_all(grouped, "snap", split_axis=1, concat_axis=0, tiled=True)
        padded = jnp.concatenate(
            [jnp.zeros((lag_count - 1,) + owned_rows.shape[1:], jnp.bfloat16), owned_rows], axis=0
        )
        mixed_rows = lagged(padded, lag_mix[layer_index], lag_count - 1, owned_rows.shape[0])
        finished = mlp_branch(
            owned_rows,
            mixed_rows,
            time_gain[layer_index],
            time_up[layer_index],
            time_down[layer_index],
        )
        state = lax.all_to_all(finished, "snap", split_axis=0, concat_axis=1, tiled=True).reshape(
            snap_dev, vert_dev, feature_width
        )
    return state


def solution(mesh):
    return jax.shard_map(
        on_device,
        mesh=mesh,
        in_specs=(
            P("snap", "vert", None),
            P("snap", "vert", None),
            P("snap", "vert", None, None, None),
            P(),
            P(),
            P(),
            P(),
            P(),
            P(),
            P(),
        ),
        out_specs=P("snap", "vert", None),
        check_vma=False,
    )
```

profile of v0, /device:TPU:32, one launch (start us, length us, event | category | flops | bytes accessed | tf_op | source)
XLA Modules:
  0.0 265.0 jit_solution(5932802984013628403)
XLA Ops:
  6.5 0.7 all-gather.3.cloned.1.call-update
  7.3 0.7 fusion.81
  8.0 0.8 slice_bitcast_fusion.9
  8.8 53.5 %all-gather.3.cloned.1.call-done = bf16[2,8192,128]{2,1,0:T(8,128)(2,1)} async-done(((bf16[2,1024,128]{2,1,0:T(8,128)(2,1)}), bf16[2,8192,128]{2,1,0:T(8,128)(2,1)}) %all-gather.3.cloned.1.call-update) | async-done | bytes 4194320 | tf_op jit(solution)/shard_map/all_gather | solution.py:66
  62.3 5.3 %gather_fusion = bf16[128,128,128]{2,1,0:T(8,128)(2,1)} fusion(bf16[2,64,128,128]{3,2,1,0:T(8,128)(2,1)} %bitcast.150, s32[128]{0:T(128)S(1)} %reshape.226), kind=kCustom, calls=%fused_computation | custom fusion | bytes 8389632 | tf_op jit(solution)/shard_map/vmap()/gather | solution.py:43
  67.6 5.9 %multiply_reduce_fusion.3 = (f32[2,8,128]{2,1,0:T(8,128)S(1)}, f32[2,8,128,128]{2,3,1,0:T(8,128)S(1)}) fusion(bf16[2,8,8,128,128]{4,3,2,1,0:T(8,128)(2,1)} %bitcast.143, s32[2,8,8,128,128]{4,3,2,1,0:T(8,128)} %param.12), kind=kOutput, calls=%fused_computation.91 | convolution fusion | flops 539490304 | bytes 13639680 | tf_op jit(solution)/shard_map/vmap(rkij,rkjf->rif)/dot_general | solution.py:44
  73.5 0.3 multiply_convert_fusion.3
  73.9 1.4 fusion.23
  75.4 0.7 fusion.42
  76.1 0.9 copy.19
  77.0 13.4 %all-to-all-start = ((bf16[2,32,32,128]{3,2,0,1:T(8,128)(2,1)}), bf16[2,32,32,128]{3,2,0,1:T(8,128)(2,1)S(1)}, u32[]{:S(2)}, u32[]{:S(2)}) async-start(bf16[2,32,32,128]{3,2,0,1:T(8,128)(2,1)} %copy.19), calls=%async_computation | async-start | bytes 1048576 | tf_op jit(solution)/shard_map/all_to_all | solution.py:72
  90.5 20.3 %all-to-all-done = bf16[2,32,32,128]{3,2,0,1:T(8,128)(2,1)S(1)} async-done(((bf16[2,32,32,128]{3,2,0,1:T(8,128)(2,1)}), bf16[2,32,32,128]{3,2,0,1:T(8,128)(2,1)S(1)}, u32[]{:S(2)}, u32[]{:S(2)}) %all-to-all-start) | async-done | bytes 524320 | tf_op jit(solution)/shard_map/all_to_all | solution.py:72
  111.0 0.7 multiply_reduce_fusion.2
  111.7 0.3 multiply_convert_fusion.2
  112.0 2.9 %fusion.7 = bf16[2048,1024]{1,0:T(8,128)(2,1)S(1)} fusion(bf16[2048,128]{1,0:T(8,128)(2,1)S(1)} %bitcast.161, bf16[2,128,1024]{2,1,0:T(8,128)(2,1)S(1)} %copy-done.6), kind=kOutput, calls=%fused_computation.11 | convolution fusion | flops 555745280 | bytes 4980736 | tf_op jit(solution)/shard_map/dot_general | solution.py:20
  115.0 1.3 fusion.47
  116.3 20.8 %all_to_all.66 = bf16[64,1,32,128]{3,2,1,0:T(8,128)(2,1)S(1)} all-to-all(bf16[64,1,32,128]{3,2,1,0:T(8,128)(2,1)S(1)} %fusion.47), channel_id=1, replica_groups=mesh['snap'=32,'vert'=8] {'snap'}, dimensions={0} | all-to-all | bytes 1048576 | tf_op jit(solution)/shard_map/all_to_all | solution.py:84
  137.0 0.8 copy.21
  137.9 45.9 %all-gather.5.cloned.1.call-done = bf16[2,8192,128]{2,1,0:T(8,128)(2,1)} async-done(((bf16[2,1024,128]{2,1,0:T(8,128)(2,1)}), bf16[2,8192,128]{2,1,0:T(8,128)(2,1)}) %all-gather.5.cloned.1.call-update) | async-done | bytes 4194320 | tf_op jit(solution)/shard_map/all_gather | solution.py:66
  183.8 5.3 %gather_fusion.1 = bf16[128,128,128]{2,1,0:T(8,128)(2,1)} fusion(bf16[2,64,128,128]{3,2,1,0:T(8,128)(2,1)} %bitcast.151, s32[128]{0:T(128)S(1)} %reshape.226), kind=kCustom, calls=%fused_computation.1 | custom fusion | bytes 8389632 | tf_op jit(solution)/shard_map/vmap()/gather | solution.py:43
  189.1 5.9 %multiply_reduce_fusion.1 = (f32[2,8,128]{2,1,0:T(8,128)S(1)}, f32[2,8,128,128]{2,3,1,0:T(8,128)S(1)}) fusion(bf16[2,8,8,128,128]{4,3,2,1,0:T(8,128)(2,1)} %bitcast.142, s32[2,8,8,128,128]{4,3,2,1,0:T(8,128)} %param.12), kind=kOutput, calls=%fused_computation.87 | convolution fusion | flops 539490304 | bytes 13639680 | tf_op jit(solution)/shard_map/vmap(rkij,rkjf->rif)/dot_general | solution.py:44
  195.0 0.3 multiply_convert_fusion.1
  195.4 1.4 fusion.31
  196.8 0.7 fusion.43
  197.6 33.7 %all_to_all.67 = bf16[2,32,32,128]{3,2,0,1:T(8,128)(2,1)S(1)} all-to-all(bf16[2,32,32,128]{3,2,0,1:T(8,128)(2,1)S(1)} %copy.22), channel_id=1, replica_groups=mesh['snap'=32,'vert'=8] {'snap'}, dimensions={1} | all-to-all | bytes 1048576 | tf_op jit(solution)/shard_map/all_to_all | solution.py:72
  231.2 0.1 pad_convert_fusion
  231.4 0.7 multiply_reduce_fusion
  232.1 0.3 multiply_convert_fusion
  232.4 2.9 %fusion.15 = bf16[2048,1024]{1,0:T(8,128)(2,1)S(1)} fusion(bf16[2048,128]{1,0:T(8,128)(2,1)S(1)} %bitcast.163, bf16[2,128,1024]{2,1,0:T(8,128)(2,1)S(1)} %copy-done.6), kind=kOutput, calls=%fused_computation.19 | convolution fusion | flops 555745280 | bytes 4980736 | tf_op jit(solution)/shard_map/dot_general | solution.py:20
  235.3 1.3 fusion.46
  236.6 20.8 %all_to_all.68 = bf16[64,1,32,128]{3,2,1,0:T(8,128)(2,1)S(1)} all-to-all(bf16[64,1,32,128]{3,2,1,0:T(8,128)(2,1)S(1)} %fusion.46), channel_id=1, replica_groups=mesh['snap'=32,'vert'=8] {'snap'}, dimensions={0} | all-to-all | bytes 1048576 | tf_op jit(solution)/shard_map/all_to_all | solution.py:84
  257.3 0.8 copy.24
  (28 shorter events, 0.4 us)
Async XLA Ops:
  6.5 55.8 %all-gather.3.cloned.1.call-start = ((), (), s32[]{:S(2)}) async-start(), calls=%async_computation.4 | async-start | bytes 4718592 | tf_op jit(solution)/shard_map/all_gather | solution.py:66
  67.6 6.3 %copy-start.7 = (bf16[2,128,512]{2,1,0:T(8,128)(2,1)S(1)}, bf16[2,128,512]{2,1,0:T(8,128)(2,1)}, u32[]{:S(2)}) copy-start(bf16[2,128,512]{2,1,0:T(8,128)(2,1)} %param.14) | copy-start | bytes 786436
  73.9 1.5 copy-start.1
  73.9 1.5 copy-start.3
  75.4 15.1 %copy-start.5 = (f32[2,128]{1,0:T(2,128)S(1)}, f32[2,128]{1,0:T(2,128)}, u32[]{:S(2)}) copy-start(f32[2,128]{1,0:T(2,128)} %param.17) | copy-start | bytes 3076
  75.4 15.1 %copy-start.4 = (f32[2,8,128]{2,1,0:T(8,128)S(1)}, f32[2,8,128]{2,1,0:T(8,128)}, u32[]{:S(2)}) copy-start(f32[2,8,128]{2,1,0:T(8,128)} %param.16) | copy-start | bytes 24580
  77.0 33.9 %all-to-all-start = ((bf16[2,32,32,128]{3,2,0,1:T(8,128)(2,1)}), bf16[2,32,32,128]{3,2,0,1:T(8,128)(2,1)S(1)}, u32[]{:S(2)}, u32[]{:S(2)}) async-start(bf16[2,32,32,128]{3,2,0,1:T(8,128)(2,1)} %copy.19), calls=%async_computation | async-start | bytes 1048576 | tf_op jit(solution)/shard_map/all_to_all | solution.py:72
  90.4 93.4 %all-gather.5.cloned.1.call-start = ((), (), s32[]{:S(2)}) async-start(), calls=%async_computation.5 | async-start | bytes 4718592 | tf_op jit(solution)/shard_map/all_gather | solution.py:66
  111.0 1.0 copy-start.6
  112.0 3.0 %copy-start.2 = (bf16[2,1024,128]{2,1,0:T(8,128)(2,1)S(1)}, bf16[2,1024,128]{2,1,0:T(8,128)(2,1)}, u32[]{:S(2)}) copy-start(bf16[2,1024,128]{2,1,0:T(8,128)(2,1)} %param.19) | copy-start | bytes 1572868
  195.3 1.5 copy-start
Sparse Core Ops, SparseCore 0:
  9.1 53.0 all-gather.2
  138.0 45.7 all-gather.4
where the time goes:
time: 266 us; the launch traced here: 265 us
  waiting for transfers between devices  120 us (45%)
  blocking collectives  75.2 us (28%)
  matrix products  24.5 us (9%)
  local copies, waits for them, and re-layouts  14 us (5%)
  between operations  13.7 us (5%)
  starting transfers between devices  13.5 us (5%)
  other arithmetic  3.68 us (1%)
    all_gather x2, waiting for transfers between devices, on_device(): gathered = lax.all_gather(state, 'vert', axis=1, tiled=True)  99.4 us
    all_to_all x2, blocking collectives, on_device(): lax.all_to_all(finished, 'snap', split_axis=0, concat_axis=1, tiled=True)  41.5 us
    all_to_all x1, blocking collectives, on_device(): lax.all_to_all(grouped, 'snap', split_axis=1, concat_axis=0, tiled=True)  33.7 us
    all_to_all x1, waiting for transfers between devices, on_device(): lax.all_to_all(grouped, 'snap', split_axis=1, concat_axis=0, tiled=True)  20.3 us
    all_to_all x1, starting transfers between devices, on_device(): lax.all_to_all(grouped, 'snap', split_axis=1, concat_axis=0, tiled=True)  13.4 us
    dot_general x2, matrix products, aggregate(): jnp.einsum('rkij,rkjf->rif', blocks, picked, preferred_element_type=jnp.f...  11.8 us
    gather x3, local copies, waits for them, and re-layouts, aggregate(): picked = stacked[columns]  10.6 us
    dot_general x4, matrix products, mlp_branch(): jnp.dot(normed, up_weight, preferred_element_type=jnp.float32)  8.73 us
  transfers between devices with their start and end apart: 3, of which 3 were waited for; matrix products, arithmetic and copies ran while one was open for 1% of the time, Pallas kernels for 0%

commit v1 on v0

v1 whole, which is shorter than its diff:
```python
import functools

import jax
import jax.numpy as jnp
from jax import lax
from jax.experimental import pallas as pl
from jax.experimental.pallas import tpu as pltpu
from jax.sharding import Mesh, PartitionSpec as P

EPS = 1e-06
AXES = ("zh", "x", "y", "zl", "co")
PLANE = ("x", "y")
LINE = ("zl", "co")


def gelu(x):
    inner = 0.7978845608028654 * (x + 0.044715 * (x * x * x))
    return (0.5 * x) * (1.0 + jnp.tanh(inner))


def rms(x, gain):
    scale = lax.rsqrt(jnp.mean(x * x, axis=-1, keepdims=True) + EPS)
    return (x * scale * gain).astype(jnp.bfloat16)


def mlp(residual, rows, gain, up, down):
    hidden = gelu(
        jnp.dot(rms(rows, gain), up, preferred_element_type=jnp.float32)
    ).astype(jnp.bfloat16)
    branch = jnp.dot(hidden, down, preferred_element_type=jnp.float32)
    return (residual.astype(jnp.float32) + branch).astype(jnp.bfloat16)


def graph_kernel(layer, chips, steps, blocked, *refs):
    place, cols, own, mate = refs[:4]
    pieces = refs[4 : 4 + 4 * steps]
    weights, gain, up, down, out, state, tiles, summed, state_sem, tile_sem = refs[
        4 + 4 * steps :
    ]
    z, c = place[0], place[1]
    snaps, row_tiles, k_count = cols.shape
    span = out.shape[0]
    half = out.shape[2]
    tile = 2 * half

    def move(piece, slot):
        for t in range(snaps):
            pltpu.make_async_copy(
                piece.at[:, t] if blocked else piece.at[t],
                state.at[t, pl.ds(slot * span, span)],
                state_sem.at[t, slot],
            ).start()

    move(own, 2 * z + c)
    move(mate, 2 * z + 1 - c)
    for step in range(1, steps + 1):
        ahead, behind, ahead_mate, behind_mate = pieces[4 * (step - 1) : 4 * step]
        shift = step * (1 - 2 * c)

        def place_pair(mine, other, chip):
            @pl.when(jnp.logical_and(chip >= 0, chip < chips))
            def _():
                move(mine, 2 * chip + c)
                move(other, 2 * chip + 1 - c)

        place_pair(ahead, behind_mate, z - shift)
        place_pair(behind, ahead_mate, z + shift)

    def tile_copy(t):
        return pltpu.make_async_copy(weights.at[t], tiles.at[t], tile_sem.at[t])

    for t in range(snaps):
        tile_copy(t).start()
    for t in range(snaps):
        for slot in range(2 * chips):
            pltpu.make_async_copy(
                own.at[:, t] if blocked else own.at[t],
                state.at[t, pl.ds(slot * span, span)],
                state_sem.at[t, slot],
            ).wait()
        tile_copy(t).wait()
        for r in range(row_tiles):
            picked = jnp.concatenate(
                [
                    state[t, pl.ds(2 * cols[t, r, k], 2)].reshape(tile, tile)
                    for k in range(k_count)
                ],
                axis=0,
            )
            summed[pl.ds(r * tile, tile)] = jnp.dot(
                tiles[t, r], picked, preferred_element_type=jnp.float32
            )
        chunk = 512
        for q in range(row_tiles * tile // chunk):
            blocks = chunk // half
            residual = state[t, pl.ds((2 * z + c) * span + q * blocks, blocks)]
            done = mlp(
                residual.reshape(chunk, tile),
                summed[pl.ds(q * chunk, chunk)],
                gain[layer],
                up[layer],
                down[layer],
            )
            out[pl.ds(q * blocks, blocks), t] = done.reshape(blocks, half, tile)


def graph_stage(layer, blocked, place, cols, own, mate, pieces, weights, gain, up, down):
    steps = len(pieces) // 4
    chips = steps + 1
    snaps, row_tiles, k_count = cols.shape
    width = own.shape[-1]
    span = row_tiles * 2
    half = width // 2
    any_spec = pl.BlockSpec(memory_space=pl.ANY)
    smem = pl.BlockSpec(memory_space=pltpu.SMEM)
    vmem = pl.BlockSpec(memory_space=pltpu.VMEM)
    return pl.pallas_call(
        functools.partial(graph_kernel, layer, chips, steps, blocked),
        out_shape=jax.ShapeDtypeStruct((span, snaps, half, width), jnp.bfloat16),
        in_specs=[smem, smem]
        + [any_spec] * (3 + len(pieces))
        + [vmem] * 3,
        out_specs=pl.BlockSpec(memory_space=pltpu.VMEM),
        scratch_shapes=[
            pltpu.VMEM((snaps, 2 * chips * span, half, width), jnp.bfloat16),
            pltpu.VMEM(weights.shape, jnp.bfloat16),
            pltpu.VMEM((row_tiles * width, width), jnp.float32),
            pltpu.SemaphoreType.DMA((snaps, 2 * chips)),
            pltpu.SemaphoreType.DMA((snaps,)),
        ],
        compiler_params=pltpu.CompilerParams(vmem_limit_bytes=40 << 20),
        name="graph",
    )(place, cols, own, mate, *pieces, weights, gain, up, down)


def time_kernel(layer, own, halo, lags, gain, up, down, out, ext, sem):
    before = halo.shape[0]
    snaps, rows, width = own.shape
    first = pltpu.make_async_copy(halo, ext.at[pl.ds(0, before)], sem.at[0])
    second = pltpu.make_async_copy(own, ext.at[pl.ds(before, snaps)], sem.at[1])
    first.start()
    second.start()
    first.wait()
    second.wait()
    group = 8
    for q in range(snaps // group):
        mixed = jnp.zeros((group, rows, width), jnp.float32)
        for m in range(before + 1):
            part = ext[pl.ds(before + q * group - m, group)].astype(jnp.float32)
            mixed = mixed + lags[layer, m].reshape(1, 1, width) * part
        residual = ext[pl.ds(before + q * group, group)]
        done = mlp(
            residual.reshape(group * rows, width),
            mixed.reshape(group * rows, width),
            gain[layer],
            up[layer],
            down[layer],
        )
        out[pl.ds(q * group, group)] = done.reshape(group, rows, width)


def time_stage(layer, own, halo, lags, gain, up, down):
    snaps, rows, width = own.shape
    any_spec = pl.BlockSpec(memory_space=pl.ANY)
    vmem = pl.BlockSpec(memory_space=pltpu.VMEM)
    return pl.pallas_call(
        functools.partial(time_kernel, layer),
        out_shape=jax.ShapeDtypeStruct(own.shape, jnp.bfloat16),
        in_specs=[any_spec] * 2 + [vmem] * 4,
        out_specs=pl.BlockSpec(memory_space=pltpu.VMEM),
        scratch_shapes=[
            pltpu.VMEM((halo.shape[0] + snaps, rows, width), jnp.bfloat16),
            pltpu.SemaphoreType.DMA((2,)),
        ],
        compiler_params=pltpu.CompilerParams(vmem_limit_bytes=40 << 20),
        name="time",
    )(own, halo, lags, gain, up, down)


def line_paths(chips):
    climb = [(2 * z, 2 * z + 2) for z in range(chips - 1)]
    sink = [(2 * z + 3, 2 * z + 1) for z in range(chips - 1)]
    forward = climb + sink + [(2 * chips - 2, 2 * chips - 1), (1, 0)]
    return forward, [(b, a) for a, b in forward]


def gather_line(state):
    chips = lax.axis_size("zl")
    forward, backward = line_paths(chips)
    core = lax.axis_index("co")
    swap = lambda v: lax.ppermute(v, "co", [(0, 1), (1, 0)])
    mate = swap(state)
    ahead = behind = state
    pieces = []
    for _ in range(chips - 1):
        ahead = lax.ppermute(ahead, LINE, forward)
        behind = lax.ppermute(behind, LINE, backward)
        pieces.append((ahead, behind, swap(ahead), swap(behind)))
    return mate, pieces


def on_device(
    features,
    tile_cols,
    tile_weights,
    graph_gain,
    graph_up,
    graph_down,
    lag_mix,
    time_gain,
    time_up,
    time_down,
):
    snap_dev, vert_dev, width = features.shape
    row_tiles, k_count = tile_cols.shape[1:]
    owners = lax.axis_size(PLANE)
    half = vert_dev // owners
    lag_count = lag_mix.shape[1]
    core = lax.axis_index("co")
    place = jnp.stack([lax.axis_index("zl"), core]).astype(jnp.int32)
    weights = (
        tile_weights.astype(jnp.bfloat16)
        .transpose(0, 1, 3, 2, 4)
        .reshape(snap_dev, row_tiles, width, k_count * width)
    )
    g_gain = graph_gain[:, None, :]
    t_gain = time_gain[:, None, :]
    state = features.reshape(snap_dev, owners, half, width)
    for layer in range(graph_up.shape[0]):
        mate, moved = gather_line(state)
        pieces = []
        for ahead, behind, ahead_mate, behind_mate in moved:
            pieces += [ahead, behind, ahead_mate, behind_mate]
        graph_out = graph_stage(
            layer,
            layer > 0,
            place,
            tile_cols,
            state,
            mate,
            pieces,
            weights,
            g_gain,
            graph_up,
            graph_down,
        )
        owned = lax.all_to_all(graph_out, PLANE, 0, 0, tiled=True)
        owned = owned.reshape(owners * snap_dev, half, width)
        halo = lax.ppermute(owned[1 - lag_count :], "zh", [(0, 1)])
        finished = time_stage(layer, owned, halo, lag_mix, t_gain, time_up, time_down)
        state = lax.all_to_all(
            finished.reshape(owners, snap_dev, half, width), PLANE, 0, 0, tiled=True
        )
    return state.transpose(1, 0, 2, 3).reshape(snap_dev, vert_dev, width)


def solution(mesh):
    fine = Mesh(mesh.devices.reshape(2, 4, 4, 4, 2), AXES)
    snap, vert = ("zh", "x", "y"), LINE
    return jax.shard_map(
        on_device,
        mesh=fine,
        in_specs=(
            P(snap, vert, None),
            P(snap, vert, None),
            P(snap, vert, None, None, None),
        )
        + (P(),) * 7,
        out_specs=P(snap, vert, None),
        check_vma=False,
    )
```

time: 266 us -> 189 us (0.71)
  waiting for transfers between devices: 120 us -> 68.9 us
  matrix products: 24.5 us -> 0 us
  starting transfers between devices: 13.5 us -> 32.6 us
  Pallas kernels: 0 us -> 18.4 us
  between operations: 13.7 us -> 0.25 us
  local copies, waits for them, and re-layouts: 14 us -> 0.89 us
  blocking collectives: 75.2 us -> 63.2 us
    all_gather x2 -> x0, waiting for transfers between devices: 99.4 us -> none  [on_device(): gathered = lax.all_gather(state, 'vert', axis=1, tiled=True)]
    ppermute x0 -> x28, waiting for transfers between devices: none -> 68.9 us  [the longest x6 59.7 us: gather_line(): behind = lax.ppermute(behind, LINE, backward)]
    ppermute x0 -> x28, starting transfers between devices: none -> 32.6 us  [the longest x2 15.9 us: on_device(): halo = lax.ppermute(owned[1 - lag_count:], 'zh', [(0, 1)])]
    dot_general x10 -> x0, matrix products: 24.5 us -> none  [the longest x2 11.8 us: aggregate(): jnp.einsum('rkij,rkjf->rif', blocks, picked, preferred_element_type=jnp.f...]
    all_to_all x1 -> x0, waiting for transfers between devices: 20.3 us -> none  [on_device(): lax.all_to_all(grouped, 'snap', split_axis=1, concat_axis=0, tiled=True)]
    pallas_call x0 -> x4, Pallas kernels: none -> 18.4 us  [the longest x2 9.8 us: graph_stage(): pl.pallas_call(functools.partial(graph_kernel, layer, chips, steps, block...]
    all_to_all x1 -> x0, starting transfers between devices: 13.4 us -> none  [on_device(): lax.all_to_all(grouped, 'snap', split_axis=1, concat_axis=0, tiled=True)]
    all_to_all x3 -> x4, blocking collectives: 75.2 us -> 63.2 us  [the longest x2 34.6 us: on_device(): owned = lax.all_to_all(graph_out, PLANE, 0, 0, tiled=True)]
  transfers between devices with their start and end apart: 3 -> 28, of which waited for: 3 -> 11; matrix products, arithmetic and copies ran while one was open for 1% -> 2% of each run, Pallas kernels for 0% -> 0%
where the time goes in v1:
time: 189 us
  waiting for transfers between devices  68.9 us (36%)
  blocking collectives  63.2 us (33%)
  starting transfers between devices  32.6 us (17%)
  Pallas kernels  18.4 us (10%)
  other arithmetic  4.38 us (2%)
    ppermute x6, waiting for transfers between devices, gather_line(): behind = lax.ppermute(behind, LINE, backward)  59.7 us
    all_to_all x2, blocking collectives, on_device(): owned = lax.all_to_all(graph_out, PLANE, 0, 0, tiled=True)  34.6 us
    all_to_all x2, blocking collectives, on_device(): lax.all_to_all(finished.reshape(owners, snap_dev, half, width), PLANE, 0,...  28.7 us
    ppermute x2, starting transfers between devices, on_device(): halo = lax.ppermute(owned[1 - lag_count:], 'zh', [(0, 1)])  15.9 us
    pallas_call x2, Pallas kernels, graph_stage(): pl.pallas_call(functools.partial(graph_kernel, layer, chips, steps, block...  9.8 us
    pallas_call x2, Pallas kernels, time_stage(): pl.pallas_call(functools.partial(time_kernel, layer), out_shape=jax.Shape...  8.63 us
    ppermute x6, starting transfers between devices, gather_line(): behind = lax.ppermute(behind, LINE, backward)  7.66 us
    ppermute x2, waiting for transfers between devices, on_device(): halo = lax.ppermute(owned[1 - lag_count:], 'zh', [(0, 1)])  6.51 us
  transfers between devices with their start and end apart: 28, of which 11 were waited for; matrix products, arithmetic and copies ran while one was open for 2% of the time, Pallas kernels for 0%

profile of v1, /device:TPU:32, one launch (start us, length us, event | category | flops | bytes accessed | tf_op | source)
XLA Modules:
  0.0 188.7 jit_solution(4069258205340058552)
XLA Ops:
  0.0 1.8 collective-permute-start.2
  2.0 12.3 %collective-permute-done.2.refs_5_ = bf16[2,16,64,128]{3,2,1,0:T(8,128)(2,1)S(1)} collective-permute-done((bf16[2,16,64,128]{3,2,1,0:T(8,128)(2,1)}, bf16[2,16,64,128]{3,2,1,0:T(8,128)(2,1)S(1)}, u32[]{:S(2)}, u32[]{:S(2)}) %collective-permute-start.2) | collective-permute-done | bytes 524320 | tf_op jit(solution)/shard_map/ppermute | solution.py:197
  14.3 1.5 collective-permute-start.6
  15.8 0.7 collective-permute-start.5
  17.0 11.8 %collective-permute-done.6.refs_9_ = bf16[2,16,64,128]{3,2,1,0:T(8,128)(2,1)S(1)} collective-permute-done((bf16[2,16,64,128]{3,2,1,0:T(8,128)(2,1)S(1)}, bf16[2,16,64,128]{3,2,1,0:T(8,128)(2,1)S(1)}, u32[]{:S(2)}, u32[]{:S(2)}) %collective-permute-start.6) | collective-permute-done | bytes 524320 | tf_op jit(solution)/shard_map/ppermute | solution.py:197
  28.9 1.9 %collective-permute-start.9 = (bf16[2,16,64,128]{3,2,1,0:T(8,128)(2,1)S(1)}, bf16[2,16,64,128]{3,2,1,0:T(8,128)(2,1)}, u32[]{:S(2)}, u32[]{:S(2)}) collective-permute-start(bf16[2,16,64,128]{3,2,1,0:T(8,128)(2,1)S(1)} %collective-permute-done.5.refs_8_), channel_id=1, source_target_pairs={{0,2},{2,4},{4,6},{3,1},{5,3},{7,5},{6,7},{1,0},{8,10},{10,12},{12... | collective-permute-start | bytes 1572872 | tf_op jit(solution)/shard_map/ppermute | solution.py:196
  31.7 10.9 %collective-permute-done.10.refs_13_ = bf16[2,16,64,128]{3,2,1,0:T(8,128)(2,1)} collective-permute-done((bf16[2,16,64,128]{3,2,1,0:T(8,128)(2,1)S(1)}, bf16[2,16,64,128]{3,2,1,0:T(8,128)(2,1)}, u32[]{:S(2)}, u32[]{:S(2)}) %collective-permute-start.10) | collective-permute-done | bytes 524320 | tf_op jit(solution)/shard_map/ppermute | solution.py:197
  42.5 0.5 collective-permute-start.11
  43.0 4.3 %copy_bitcast_fusion.refs_16_ = bf16[2,8,128,1024]{3,2,1,0:T(8,128)(2,1)S(1)} fusion(s32[2,8,8,128,128]{4,3,2,1,0:T(8,128)} %param.12), kind=kLoop, calls=%fused_computation | loop fusion | flops 2097152 | bytes 12582912 | tf_op jit(solution)/shard_map/reshape | solution.py:224
  47.5 5.0 %graph.2 = bf16[16,2,64,128]{3,2,1,0:T(8,128)(2,1)S(1)} custom-call(s32[2]{0:T(128)S(1)} %pad_add_fusion.refs_0_, s32[2,8,8]{2,1,0:T(8,128)S(1)} %copy-done.6, bf16[2,16,64,128]{3,2,1,0:T(8,128)(2,1)S(1)} %bitcast.26, bf16[2,16,64,128]{3,2,1,0:T(8,128)(2,1)S(1)} %collective-permute-done.refs_3_, bf16[2,16,64,128]{3,2,1,0:T(8,128)(2,1)S(1)} %collective-permute-done.1.refs_4_, ...), custom_call_target="tpu_custom_call" | custom-call | tf_op jit(solution)/shard_map/graph/pallas_call | solution.py:117
  52.5 18.5 %all_to_all.20 = bf16[16,2,64,128]{3,2,1,0:T(8,128)(2,1)S(1)} all-to-all(bf16[16,2,64,128]{3,2,1,0:T(8,128)(2,1)S(1)} %graph.2), channel_id=1, replica_groups=mesh['zh'=2,'x'=4,'y'=4,'zl'=4,'co'=2] {'x','y'}, dimensions={0} | all-to-all | bytes 1048576 | tf_op jit(solution)/shard_map/all_to_all | solution.py:247
  71.0 6.8 %collective-permute-start.13 = (bf16[7,64,128]{2,1,0:T(8,128)(2,1)S(1)}, bf16[7,64,128]{2,1,0:T(8,128)(2,1)S(1)}, u32[]{:S(2)}, u32[]{:S(2)}) collective-permute-start(bf16[7,64,128]{2,1,0:T(8,128)(2,1)S(1)} %slice.8), channel_id=1, source_target_pairs={{0,128},{1,129},{2,130},{3,131},{4,132},{5,133},{6,134},{7,135},{8... | collective-permute-start | bytes 344072 | tf_op jit(solution)/shard_map/ppermute | solution.py:249
  77.8 3.3 %collective-permute-done.13.halo = bf16[7,64,128]{2,1,0:T(8,128)(2,1)S(1)} collective-permute-done((bf16[7,64,128]{2,1,0:T(8,128)(2,1)S(1)}, bf16[7,64,128]{2,1,0:T(8,128)(2,1)S(1)}, u32[]{:S(2)}, u32[]{:S(2)}) %collective-permute-start.13) | collective-permute-done | bytes 114720 | tf_op jit(solution)/shard_map/ppermute | solution.py:249
  81.1 4.3 %time.2 = bf16[32,64,128]{2,1,0:T(8,128)(2,1)S(1)} custom-call(bf16[32,64,128]{2,1,0:T(8,128)(2,1)S(1)} %bitcast.18, bf16[7,64,128]{2,1,0:T(8,128)(2,1)S(1)} %collective-permute-done.13.halo, f32[2,8,128]{2,1,0:T(8,128)S(1)} %copy-done.5, f32[2,1,128]{2,1,0:T(1,128)S(1)} %bitcast.29, bf16[2,128,1024]{2,1,0:T(8,128)(2,1)S(1)} %copy-done, ...), custom_call_target="tpu_custom_call" | custom-call | tf_op jit(solution)/shard_map/time/pallas_call | solution.py:166
  85.4 14.2 %all_to_all.21.refs_2_ = bf16[16,2,64,128]{3,2,1,0:T(8,128)(2,1)S(1)} all-to-all(bf16[16,2,64,128]{3,2,1,0:T(8,128)(2,1)S(1)} %bitcast.21), channel_id=1, replica_groups=mesh['zh'=2,'x'=4,'y'=4,'zl'=4,'co'=2] {'x','y'}, dimensions={0} | all-to-all | bytes 1048576 | tf_op jit(solution)/shard_map/all_to_all | solution.py:251
  99.6 2.0 %collective-permute-start.15 = (bf16[16,2,64,128]{3,2,1,0:T(8,128)(2,1)S(1)}, bf16[16,2,64,128]{3,2,1,0:T(8,128)(2,1)S(1)}, u32[]{:S(2)}, u32[]{:S(2)}) collective-permute-start(bf16[16,2,64,128]{3,2,1,0:T(8,128)(2,1)S(1)} %all_to_all.21.refs_2_), channel_id=1, source_target_pairs={{0,2},{2,4},{4,6},{3,1},{5,3},{7,5},{6,7},{1,0},{8,10},{10,12},{12... | collective-permute-start | bytes 1572872 | tf_op jit(solution)/shard_map/ppermute | solution.py:196
  101.6 9.1 %collective-permute-done.16.refs_5_ = bf16[16,2,64,128]{3,2,1,0:T(8,128)(2,1)S(1)} collective-permute-done((bf16[16,2,64,128]{3,2,1,0:T(8,128)(2,1)S(1)}, bf16[16,2,64,128]{3,2,1,0:T(8,128)(2,1)S(1)}, u32[]{:S(2)}, u32[]{:S(2)}) %collective-permute-start.16) | collective-permute-done | bytes 524320 | tf_op jit(solution)/shard_map/ppermute | solution.py:197
  110.7 1.7 collective-permute-start.20
  113.2 8.8 %collective-permute-done.20.refs_9_ = bf16[16,2,64,128]{3,2,1,0:T(8,128)(2,1)S(1)} collective-permute-done((bf16[16,2,64,128]{3,2,1,0:T(8,128)(2,1)S(1)}, bf16[16,2,64,128]{3,2,1,0:T(8,128)(2,1)S(1)}, u32[]{:S(2)}, u32[]{:S(2)}) %collective-permute-start.20) | collective-permute-done | bytes 524320 | tf_op jit(solution)/shard_map/ppermute | solution.py:197
  122.0 2.5 %collective-permute-start.24 = (bf16[16,2,64,128]{3,2,1,0:T(8,128)(2,1)S(1)}, bf16[16,2,64,128]{3,2,1,0:T(8,128)(2,1)S(1)}, u32[]{:S(2)}, u32[]{:S(2)}) collective-permute-start(bf16[16,2,64,128]{3,2,1,0:T(8,128)(2,1)S(1)} %collective-permute-done.20.refs_9_), channel_id=1, source_target_pairs={{2,0},{4,2},{6,4},{1,3},{3,5},{5,7},{7,6},{0,1},{10,8},{12,10},{14... | collective-permute-start | bytes 1572872 | tf_op jit(solution)/shard_map/ppermute | solution.py:197
  124.5 1.2 collective-permute-start.23
  126.3 6.8 %collective-permute-done.24.refs_13_ = bf16[16,2,64,128]{3,2,1,0:T(8,128)(2,1)S(1)} collective-permute-done((bf16[16,2,64,128]{3,2,1,0:T(8,128)(2,1)S(1)}, bf16[16,2,64,128]{3,2,1,0:T(8,128)(2,1)S(1)}, u32[]{:S(2)}, u32[]{:S(2)}) %collective-permute-start.24) | collective-permute-done | bytes 524320 | tf_op jit(solution)/shard_map/ppermute | solution.py:197
  133.2 0.5 collective-permute-done.23.refs_12_
  133.7 1.3 collective-permute-done.26.refs_15_
  135.1 0.7 collective-permute-done.25.refs_14_
  135.8 4.8 %graph.3 = bf16[16,2,64,128]{3,2,1,0:T(8,128)(2,1)S(1)} custom-call(s32[2]{0:T(128)S(1)} %pad_add_fusion.refs_0_, s32[2,8,8]{2,1,0:T(8,128)S(1)} %copy-done.6, bf16[16,2,64,128]{3,2,1,0:T(8,128)(2,1)S(1)} %all_to_all.21.refs_2_, bf16[16,2,64,128]{3,2,1,0:T(8,128)(2,1)S(1)} %collective-permute-done.14.refs_3_, ...), custom_call_target="tpu_custom_call" | custom-call | tf_op jit(solution)/shard_map/graph/pallas_call | solution.py:117
  140.6 16.1 %all_to_all.22 = bf16[16,2,64,128]{3,2,1,0:T(8,128)(2,1)S(1)} all-to-all(bf16[16,2,64,128]{3,2,1,0:T(8,128)(2,1)S(1)} %graph.3), channel_id=1, replica_groups=mesh['zh'=2,'x'=4,'y'=4,'zl'=4,'co'=2] {'x','y'}, dimensions={0} | all-to-all | bytes 1048576 | tf_op jit(solution)/shard_map/all_to_all | solution.py:247
  156.7 9.1 %collective-permute-start.27 = (bf16[7,64,128]{2,1,0:T(8,128)(2,1)S(1)}, bf16[7,64,128]{2,1,0:T(8,128)(2,1)S(1)}, u32[]{:S(2)}, u32[]{:S(2)}) collective-permute-start(bf16[7,64,128]{2,1,0:T(8,128)(2,1)S(1)} %slice.9), channel_id=1, source_target_pairs={{0,128},{1,129},{2,130},{3,131},{4,132},{5,133},{6,134},{7,135},{8... | collective-permute-start | bytes 344072 | tf_op jit(solution)/shard_map/ppermute | solution.py:249
  165.8 3.3 %collective-permute-done.27.halo = bf16[7,64,128]{2,1,0:T(8,128)(2,1)S(1)} collective-permute-done((bf16[7,64,128]{2,1,0:T(8,128)(2,1)S(1)}, bf16[7,64,128]{2,1,0:T(8,128)(2,1)S(1)}, u32[]{:S(2)}, u32[]{:S(2)}) %collective-permute-start.27) | collective-permute-done | bytes 114720 | tf_op jit(solution)/shard_map/ppermute | solution.py:249
  169.0 4.3 %time.3 = bf16[32,64,128]{2,1,0:T(8,128)(2,1)S(1)} custom-call(bf16[32,64,128]{2,1,0:T(8,128)(2,1)S(1)} %bitcast.20, bf16[7,64,128]{2,1,0:T(8,128)(2,1)S(1)} %collective-permute-done.27.halo, f32[2,8,128]{2,1,0:T(8,128)S(1)} %copy-done.5, f32[2,1,128]{2,1,0:T(1,128)S(1)} %bitcast.30, bf16[2,128,1024]{2,1,0:T(8,128)(2,1)S(1)} %copy-done, ...), custom_call_target="tpu_custom_call" | custom-call | tf_op jit(solution)/shard_map/time/pallas_call | solution.py:166
  173.4 14.5 %all_to_all.23 = bf16[16,2,64,128]{3,2,1,0:T(8,128)(2,1)S(1)} all-to-all(bf16[16,2,64,128]{3,2,1,0:T(8,128)(2,1)S(1)} %bitcast.22), channel_id=1, replica_groups=mesh['zh'=2,'x'=4,'y'=4,'zl'=4,'co'=2] {'x','y'}, dimensions={0} | all-to-all | bytes 1048576 | tf_op jit(solution)/shard_map/all_to_all | solution.py:251
  187.9 0.8 copy.12
  (55 shorter events, 3.1 us)
Async XLA Ops:
  0.0 14.3 %collective-permute-start.2 = (bf16[2,16,64,128]{3,2,1,0:T(8,128)(2,1)}, bf16[2,16,64,128]{3,2,1,0:T(8,128)(2,1)S(1)}, u32[]{:S(2)}, u32[]{:S(2)}) collective-permute-start(bf16[2,16,64,128]{3,2,1,0:T(8,128)(2,1)} %bitcast.23), channel_id=1, source_target_pairs={{2,0},{4,2},{6,4},{1,3},{3,5},{5,7},{7,6},{0,1},{10,8},{12,10},{14... | collective-permute-start | bytes 1572872 | tf_op jit(solution)/shard_map/ppermute | solution.py:197
  1.8 14.0 %collective-permute-start.1 = (bf16[2,16,64,128]{3,2,1,0:T(8,128)(2,1)}, bf16[2,16,64,128]{3,2,1,0:T(8,128)(2,1)S(1)}, u32[]{:S(2)}, u32[]{:S(2)}) collective-permute-start(bf16[2,16,64,128]{3,2,1,0:T(8,128)(2,1)} %bitcast.24), channel_id=1, source_target_pairs={{0,2},{2,4},{4,6},{3,1},{5,3},{7,5},{6,7},{1,0},{8,10},{10,12},{12... | collective-permute-start | bytes 1572872 | tf_op jit(solution)/shard_map/ppermute | solution.py:196
  14.3 14.5 %collective-permute-start.6 = (bf16[2,16,64,128]{3,2,1,0:T(8,128)(2,1)S(1)}, bf16[2,16,64,128]{3,2,1,0:T(8,128)(2,1)S(1)}, u32[]{:S(2)}, u32[]{:S(2)}) collective-permute-start(bf16[2,16,64,128]{3,2,1,0:T(8,128)(2,1)S(1)} %collective-permute-done.2.refs_5_), channel_id=1, source_target_pairs={{2,0},{4,2},{6,4},{1,3},{3,5},{5,7},{7,6},{0,1},{10,8},{12,10},{14... | collective-permute-start | bytes 1572872 | tf_op jit(solution)/shard_map/ppermute | solution.py:197
  15.8 13.1 %collective-permute-start.5 = (bf16[2,16,64,128]{3,2,1,0:T(8,128)(2,1)S(1)}, bf16[2,16,64,128]{3,2,1,0:T(8,128)(2,1)S(1)}, u32[]{:S(2)}, u32[]{:S(2)}) collective-permute-start(bf16[2,16,64,128]{3,2,1,0:T(8,128)(2,1)S(1)} %collective-permute-done.1.refs_4_), channel_id=1, source_target_pairs={{0,2},{2,4},{4,6},{3,1},{5,3},{7,5},{6,7},{1,0},{8,10},{10,12},{12... | collective-permute-start | bytes 1572872 | tf_op jit(solution)/shard_map/ppermute | solution.py:196
  16.5 14.6 %collective-permute-start = (bf16[2,16,64,128]{3,2,1,0:T(8,128)(2,1)}, bf16[2,16,64,128]{3,2,1,0:T(8,128)(2,1)S(1)}, u32[]{:S(2)}, u32[]{:S(2)}) collective-permute-start(bf16[2,16,64,128]{3,2,1,0:T(8,128)(2,1)} %bitcast.25), channel_id=1, source_target_pairs={{0,1},{1,0},{2,3},{3,2},{4,5},{5,4},{6,7},{7,6},{8,9},{9,8},{10,11... | collective-permute-start | bytes 1572872 | tf_op jit(solution)/shard_map/ppermute | solution.py:191
  16.5 15.1 %collective-permute-start.4 = (bf16[2,16,64,128]{3,2,1,0:T(8,128)(2,1)S(1)}, bf16[2,16,64,128]{3,2,1,0:T(8,128)(2,1)S(1)}, u32[]{:S(2)}, u32[]{:S(2)}) collective-permute-start(bf16[2,16,64,128]{3,2,1,0:T(8,128)(2,1)S(1)} %collective-permute-done.2.refs_5_), channel_id=1, source_target_pairs={{0,1},{1,0},{2,3},{3,2},{4,5},{5,4},{6,7},{7,6},{8,9},{9,8},{10,11... | collective-permute-start | bytes 1572872 | tf_op jit(solution)/shard_map/ppermute | solution.py:191
  28.8 13.7 %collective-permute-start.10 = (bf16[2,16,64,128]{3,2,1,0:T(8,128)(2,1)S(1)}, bf16[2,16,64,128]{3,2,1,0:T(8,128)(2,1)}, u32[]{:S(2)}, u32[]{:S(2)}) collective-permute-start(bf16[2,16,64,128]{3,2,1,0:T(8,128)(2,1)S(1)} %collective-permute-done.6.refs_9_), channel_id=1, source_target_pairs={{2,0},{4,2},{6,4},{1,3},{3,5},{5,7},{7,6},{0,1},{10,8},{12,10},{14... | collective-permute-start | bytes 1572872 | tf_op jit(solution)/shard_map/ppermute | solution.py:197
  28.9 13.6 %collective-permute-start.9 = (bf16[2,16,64,128]{3,2,1,0:T(8,128)(2,1)S(1)}, bf16[2,16,64,128]{3,2,1,0:T(8,128)(2,1)}, u32[]{:S(2)}, u32[]{:S(2)}) collective-permute-start(bf16[2,16,64,128]{3,2,1,0:T(8,128)(2,1)S(1)} %collective-permute-done.5.refs_8_), channel_id=1, source_target_pairs={{0,2},{2,4},{4,6},{3,1},{5,3},{7,5},{6,7},{1,0},{8,10},{10,12},{12... | collective-permute-start | bytes 1572872 | tf_op jit(solution)/shard_map/ppermute | solution.py:196
  31.0 16.4 %collective-permute-start.3 = (bf16[2,16,64,128]{3,2,1,0:T(8,128)(2,1)S(1)}, bf16[2,16,64,128]{3,2,1,0:T(8,128)(2,1)S(1)}, u32[]{:S(2)}, u32[]{:S(2)}) collective-permute-start(bf16[2,16,64,128]{3,2,1,0:T(8,128)(2,1)S(1)} %collective-permute-done.1.refs_4_), channel_id=1, source_target_pairs={{0,1},{1,0},{2,3},{3,2},{4,5},{5,4},{6,7},{7,6},{8,9},{9,8},{10,11... | collective-permute-start | bytes 1572872 | tf_op jit(solution)/shard_map/ppermute | solution.py:191
  31.1 16.3 %collective-permute-start.8 = (bf16[2,16,64,128]{3,2,1,0:T(8,128)(2,1)S(1)}, bf16[2,16,64,128]{3,2,1,0:T(8,128)(2,1)S(1)}, u32[]{:S(2)}, u32[]{:S(2)}) collective-permute-start(bf16[2,16,64,128]{3,2,1,0:T(8,128)(2,1)S(1)} %collective-permute-done.6.refs_9_), channel_id=1, source_target_pairs={{0,1},{1,0},{2,3},{3,2},{4,5},{5,4},{6,7},{7,6},{8,9},{9,8},{10,11... | collective-permute-start | bytes 1572872 | tf_op jit(solution)/shard_map/ppermute | solution.py:191
  31.6 15.8 %collective-permute-start.7 = (bf16[2,16,64,128]{3,2,1,0:T(8,128)(2,1)S(1)}, bf16[2,16,64,128]{3,2,1,0:T(8,128)(2,1)S(1)}, u32[]{:S(2)}, u32[]{:S(2)}) collective-permute-start(bf16[2,16,64,128]{3,2,1,0:T(8,128)(2,1)S(1)} %collective-permute-done.5.refs_8_), channel_id=1, source_target_pairs={{0,1},{1,0},{2,3},{3,2},{4,5},{5,4},{6,7},{7,6},{8,9},{9,8},{10,11... | collective-permute-start | bytes 1572872 | tf_op jit(solution)/shard_map/ppermute | solution.py:191
  42.5 4.9 %collective-permute-start.12 = (bf16[2,16,64,128]{3,2,1,0:T(8,128)(2,1)}, bf16[2,16,64,128]{3,2,1,0:T(8,128)(2,1)S(1)}, u32[]{:S(2)}, u32[]{:S(2)}) collective-permute-start(bf16[2,16,64,128]{3,2,1,0:T(8,128)(2,1)} %collective-permute-done.10.refs_13_), channel_id=1, source_target_pairs={{0,1},{1,0},{2,3},{3,2},{4,5},{5,4},{6,7},{7,6},{8,9},{9,8},{10,11... | collective-permute-start | bytes 1572872 | tf_op jit(solution)/shard_map/ppermute | solution.py:191
  42.5 4.9 %collective-permute-start.11 = (bf16[2,16,64,128]{3,2,1,0:T(8,128)(2,1)}, bf16[2,16,64,128]{3,2,1,0:T(8,128)(2,1)S(1)}, u32[]{:S(2)}, u32[]{:S(2)}) collective-permute-start(bf16[2,16,64,128]{3,2,1,0:T(8,128)(2,1)} %collective-permute-done.9.refs_12_), channel_id=1, source_target_pairs={{0,1},{1,0},{2,3},{3,2},{4,5},{5,4},{6,7},{7,6},{8,9},{9,8},{10,11... | collective-permute-start | bytes 1572872 | tf_op jit(solution)/shard_map/ppermute | solution.py:191
  47.5 33.6 %copy-start = (bf16[2,128,1024]{2,1,0:T(8,128)(2,1)S(1)}, bf16[2,128,1024]{2,1,0:T(8,128)(2,1)}, u32[]{:S(2)}) copy-start(bf16[2,128,1024]{2,1,0:T(8,128)(2,1)} %up.3) | copy-start | bytes 1572868
  47.5 33.6 %copy-start.1 = (bf16[2,1024,128]{2,1,0:T(8,128)(2,1)S(1)}, bf16[2,1024,128]{2,1,0:T(8,128)(2,1)}, u32[]{:S(2)}) copy-start(bf16[2,1024,128]{2,1,0:T(8,128)(2,1)} %down.3) | copy-start | bytes 1572868
  47.5 33.6 %copy-start.5 = (f32[2,8,128]{2,1,0:T(8,128)S(1)}, f32[2,8,128]{2,1,0:T(8,128)}, u32[]{:S(2)}) copy-start(f32[2,8,128]{2,1,0:T(8,128)} %lags.3) | copy-start | bytes 24580
  47.5 33.6 %copy-start.8 = (f32[2,128]{1,0:T(2,128)S(1)}, f32[2,128]{1,0:T(2,128)}, u32[]{:S(2)}) copy-start(f32[2,128]{1,0:T(2,128)} %param.17) | copy-start | bytes 3076
  71.0 10.0 %collective-permute-start.13 = (bf16[7,64,128]{2,1,0:T(8,128)(2,1)S(1)}, bf16[7,64,128]{2,1,0:T(8,128)(2,1)S(1)}, u32[]{:S(2)}, u32[]{:S(2)}) collective-permute-start(bf16[7,64,128]{2,1,0:T(8,128)(2,1)S(1)} %slice.8), channel_id=1, source_target_pairs={{0,128},{1,129},{2,130},{3,131},{4,132},{5,133},{6,134},{7,135},{8... | collective-permute-start | bytes 344072 | tf_op jit(solution)/shard_map/ppermute | solution.py:249
  99.6 11.1 %collective-permute-start.16 = (bf16[16,2,64,128]{3,2,1,0:T(8,128)(2,1)S(1)}, bf16[16,2,64,128]{3,2,1,0:T(8,128)(2,1)S(1)}, u32[]{:S(2)}, u32[]{:S(2)}) collective-permute-start(bf16[16,2,64,128]{3,2,1,0:T(8,128)(2,1)S(1)} %all_to_all.21.refs_2_), channel_id=1, source_target_pairs={{2,0},{4,2},{6,4},{1,3},{3,5},{5,7},{7,6},{0,1},{10,8},{12,10},{14... | collective-permute-start | bytes 1572872 | tf_op jit(solution)/shard_map/ppermute | solution.py:197
  99.6 12.9 %collective-permute-start.15 = (bf16[16,2,64,128]{3,2,1,0:T(8,128)(2,1)S(1)}, bf16[16,2,64,128]{3,2,1,0:T(8,128)(2,1)S(1)}, u32[]{:S(2)}, u32[]{:S(2)}) collective-permute-start(bf16[16,2,64,128]{3,2,1,0:T(8,128)(2,1)S(1)} %all_to_all.21.refs_2_), channel_id=1, source_target_pairs={{0,2},{2,4},{4,6},{3,1},{5,3},{7,5},{6,7},{1,0},{8,10},{10,12},{12... | collective-permute-start | bytes 1572872 | tf_op jit(solution)/shard_map/ppermute | solution.py:196
  110.7 11.4 %collective-permute-start.20 = (bf16[16,2,64,128]{3,2,1,0:T(8,128)(2,1)S(1)}, bf16[16,2,64,128]{3,2,1,0:T(8,128)(2,1)S(1)}, u32[]{:S(2)}, u32[]{:S(2)}) collective-permute-start(bf16[16,2,64,128]{3,2,1,0:T(8,128)(2,1)S(1)} %collective-permute-done.16.refs_5_), channel_id=1, source_target_pairs={{2,0},{4,2},{6,4},{1,3},{3,5},{5,7},{7,6},{0,1},{10,8},{12,10},{14... | collective-permute-start | bytes 1572872 | tf_op jit(solution)/shard_map/ppermute | solution.py:197
  112.4 12.1 %collective-permute-start.19 = (bf16[16,2,64,128]{3,2,1,0:T(8,128)(2,1)S(1)}, bf16[16,2,64,128]{3,2,1,0:T(8,128)(2,1)S(1)}, u32[]{:S(2)}, u32[]{:S(2)}) collective-permute-start(bf16[16,2,64,128]{3,2,1,0:T(8,128)(2,1)S(1)} %collective-permute-done.15.refs_4_), channel_id=1, source_target_pairs={{0,2},{2,4},{4,6},{3,1},{5,3},{7,5},{6,7},{1,0},{8,10},{10,12},{12... | collective-permute-start | bytes 1572872 | tf_op jit(solution)/shard_map/ppermute | solution.py:196
  112.7 13.0 %collective-permute-start.14 = (bf16[16,2,64,128]{3,2,1,0:T(8,128)(2,1)S(1)}, bf16[16,2,64,128]{3,2,1,0:T(8,128)(2,1)S(1)}, u32[]{:S(2)}, u32[]{:S(2)}) collective-permute-start(bf16[16,2,64,128]{3,2,1,0:T(8,128)(2,1)S(1)} %all_to_all.21.refs_2_), channel_id=1, source_target_pairs={{0,1},{1,0},{2,3},{3,2},{4,5},{5,4},{6,7},{7,6},{8,9},{9,8},{10,11... | collective-permute-start | bytes 1572872 | tf_op jit(solution)/shard_map/ppermute | solution.py:191
  112.7 13.5 %collective-permute-start.18 = (bf16[16,2,64,128]{3,2,1,0:T(8,128)(2,1)S(1)}, bf16[16,2,64,128]{3,2,1,0:T(8,128)(2,1)S(1)}, u32[]{:S(2)}, u32[]{:S(2)}) collective-permute-start(bf16[16,2,64,128]{3,2,1,0:T(8,128)(2,1)S(1)} %collective-permute-done.16.refs_5_), channel_id=1, source_target_pairs={{0,1},{1,0},{2,3},{3,2},{4,5},{5,4},{6,7},{7,6},{8,9},{9,8},{10,11... | collective-permute-start | bytes 1572872 | tf_op jit(solution)/shard_map/ppermute | solution.py:191
  122.0 11.1 %collective-permute-start.24 = (bf16[16,2,64,128]{3,2,1,0:T(8,128)(2,1)S(1)}, bf16[16,2,64,128]{3,2,1,0:T(8,128)(2,1)S(1)}, u32[]{:S(2)}, u32[]{:S(2)}) collective-permute-start(bf16[16,2,64,128]{3,2,1,0:T(8,128)(2,1)S(1)} %collective-permute-done.20.refs_9_), channel_id=1, source_target_pairs={{2,0},{4,2},{6,4},{1,3},{3,5},{5,7},{7,6},{0,1},{10,8},{12,10},{14... | collective-permute-start | bytes 1572872 | tf_op jit(solution)/shard_map/ppermute | solution.py:197
  124.5 9.2 %collective-permute-start.23 = (bf16[16,2,64,128]{3,2,1,0:T(8,128)(2,1)S(1)}, bf16[16,2,64,128]{3,2,1,0:T(8,128)(2,1)S(1)}, u32[]{:S(2)}, u32[]{:S(2)}) collective-permute-start(bf16[16,2,64,128]{3,2,1,0:T(8,128)(2,1)S(1)} %collective-permute-done.19.refs_8_), channel_id=1, source_target_pairs={{0,2},{2,4},{4,6},{3,1},{5,3},{7,5},{6,7},{1,0},{8,10},{10,12},{12... | collective-permute-start | bytes 1572872 | tf_op jit(solution)/shard_map/ppermute | solution.py:196
  125.7 8.0 %collective-permute-start.17 = (bf16[16,2,64,128]{3,2,1,0:T(8,128)(2,1)S(1)}, bf16[16,2,64,128]{3,2,1,0:T(8,128)(2,1)S(1)}, u32[]{:S(2)}, u32[]{:S(2)}) collective-permute-start(bf16[16,2,64,128]{3,2,1,0:T(8,128)(2,1)S(1)} %collective-permute-done.15.refs_4_), channel_id=1, source_target_pairs={{0,1},{1,0},{2,3},{3,2},{4,5},{5,4},{6,7},{7,6},{8,9},{9,8},{10,11... | collective-permute-start | bytes 1572872 | tf_op jit(solution)/shard_map/ppermute | solution.py:191
  125.7 8.0 %collective-permute-start.22 = (bf16[16,2,64,128]{3,2,1,0:T(8,128)(2,1)S(1)}, bf16[16,2,64,128]{3,2,1,0:T(8,128)(2,1)S(1)}, u32[]{:S(2)}, u32[]{:S(2)}) collective-permute-start(bf16[16,2,64,128]{3,2,1,0:T(8,128)(2,1)S(1)} %collective-permute-done.20.refs_9_), channel_id=1, source_target_pairs={{0,1},{1,0},{2,3},{3,2},{4,5},{5,4},{6,7},{7,6},{8,9},{9,8},{10,11... | collective-permute-start | bytes 1572872 | tf_op jit(solution)/shard_map/ppermute | solution.py:191
  126.2 7.5 %collective-permute-start.21 = (bf16[16,2,64,128]{3,2,1,0:T(8,128)(2,1)S(1)}, bf16[16,2,64,128]{3,2,1,0:T(8,128)(2,1)S(1)}, u32[]{:S(2)}, u32[]{:S(2)}) collective-permute-start(bf16[16,2,64,128]{3,2,1,0:T(8,128)(2,1)S(1)} %collective-permute-done.19.refs_8_), channel_id=1, source_target_pairs={{0,1},{1,0},{2,3},{3,2},{4,5},{5,4},{6,7},{7,6},{8,9},{9,8},{10,11... | collective-permute-start | bytes 1572872 | tf_op jit(solution)/shard_map/ppermute | solution.py:191
  133.2 1.9 %collective-permute-start.26 = (bf16[16,2,64,128]{3,2,1,0:T(8,128)(2,1)S(1)}, bf16[16,2,64,128]{3,2,1,0:T(8,128)(2,1)S(1)}, u32[]{:S(2)}, u32[]{:S(2)}) collective-permute-start(bf16[16,2,64,128]{3,2,1,0:T(8,128)(2,1)S(1)} %collective-permute-done.24.refs_13_), channel_id=1, source_target_pairs={{0,1},{1,0},{2,3},{3,2},{4,5},{5,4},{6,7},{7,6},{8,9},{9,8},{10,11... | collective-permute-start | bytes 1572872 | tf_op jit(solution)/shard_map/ppermute | solution.py:191
  133.7 2.1 %collective-permute-start.25 = (bf16[16,2,64,128]{3,2,1,0:T(8,128)(2,1)S(1)}, bf16[16,2,64,128]{3,2,1,0:T(8,128)(2,1)S(1)}, u32[]{:S(2)}, u32[]{:S(2)}) collective-permute-start(bf16[16,2,64,128]{3,2,1,0:T(8,128)(2,1)S(1)} %collective-permute-done.23.refs_12_), channel_id=1, source_target_pairs={{0,1},{1,0},{2,3},{3,2},{4,5},{5,4},{6,7},{7,6},{8,9},{9,8},{10,11... | collective-permute-start | bytes 1572872 | tf_op jit(solution)/shard_map/ppermute | solution.py:191
  156.7 12.3 %collective-permute-start.27 = (bf16[7,64,128]{2,1,0:T(8,128)(2,1)S(1)}, bf16[7,64,128]{2,1,0:T(8,128)(2,1)S(1)}, u32[]{:S(2)}, u32[]{:S(2)}) collective-permute-start(bf16[7,64,128]{2,1,0:T(8,128)(2,1)S(1)} %slice.9), channel_id=1, source_target_pairs={{0,128},{1,129},{2,130},{3,131},{4,132},{5,133},{6,134},{7,135},{8... | collective-permute-start | bytes 344072 | tf_op jit(solution)/shard_map/ppermute | solution.py:249
  (5 other events, 82.4 us)

commit v2 on v1

v2 whole, which is shorter than its diff:
```python
import functools

import jax
import jax.numpy as jnp
from jax import lax
from jax.experimental import pallas as pl
from jax.experimental.pallas import tpu as pltpu
from jax.sharding import Mesh, PartitionSpec as P

EPS = 1e-06
AXES = ("zh", "x", "y", "zl", "co")
OWNERS = ("x", "y")
LINE = ("zl", "co")


def rms(x, gain):
    scale = lax.rsqrt(jnp.mean(x * x, axis=-1, keepdims=True) + EPS)
    return (x * scale * gain).astype(jnp.bfloat16)


def mlp(residual, rows, gain, up, down):
    x = jnp.dot(rms(rows, gain), up, preferred_element_type=jnp.float32)
    inner = x * (0.7978845608028654 + 0.035677408136300125 * (x * x))
    doubled = (x + x * jnp.tanh(inner)).astype(jnp.bfloat16)
    branch = jnp.dot(doubled, down, preferred_element_type=jnp.float32)
    return (residual.astype(jnp.float32) + 0.5 * branch).astype(jnp.bfloat16)


def graph_kernel(layer, chips, blocked, near, *refs):
    count = 4 * chips - 2
    cols = refs[0]
    pieces = refs[1 : 1 + count]
    weights, gain, up, down, out, state, summed, sem = refs[1 + count :]
    z, c = lax.axis_index("zl"), lax.axis_index("co")
    snaps, row_tiles, k_count = cols.shape
    span, _, part, tile = out.shape
    per_tile = tile // part

    def fetch(piece, t, slot):
        return pltpu.make_async_copy(
            piece.at[:, t] if blocked else piece.at[t],
            state.at[t, pl.ds(slot * span, span)],
            sem.at[t, slot],
        )

    def place_piece(piece, slot):
        for t in range(snaps):
            if near:
                state[t, pl.ds(slot * span, span)] = piece[:, t] if blocked else piece[t]
            else:
                fetch(piece, t, slot).start()

    if near:
        for t in range(snaps):
            fetch(pieces[0], t, 2 * z + c).start()
    else:
        place_piece(pieces[0], 2 * z + c)
    place_piece(pieces[1], 2 * z + 1 - c)
    for step in range(1, chips):
        ahead, behind, ahead_mate, behind_mate = pieces[4 * step - 2 : 4 * step + 2]
        shift = step * (1 - 2 * c)

        def place_pair(mine, other, chip):
            @pl.when(jnp.logical_and(chip >= 0, chip < chips))
            def _():
                place_piece(mine, 2 * chip + c)
                place_piece(other, 2 * chip + 1 - c)

        place_pair(ahead, behind_mate, z - shift)
        place_pair(behind, ahead_mate, z + shift)

    for t in range(snaps):
        if near:
            fetch(pieces[0], t, 2 * z + c).wait()
        else:
            for slot in range(2 * chips):
                fetch(pieces[0], t, slot).wait()
    chunk = 512
    blocks = chunk // part

    @pl.loop(0, snaps)
    def _(t):
        for r in range(row_tiles):
            picked = jnp.concatenate(
                [
                    state[t, pl.ds(per_tile * cols[t, r, k], per_tile)].reshape(tile, tile)
                    for k in range(k_count)
                ],
                axis=0,
            )
            summed[pl.ds(r * tile, tile)] = jnp.dot(
                weights[t, r], picked, preferred_element_type=jnp.float32
            )
        for q in range(row_tiles * tile // chunk):
            residual = state[t, pl.ds((2 * z + c) * span + q * blocks, blocks)]
            done = mlp(
                residual.reshape(chunk, tile),
                summed[pl.ds(q * chunk, chunk)],
                gain[layer],
                up[layer],
                down[layer],
            )
            out[pl.ds(q * blocks, blocks), t] = done.reshape(blocks, part, tile)


def graph_stage(layer, cols, pieces, weights, gain, up, down):
    snaps, row_tiles, _ = cols.shape
    chips = (len(pieces) + 2) // 4
    part, width = pieces[0].shape[2:]
    span = row_tiles * width // part
    any_spec = pl.BlockSpec(memory_space=pl.ANY)
    smem = pl.BlockSpec(memory_space=pltpu.SMEM)
    vmem = pl.BlockSpec(memory_space=pltpu.VMEM)
    return pl.pallas_call(
        functools.partial(graph_kernel, layer, chips, layer > 0, True),
        out_shape=jax.ShapeDtypeStruct((span, snaps, part, width), jnp.bfloat16),
        in_specs=[smem, any_spec]
        + [vmem] * (len(pieces) - 1)
        + [vmem] * 4,
        out_specs=vmem,
        scratch_shapes=[
            pltpu.VMEM((snaps, 2 * chips * span, part, width), jnp.bfloat16),
            pltpu.VMEM((row_tiles * width, width), jnp.float32),
            pltpu.SemaphoreType.DMA((snaps, 2 * chips)),
        ],
        compiler_params=pltpu.CompilerParams(vmem_limit_bytes=12 << 20),
        name="graph",
    )(cols, *pieces, weights, gain, up, down)


def tie(value, other):
    any_spec = pl.BlockSpec(memory_space=pl.ANY)
    return pl.pallas_call(
        lambda *refs: None,
        out_shape=jax.ShapeDtypeStruct(value.shape, value.dtype),
        in_specs=[any_spec] * 2,
        out_specs=any_spec,
        input_output_aliases={0: 0},
        compiler_params=pltpu.CompilerParams(vmem_limit_bytes=1 << 18),
        name="tie",
    )(value, other)


GROUP = 8


def late_kernel(layer, own, lags, gain, up, down, out):
    before = lags.shape[1] - 1
    rows, width = own.shape[1:]
    for q in range(1, own.shape[0] // GROUP):
        mixed = jnp.zeros((GROUP, rows, width), jnp.float32)
        for m in range(before + 1):
            part = own[pl.ds(q * GROUP - m, GROUP)].astype(jnp.float32)
            mixed = mixed + lags[layer, m].reshape(1, 1, width) * part
        done = mlp(
            own[pl.ds(q * GROUP, GROUP)].reshape(GROUP * rows, width),
            mixed.reshape(GROUP * rows, width),
            gain[layer],
            up[layer],
            down[layer],
        )
        out[pl.ds(q * GROUP, GROUP)] = done.reshape(GROUP, rows, width)


def early_kernel(layer, own, halo, lags, gain, up, down, later, out, ext):
    before = halo.shape[0]
    rows, width = own.shape[1:]
    ext[pl.ds(0, before)] = jnp.where(lax.axis_index("zh") > 0, halo[...], jnp.zeros_like(halo))
    ext[pl.ds(before, GROUP)] = own[pl.ds(0, GROUP)]
    mixed = jnp.zeros((GROUP, rows, width), jnp.float32)
    for m in range(before + 1):
        part = ext[pl.ds(before - m, GROUP)].astype(jnp.float32)
        mixed = mixed + lags[layer, m].reshape(1, 1, width) * part
    done = mlp(
        own[pl.ds(0, GROUP)].reshape(GROUP * rows, width),
        mixed.reshape(GROUP * rows, width),
        gain[layer],
        up[layer],
        down[layer],
    )
    out[pl.ds(0, GROUP)] = done.reshape(GROUP, rows, width)


def time_stage(layer, own, lags, gain, up, down):
    before = lags.shape[1] - 1
    halo = lax.ppermute(own[-before:], "zh", [(0, 1), (1, 0)])
    vmem = pl.BlockSpec(memory_space=pltpu.VMEM)
    params = pltpu.CompilerParams(vmem_limit_bytes=4 << 20)
    out_shape = jax.ShapeDtypeStruct(own.shape, jnp.bfloat16)
    later = pl.pallas_call(
        functools.partial(late_kernel, layer),
        out_shape=out_shape,
        in_specs=[vmem] * 5,
        out_specs=vmem,
        compiler_params=params,
        name="late",
    )(own, lags, gain, up, down)
    return pl.pallas_call(
        functools.partial(early_kernel, layer),
        out_shape=out_shape,
        in_specs=[vmem] * 7,
        out_specs=vmem,
        scratch_shapes=[pltpu.VMEM((before + GROUP,) + own.shape[1:], jnp.bfloat16)],
        input_output_aliases={6: 0},
        compiler_params=params,
        name="early",
    )(own, halo, lags, gain, up, down, later)


def line_paths(chips):
    climb = [(2 * z, 2 * z + 2) for z in range(chips - 1)]
    sink = [(2 * z + 3, 2 * z + 1) for z in range(chips - 1)]
    forward = climb + sink + [(2 * chips - 2, 2 * chips - 1), (1, 0)]
    return forward, [(b, a) for a, b in forward]


def gather_line(state, beside=None):
    chips = lax.axis_size("zl")
    forward, backward = line_paths(chips)
    swap = lambda v: lax.ppermute(v, "co", [(0, 1), (1, 0)])
    ahead = state
    behind = state if beside is None else tie(state, beside)
    pieces = [state, swap(state)]
    for _ in range(chips - 1):
        ahead = lax.ppermute(ahead, LINE, forward)
        behind = lax.ppermute(behind, LINE, backward)
        pieces += [ahead, behind, swap(ahead), swap(behind)]
    return pieces


def on_device(
    features,
    tile_cols,
    tile_weights,
    graph_gain,
    graph_up,
    graph_down,
    lag_mix,
    time_gain,
    time_up,
    time_down,
):
    snaps, vert_dev, width = features.shape
    owners = lax.axis_size(OWNERS)
    part = vert_dev // owners
    g_gain = graph_gain[:, None, :]
    t_gain = time_gain[:, None, :]
    row_tiles, k_count = tile_cols.shape[1:]
    weights = (
        tile_weights.astype(jnp.bfloat16)
        .transpose(0, 1, 3, 2, 4)
        .reshape(snaps, row_tiles, width, k_count * width)
    )
    state = features.reshape(snaps, owners, part, width)
    for layer in range(graph_up.shape[0]):
        pieces = gather_line(state, weights if layer == 0 else None)
        graph_out = graph_stage(
            layer, tile_cols, pieces, weights, g_gain, graph_up, graph_down
        )
        owned = lax.all_to_all(graph_out, OWNERS, 0, 0, tiled=True)
        owned = owned.reshape(owners * snaps, part, width)
        finished = time_stage(layer, owned, lag_mix, t_gain, time_up, time_down)
        state = lax.all_to_all(
            finished.reshape(owners, snaps, part, width), OWNERS, 0, 0, tiled=True
        )
    return state.transpose(1, 0, 2, 3).reshape(snaps, vert_dev, width)


def solution(mesh):
    fine = Mesh(mesh.devices.reshape(2, 4, 4, 4, 2), AXES)
    snap, vert = ("zh", "x", "y"), LINE
    return jax.shard_map(
        on_device,
        mesh=fine,
        in_specs=(
            P(snap, vert, None),
            P(snap, vert, None),
            P(snap, vert, None, None, None),
        )
        + (P(),) * 7,
        out_specs=P(snap, vert, None),
        check_vma=False,
    )
```

time: 189 us -> 180 us (0.952)
  starting transfers between devices: 32.6 us -> 25.7 us
  Pallas kernels: 18.4 us -> 15.4 us
  blocking collectives: 63.2 us -> 66.1 us
    ppermute x6, waiting for transfers between devices: 59.7 us -> 48.2 us  [gather_line(): behind = lax.ppermute(behind, LINE, backward)]
    ppermute x6, waiting for transfers between devices: 0.56 us -> 9.8 us  [gather_line(): ahead = lax.ppermute(ahead, LINE, forward)]
    ppermute x2, starting transfers between devices: 15.9 us -> 9.49 us  [time_stage(): halo = lax.ppermute(own[-before:], 'zh', [(0, 1), (1, 0)])]
    ppermute x6, starting transfers between devices: 7.66 us -> 1.35 us  [gather_line(): behind = lax.ppermute(behind, LINE, backward)]
    ppermute x6, starting transfers between devices: 6.28 us -> 12.1 us  [gather_line(): ahead = lax.ppermute(ahead, LINE, forward)]
    pallas_call x4 -> x7, Pallas kernels: 18.4 us -> 15.4 us  [the longest x2 8 us: graph_stage(): pl.pallas_call(functools.partial(graph_kernel, layer, chips, layer > 0, T...]
    all_to_all x4, blocking collectives: 63.2 us -> 66.1 us  [the longest x2 36.5 us: on_device(): owned = lax.all_to_all(graph_out, OWNERS, 0, 0, tiled=True)]
    ppermute x14, waiting for transfers between devices: 2.12 us -> 4.04 us  [gather_line(): swap = lambda v: lax.ppermute(v, 'co', [(0, 1), (1, 0)])]
  transfers between devices with their start and end apart: 28 -> 28, of which waited for: 11 -> 14; matrix products, arithmetic and copies ran while one was open for 2% -> 2% of each run, Pallas kernels for 0% -> 3%
where the time goes in v2:
time: 180 us
  waiting for transfers between devices  67.5 us (38%)
  blocking collectives  66.1 us (37%)
  starting transfers between devices  25.7 us (14%)
  Pallas kernels  15.4 us (9%)
  other arithmetic  4.3 us (2%)
    ppermute x6, waiting for transfers between devices, gather_line(): behind = lax.ppermute(behind, LINE, backward)  48.2 us
    all_to_all x2, blocking collectives, on_device(): owned = lax.all_to_all(graph_out, OWNERS, 0, 0, tiled=True)  36.5 us
    all_to_all x2, blocking collectives, on_device(): lax.all_to_all(finished.reshape(owners, snaps, part, width), OWNERS, 0, 0...  29.6 us
    ppermute x6, starting transfers between devices, gather_line(): ahead = lax.ppermute(ahead, LINE, forward)  12.1 us
    ppermute x6, waiting for transfers between devices, gather_line(): ahead = lax.ppermute(ahead, LINE, forward)  9.8 us
    ppermute x2, starting transfers between devices, time_stage(): halo = lax.ppermute(own[-before:], 'zh', [(0, 1), (1, 0)])  9.49 us
    pallas_call x2, Pallas kernels, graph_stage(): pl.pallas_call(functools.partial(graph_kernel, layer, chips, layer > 0, T...  8 us
    ppermute x2, waiting for transfers between devices, time_stage(): halo = lax.ppermute(own[-before:], 'zh', [(0, 1), (1, 0)])  5.41 us
  transfers between devices with their start and end apart: 28, of which 14 were waited for; matrix products, arithmetic and copies ran while one was open for 2% of the time, Pallas kernels for 3%

profile of v2, /device:TPU:32, one launch (start us, length us, event | category | flops | bytes accessed | tf_op | source)
XLA Modules:
  0.0 180.1 jit_solution(2274601205710431667)
XLA Ops:
  0.0 1.9 %collective-permute-start.1 = (bf16[2,16,64,128]{3,2,1,0:T(8,128)(2,1)}, bf16[2,16,64,128]{3,2,1,0:T(8,128)(2,1)S(1)}, u32[]{:S(2)}, u32[]{:S(2)}) collective-permute-start(bf16[2,16,64,128]{3,2,1,0:T(8,128)(2,1)} %bitcast.23), channel_id=1, source_target_pairs={{0,2},{2,4},{4,6},{3,1},{5,3},{7,5},{6,7},{1,0},{8,10},{10,12},{12... | collective-permute-start | bytes 1572872 | tf_op jit(solution)/shard_map/ppermute | solution.py:225
  1.9 4.3 %copy_bitcast_fusion.refs_1_.refs_15_ = bf16[2,8,128,1024]{3,2,1,0:T(8,128)(2,1)S(1)} fusion(s32[2,8,8,128,128]{4,3,2,1,0:T(8,128)} %param.12), kind=kLoop, calls=%fused_computation | loop fusion | flops 2097152 | bytes 12582912 | tf_op jit(solution)/shard_map/reshape | solution.py:252
  6.5 4.7 %collective-permute-done.1.refs_3_ = bf16[2,16,64,128]{3,2,1,0:T(8,128)(2,1)S(1)} collective-permute-done((bf16[2,16,64,128]{3,2,1,0:T(8,128)(2,1)}, bf16[2,16,64,128]{3,2,1,0:T(8,128)(2,1)S(1)}, u32[]{:S(2)}, u32[]{:S(2)}) %collective-permute-start.1) | collective-permute-done | bytes 524320 | tf_op jit(solution)/shard_map/ppermute | solution.py:225
  11.3 2.4 %collective-permute-start.5 = (bf16[2,16,64,128]{3,2,1,0:T(8,128)(2,1)S(1)}, bf16[2,16,64,128]{3,2,1,0:T(8,128)(2,1)S(1)}, u32[]{:S(2)}, u32[]{:S(2)}) collective-permute-start(bf16[2,16,64,128]{3,2,1,0:T(8,128)(2,1)S(1)} %collective-permute-done.1.refs_3_), channel_id=1, source_target_pairs={{0,2},{2,4},{4,6},{3,1},{5,3},{7,5},{6,7},{1,0},{8,10},{10,12},{12... | collective-permute-start | bytes 1572872 | tf_op jit(solution)/shard_map/ppermute | solution.py:225
  13.7 6.1 %collective-permute-done.2.refs_4_ = bf16[2,16,64,128]{3,2,1,0:T(8,128)(2,1)S(1)} collective-permute-done((bf16[2,16,64,128]{3,2,1,0:T(8,128)(2,1)S(1)}, bf16[2,16,64,128]{3,2,1,0:T(8,128)(2,1)S(1)}, u32[]{:S(2)}, u32[]{:S(2)}) %collective-permute-start.2) | collective-permute-done | bytes 524320 | tf_op jit(solution)/shard_map/ppermute | solution.py:226
  20.4 3.1 %collective-permute-done.5.refs_7_ = bf16[2,16,64,128]{3,2,1,0:T(8,128)(2,1)S(1)} collective-permute-done((bf16[2,16,64,128]{3,2,1,0:T(8,128)(2,1)S(1)}, bf16[2,16,64,128]{3,2,1,0:T(8,128)(2,1)S(1)}, u32[]{:S(2)}, u32[]{:S(2)}) %collective-permute-start.5) | collective-permute-done | bytes 524320 | tf_op jit(solution)/shard_map/ppermute | solution.py:225
  23.5 2.5 %collective-permute-start.9 = (bf16[2,16,64,128]{3,2,1,0:T(8,128)(2,1)S(1)}, bf16[2,16,64,128]{3,2,1,0:T(8,128)(2,1)S(1)}, u32[]{:S(2)}, u32[]{:S(2)}) collective-permute-start(bf16[2,16,64,128]{3,2,1,0:T(8,128)(2,1)S(1)} %collective-permute-done.5.refs_7_), channel_id=1, source_target_pairs={{0,2},{2,4},{4,6},{3,1},{5,3},{7,5},{6,7},{1,0},{8,10},{10,12},{12... | collective-permute-start | bytes 1572872 | tf_op jit(solution)/shard_map/ppermute | solution.py:225
  26.0 8.0 %collective-permute-done.6.refs_8_ = bf16[2,16,64,128]{3,2,1,0:T(8,128)(2,1)S(1)} collective-permute-done((bf16[2,16,64,128]{3,2,1,0:T(8,128)(2,1)S(1)}, bf16[2,16,64,128]{3,2,1,0:T(8,128)(2,1)S(1)}, u32[]{:S(2)}, u32[]{:S(2)}) %collective-permute-start.6) | collective-permute-done | bytes 524320 | tf_op jit(solution)/shard_map/ppermute | solution.py:226
  34.6 2.0 %collective-permute-done.9.refs_11_ = bf16[2,16,64,128]{3,2,1,0:T(8,128)(2,1)S(1)} collective-permute-done((bf16[2,16,64,128]{3,2,1,0:T(8,128)(2,1)S(1)}, bf16[2,16,64,128]{3,2,1,0:T(8,128)(2,1)S(1)}, u32[]{:S(2)}, u32[]{:S(2)}) %collective-permute-start.9) | collective-permute-done | bytes 524320 | tf_op jit(solution)/shard_map/ppermute | solution.py:225
  36.6 6.9 %collective-permute-done.10.refs_12_ = bf16[2,16,64,128]{3,2,1,0:T(8,128)(2,1)S(1)} collective-permute-done((bf16[2,16,64,128]{3,2,1,0:T(8,128)(2,1)S(1)}, bf16[2,16,64,128]{3,2,1,0:T(8,128)(2,1)S(1)}, u32[]{:S(2)}, u32[]{:S(2)}) %collective-permute-start.10) | collective-permute-done | bytes 524320 | tf_op jit(solution)/shard_map/ppermute | solution.py:226
  43.5 1.9 %collective-permute-done.12.refs_14_ = bf16[2,16,64,128]{3,2,1,0:T(8,128)(2,1)S(1)} collective-permute-done((bf16[2,16,64,128]{3,2,1,0:T(8,128)(2,1)S(1)}, bf16[2,16,64,128]{3,2,1,0:T(8,128)(2,1)S(1)}, u32[]{:S(2)}, u32[]{:S(2)}) %collective-permute-start.12) | collective-permute-done | bytes 524320 | tf_op jit(solution)/shard_map/ppermute | solution.py:220
  45.5 4.0 %graph.2 = bf16[16,2,64,128]{3,2,1,0:T(8,128)(2,1)S(1)} custom-call(s32[2,8,8]{2,1,0:T(8,128)S(1)} %copy-done.6, bf16[2,16,64,128]{3,2,1,0:T(8,128)(2,1)S(1)} %bitcast.26, bf16[2,16,64,128]{3,2,1,0:T(8,128)(2,1)S(1)} %collective-permute-done.refs_2_, bf16[2,16,64,128]{3,2,1,0:T(8,128)(2,1)S(1)} %collective-permute-done.1.refs_3_, ...), custom_call_target="tpu_custom_call" | custom-call | tf_op jit(solution)/shard_map/graph/pallas_call | solution.py:114
  49.5 18.6 %all_to_all.20 = bf16[16,2,64,128]{3,2,1,0:T(8,128)(2,1)S(1)} all-to-all(bf16[16,2,64,128]{3,2,1,0:T(8,128)(2,1)S(1)} %graph.2), channel_id=1, replica_groups=mesh['zh'=2,'x'=4,'y'=4,'zl'=4,'co'=2] {'x','y'}, dimensions={0} | all-to-all | bytes 1048576 | tf_op jit(solution)/shard_map/all_to_all | solution.py:260
  68.1 4.3 %collective-permute-start.13 = (bf16[7,64,128]{2,1,0:T(8,128)(2,1)S(1)}, bf16[7,64,128]{2,1,0:T(8,128)(2,1)S(1)}, u32[]{:S(2)}, u32[]{:S(2)}) collective-permute-start(bf16[7,64,128]{2,1,0:T(8,128)(2,1)S(1)} %slice.8), channel_id=1, source_target_pairs={{0,128},{128,0},{1,129},{129,1},{2,130},{130,2},{3,131},{131,3},{4... | collective-permute-start | bytes 344072 | tf_op jit(solution)/shard_map/ppermute | solution.py:186
  72.4 2.6 %late.2.later = bf16[32,64,128]{2,1,0:T(8,128)(2,1)S(1)} custom-call(bf16[32,64,128]{2,1,0:T(8,128)(2,1)S(1)} %bitcast.16, f32[2,8,128]{2,1,0:T(8,128)S(1)} %copy-done.5, f32[2,1,128]{2,1,0:T(1,128)S(1)} %bitcast.27, bf16[2,128,1024]{2,1,0:T(8,128)(2,1)S(1)} %copy-done, bf16[2,1024,128]{2,1,0:T(8,128)(2,1)S(1)} %copy-done.1), custom_call_target="tpu_custom_call" | custom-call | tf_op jit(solution)/shard_map/late/pallas_call | solution.py:190
  75.0 3.3 %collective-permute-done.13.halo = bf16[7,64,128]{2,1,0:T(8,128)(2,1)S(1)} collective-permute-done((bf16[7,64,128]{2,1,0:T(8,128)(2,1)S(1)}, bf16[7,64,128]{2,1,0:T(8,128)(2,1)S(1)}, u32[]{:S(2)}, u32[]{:S(2)}) %collective-permute-start.13) | collective-permute-done | bytes 114720 | tf_op jit(solution)/shard_map/ppermute | solution.py:186
  78.3 1.1 early.2
  79.4 14.6 %all_to_all.21.refs_1_ = bf16[16,2,64,128]{3,2,1,0:T(8,128)(2,1)S(1)} all-to-all(bf16[16,2,64,128]{3,2,1,0:T(8,128)(2,1)S(1)} %bitcast.21), channel_id=1, replica_groups=mesh['zh'=2,'x'=4,'y'=4,'zl'=4,'co'=2] {'x','y'}, dimensions={0} | all-to-all | bytes 1048576 | tf_op jit(solution)/shard_map/all_to_all | solution.py:263
  94.1 2.0 %collective-permute-start.15 = (bf16[16,2,64,128]{3,2,1,0:T(8,128)(2,1)S(1)}, bf16[16,2,64,128]{3,2,1,0:T(8,128)(2,1)S(1)}, u32[]{:S(2)}, u32[]{:S(2)}) collective-permute-start(bf16[16,2,64,128]{3,2,1,0:T(8,128)(2,1)S(1)} %all_to_all.21.refs_1_), channel_id=1, source_target_pairs={{0,2},{2,4},{4,6},{3,1},{5,3},{7,5},{6,7},{1,0},{8,10},{10,12},{12... | collective-permute-start | bytes 1572872 | tf_op jit(solution)/shard_map/ppermute | solution.py:225
  96.1 10.2 %collective-permute-done.16.refs_4_ = bf16[16,2,64,128]{3,2,1,0:T(8,128)(2,1)S(1)} collective-permute-done((bf16[16,2,64,128]{3,2,1,0:T(8,128)(2,1)S(1)}, bf16[16,2,64,128]{3,2,1,0:T(8,128)(2,1)S(1)}, u32[]{:S(2)}, u32[]{:S(2)}) %collective-permute-start.16) | collective-permute-done | bytes 524320 | tf_op jit(solution)/shard_map/ppermute | solution.py:226
  106.6 1.7 collective-permute-start.19
  108.8 9.3 %collective-permute-done.20.refs_8_ = bf16[16,2,64,128]{3,2,1,0:T(8,128)(2,1)S(1)} collective-permute-done((bf16[16,2,64,128]{3,2,1,0:T(8,128)(2,1)S(1)}, bf16[16,2,64,128]{3,2,1,0:T(8,128)(2,1)S(1)}, u32[]{:S(2)}, u32[]{:S(2)}) %collective-permute-start.20) | collective-permute-done | bytes 524320 | tf_op jit(solution)/shard_map/ppermute | solution.py:226
  118.7 1.7 collective-permute-start.23
  121.0 7.8 %collective-permute-done.24.refs_12_ = bf16[16,2,64,128]{3,2,1,0:T(8,128)(2,1)S(1)} collective-permute-done((bf16[16,2,64,128]{3,2,1,0:T(8,128)(2,1)S(1)}, bf16[16,2,64,128]{3,2,1,0:T(8,128)(2,1)S(1)}, u32[]{:S(2)}, u32[]{:S(2)}) %collective-permute-start.24) | collective-permute-done | bytes 524320 | tf_op jit(solution)/shard_map/ppermute | solution.py:226
  129.3 1.4 collective-permute-done.26.refs_14_
  131.4 4.0 %graph.3 = bf16[16,2,64,128]{3,2,1,0:T(8,128)(2,1)S(1)} custom-call(s32[2,8,8]{2,1,0:T(8,128)S(1)} %copy-done.6, bf16[16,2,64,128]{3,2,1,0:T(8,128)(2,1)S(1)} %all_to_all.21.refs_1_, bf16[16,2,64,128]{3,2,1,0:T(8,128)(2,1)S(1)} %collective-permute-done.14.refs_2_, bf16[16,2,64,128]{3,2,1,0:T(8,128)(2,1)S(1)} %collective-permute-done.15.refs_3_, ...), custom_call_target="tpu_custom_call" | custom-call | tf_op jit(solution)/shard_map/graph/pallas_call | solution.py:114
  135.4 17.9 %all_to_all.22 = bf16[16,2,64,128]{3,2,1,0:T(8,128)(2,1)S(1)} all-to-all(bf16[16,2,64,128]{3,2,1,0:T(8,128)(2,1)S(1)} %graph.3), channel_id=1, replica_groups=mesh['zh'=2,'x'=4,'y'=4,'zl'=4,'co'=2] {'x','y'}, dimensions={0} | all-to-all | bytes 1048576 | tf_op jit(solution)/shard_map/all_to_all | solution.py:260
  153.3 5.2 %collective-permute-start.27 = (bf16[7,64,128]{2,1,0:T(8,128)(2,1)S(1)}, bf16[7,64,128]{2,1,0:T(8,128)(2,1)S(1)}, u32[]{:S(2)}, u32[]{:S(2)}) collective-permute-start(bf16[7,64,128]{2,1,0:T(8,128)(2,1)S(1)} %slice.9), channel_id=1, source_target_pairs={{0,128},{128,0},{1,129},{129,1},{2,130},{130,2},{3,131},{131,3},{4... | collective-permute-start | bytes 344072 | tf_op jit(solution)/shard_map/ppermute | solution.py:186
  158.5 2.6 %late.3.later = bf16[32,64,128]{2,1,0:T(8,128)(2,1)S(1)} custom-call(bf16[32,64,128]{2,1,0:T(8,128)(2,1)S(1)} %bitcast.19, f32[2,8,128]{2,1,0:T(8,128)S(1)} %copy-done.5, f32[2,1,128]{2,1,0:T(1,128)S(1)} %bitcast.29, bf16[2,128,1024]{2,1,0:T(8,128)(2,1)S(1)} %copy-done, bf16[2,1024,128]{2,1,0:T(8,128)(2,1)S(1)} %copy-done.1), custom_call_target="tpu_custom_call" | custom-call | tf_op jit(solution)/shard_map/late/pallas_call | solution.py:190
  161.1 2.1 %collective-permute-done.27.halo = bf16[7,64,128]{2,1,0:T(8,128)(2,1)S(1)} collective-permute-done((bf16[7,64,128]{2,1,0:T(8,128)(2,1)S(1)}, bf16[7,64,128]{2,1,0:T(8,128)(2,1)S(1)}, u32[]{:S(2)}, u32[]{:S(2)}) %collective-permute-start.27) | collective-permute-done | bytes 114720 | tf_op jit(solution)/shard_map/ppermute | solution.py:186
  163.2 1.1 early.3
  164.4 14.9 %all_to_all.23 = bf16[16,2,64,128]{3,2,1,0:T(8,128)(2,1)S(1)} all-to-all(bf16[16,2,64,128]{3,2,1,0:T(8,128)(2,1)S(1)} %bitcast.22), channel_id=1, replica_groups=mesh['zh'=2,'x'=4,'y'=4,'zl'=4,'co'=2] {'x','y'}, dimensions={0} | all-to-all | bytes 1048576 | tf_op jit(solution)/shard_map/all_to_all | solution.py:263
  (58 shorter events, 5.8 us)
Async XLA Ops:
  0.0 11.3 %collective-permute-start.1 = (bf16[2,16,64,128]{3,2,1,0:T(8,128)(2,1)}, bf16[2,16,64,128]{3,2,1,0:T(8,128)(2,1)S(1)}, u32[]{:S(2)}, u32[]{:S(2)}) collective-permute-start(bf16[2,16,64,128]{3,2,1,0:T(8,128)(2,1)} %bitcast.23), channel_id=1, source_target_pairs={{0,2},{2,4},{4,6},{3,1},{5,3},{7,5},{6,7},{1,0},{8,10},{10,12},{12... | collective-permute-start | bytes 1572872 | tf_op jit(solution)/shard_map/ppermute | solution.py:225
  6.2 39.2 %copy-start.3 = (bf16[2,128,512]{2,1,0:T(8,128)(2,1)S(1)}, bf16[2,128,512]{2,1,0:T(8,128)(2,1)}, u32[]{:S(2)}) copy-start(bf16[2,128,512]{2,1,0:T(8,128)(2,1)} %refs_17_.3) | copy-start | bytes 786436
  6.2 39.1 %copy-start.4 = (bf16[2,512,128]{2,1,0:T(8,128)(2,1)S(1)}, bf16[2,512,128]{2,1,0:T(8,128)(2,1)}, u32[]{:S(2)}) copy-start(bf16[2,512,128]{2,1,0:T(8,128)(2,1)} %refs_18_.3) | copy-start | bytes 786436
  6.3 39.1 %copy-start.6 = (s32[2,8,8]{2,1,0:T(8,128)S(1)}, s32[2,8,8]{2,1,0:T(8,128)}, u32[]{:S(2)}) copy-start(s32[2,8,8]{2,1,0:T(8,128)} %refs_0_.3) | copy-start | bytes 1540
  6.3 39.1 %copy-start.8 = (f32[2,128]{1,0:T(2,128)S(1)}, f32[2,128]{1,0:T(2,128)}, u32[]{:S(2)}) copy-start(f32[2,128]{1,0:T(2,128)} %param.13) | copy-start | bytes 3076
  6.3 13.4 %collective-permute-start.2 = (bf16[2,16,64,128]{3,2,1,0:T(8,128)(2,1)S(1)}, bf16[2,16,64,128]{3,2,1,0:T(8,128)(2,1)S(1)}, u32[]{:S(2)}, u32[]{:S(2)}) collective-permute-start(bf16[2,16,64,128]{3,2,1,0:T(8,128)(2,1)S(1)} %tie.1), channel_id=1, source_target_pairs={{2,0},{4,2},{6,4},{1,3},{3,5},{5,7},{7,6},{0,1},{10,8},{12,10},{14... | collective-permute-start | bytes 1572872 | tf_op jit(solution)/shard_map/ppermute | solution.py:226
  11.3 12.2 %collective-permute-start.5 = (bf16[2,16,64,128]{3,2,1,0:T(8,128)(2,1)S(1)}, bf16[2,16,64,128]{3,2,1,0:T(8,128)(2,1)S(1)}, u32[]{:S(2)}, u32[]{:S(2)}) collective-permute-start(bf16[2,16,64,128]{3,2,1,0:T(8,128)(2,1)S(1)} %collective-permute-done.1.refs_3_), channel_id=1, source_target_pairs={{0,2},{2,4},{4,6},{3,1},{5,3},{7,5},{6,7},{1,0},{8,10},{10,12},{12... | collective-permute-start | bytes 1572872 | tf_op jit(solution)/shard_map/ppermute | solution.py:225
  19.7 14.2 %collective-permute-start.6 = (bf16[2,16,64,128]{3,2,1,0:T(8,128)(2,1)S(1)}, bf16[2,16,64,128]{3,2,1,0:T(8,128)(2,1)S(1)}, u32[]{:S(2)}, u32[]{:S(2)}) collective-permute-start(bf16[2,16,64,128]{3,2,1,0:T(8,128)(2,1)S(1)} %collective-permute-done.2.refs_4_), channel_id=1, source_target_pairs={{2,0},{4,2},{6,4},{1,3},{3,5},{5,7},{7,6},{0,1},{10,8},{12,10},{14... | collective-permute-start | bytes 1572872 | tf_op jit(solution)/shard_map/ppermute | solution.py:226
  19.9 14.1 %collective-permute-start = (bf16[2,16,64,128]{3,2,1,0:T(8,128)(2,1)S(1)}, bf16[2,16,64,128]{3,2,1,0:T(8,128)(2,1)S(1)}, u32[]{:S(2)}, u32[]{:S(2)}) collective-permute-start(bf16[2,16,64,128]{3,2,1,0:T(8,128)(2,1)S(1)} %bitcast.25), channel_id=1, source_target_pairs={{0,1},{1,0},{2,3},{3,2},{4,5},{5,4},{6,7},{7,6},{8,9},{9,8},{10,11... | collective-permute-start | bytes 1572872 | tf_op jit(solution)/shard_map/ppermute | solution.py:220
  19.9 14.6 %collective-permute-start.3 = (bf16[2,16,64,128]{3,2,1,0:T(8,128)(2,1)S(1)}, bf16[2,16,64,128]{3,2,1,0:T(8,128)(2,1)S(1)}, u32[]{:S(2)}, u32[]{:S(2)}) collective-permute-start(bf16[2,16,64,128]{3,2,1,0:T(8,128)(2,1)S(1)} %collective-permute-done.1.refs_3_), channel_id=1, source_target_pairs={{0,1},{1,0},{2,3},{3,2},{4,5},{5,4},{6,7},{7,6},{8,9},{9,8},{10,11... | collective-permute-start | bytes 1572872 | tf_op jit(solution)/shard_map/ppermute | solution.py:220
  23.5 13.1 %collective-permute-start.9 = (bf16[2,16,64,128]{3,2,1,0:T(8,128)(2,1)S(1)}, bf16[2,16,64,128]{3,2,1,0:T(8,128)(2,1)S(1)}, u32[]{:S(2)}, u32[]{:S(2)}) collective-permute-start(bf16[2,16,64,128]{3,2,1,0:T(8,128)(2,1)S(1)} %collective-permute-done.5.refs_7_), channel_id=1, source_target_pairs={{0,2},{2,4},{4,6},{3,1},{5,3},{7,5},{6,7},{1,0},{8,10},{10,12},{12... | collective-permute-start | bytes 1572872 | tf_op jit(solution)/shard_map/ppermute | solution.py:225
  34.0 9.5 %collective-permute-start.10 = (bf16[2,16,64,128]{3,2,1,0:T(8,128)(2,1)S(1)}, bf16[2,16,64,128]{3,2,1,0:T(8,128)(2,1)S(1)}, u32[]{:S(2)}, u32[]{:S(2)}) collective-permute-start(bf16[2,16,64,128]{3,2,1,0:T(8,128)(2,1)S(1)} %collective-permute-done.6.refs_8_), channel_id=1, source_target_pairs={{2,0},{4,2},{6,4},{1,3},{3,5},{5,7},{7,6},{0,1},{10,8},{12,10},{14... | collective-permute-start | bytes 1572872 | tf_op jit(solution)/shard_map/ppermute | solution.py:226
  34.0 9.5 %collective-permute-start.4 = (bf16[2,16,64,128]{3,2,1,0:T(8,128)(2,1)S(1)}, bf16[2,16,64,128]{3,2,1,0:T(8,128)(2,1)S(1)}, u32[]{:S(2)}, u32[]{:S(2)}) collective-permute-start(bf16[2,16,64,128]{3,2,1,0:T(8,128)(2,1)S(1)} %collective-permute-done.2.refs_4_), channel_id=1, source_target_pairs={{0,1},{1,0},{2,3},{3,2},{4,5},{5,4},{6,7},{7,6},{8,9},{9,8},{10,11... | collective-permute-start | bytes 1572872 | tf_op jit(solution)/shard_map/ppermute | solution.py:220
  34.0 9.5 %collective-permute-start.7 = (bf16[2,16,64,128]{3,2,1,0:T(8,128)(2,1)S(1)}, bf16[2,16,64,128]{3,2,1,0:T(8,128)(2,1)S(1)}, u32[]{:S(2)}, u32[]{:S(2)}) collective-permute-start(bf16[2,16,64,128]{3,2,1,0:T(8,128)(2,1)S(1)} %collective-permute-done.5.refs_7_), channel_id=1, source_target_pairs={{0,1},{1,0},{2,3},{3,2},{4,5},{5,4},{6,7},{7,6},{8,9},{9,8},{10,11... | collective-permute-start | bytes 1572872 | tf_op jit(solution)/shard_map/ppermute | solution.py:220
  34.5 9.0 %collective-permute-start.8 = (bf16[2,16,64,128]{3,2,1,0:T(8,128)(2,1)S(1)}, bf16[2,16,64,128]{3,2,1,0:T(8,128)(2,1)S(1)}, u32[]{:S(2)}, u32[]{:S(2)}) collective-permute-start(bf16[2,16,64,128]{3,2,1,0:T(8,128)(2,1)S(1)} %collective-permute-done.6.refs_8_), channel_id=1, source_target_pairs={{0,1},{1,0},{2,3},{3,2},{4,5},{5,4},{6,7},{7,6},{8,9},{9,8},{10,11... | collective-permute-start | bytes 1572872 | tf_op jit(solution)/shard_map/ppermute | solution.py:220
  36.6 6.9 %collective-permute-start.11 = (bf16[2,16,64,128]{3,2,1,0:T(8,128)(2,1)S(1)}, bf16[2,16,64,128]{3,2,1,0:T(8,128)(2,1)S(1)}, u32[]{:S(2)}, u32[]{:S(2)}) collective-permute-start(bf16[2,16,64,128]{3,2,1,0:T(8,128)(2,1)S(1)} %collective-permute-done.9.refs_11_), channel_id=1, source_target_pairs={{0,1},{1,0},{2,3},{3,2},{4,5},{5,4},{6,7},{7,6},{8,9},{9,8},{10,11... | collective-permute-start | bytes 1572872 | tf_op jit(solution)/shard_map/ppermute | solution.py:220
  43.5 1.9 %collective-permute-start.12 = (bf16[2,16,64,128]{3,2,1,0:T(8,128)(2,1)S(1)}, bf16[2,16,64,128]{3,2,1,0:T(8,128)(2,1)S(1)}, u32[]{:S(2)}, u32[]{:S(2)}) collective-permute-start(bf16[2,16,64,128]{3,2,1,0:T(8,128)(2,1)S(1)} %collective-permute-done.10.refs_12_), channel_id=1, source_target_pairs={{0,1},{1,0},{2,3},{3,2},{4,5},{5,4},{6,7},{7,6},{8,9},{9,8},{10,11... | collective-permute-start | bytes 1572872 | tf_op jit(solution)/shard_map/ppermute | solution.py:220
  68.1 10.2 %collective-permute-start.13 = (bf16[7,64,128]{2,1,0:T(8,128)(2,1)S(1)}, bf16[7,64,128]{2,1,0:T(8,128)(2,1)S(1)}, u32[]{:S(2)}, u32[]{:S(2)}) collective-permute-start(bf16[7,64,128]{2,1,0:T(8,128)(2,1)S(1)} %slice.8), channel_id=1, source_target_pairs={{0,128},{128,0},{1,129},{129,1},{2,130},{130,2},{3,131},{131,3},{4... | collective-permute-start | bytes 344072 | tf_op jit(solution)/shard_map/ppermute | solution.py:186
  94.1 12.2 %collective-permute-start.16 = (bf16[16,2,64,128]{3,2,1,0:T(8,128)(2,1)S(1)}, bf16[16,2,64,128]{3,2,1,0:T(8,128)(2,1)S(1)}, u32[]{:S(2)}, u32[]{:S(2)}) collective-permute-start(bf16[16,2,64,128]{3,2,1,0:T(8,128)(2,1)S(1)} %all_to_all.21.refs_1_), channel_id=1, source_target_pairs={{2,0},{4,2},{6,4},{1,3},{3,5},{5,7},{7,6},{0,1},{10,8},{12,10},{14... | collective-permute-start | bytes 1572872 | tf_op jit(solution)/shard_map/ppermute | solution.py:226
  94.1 12.6 %collective-permute-start.15 = (bf16[16,2,64,128]{3,2,1,0:T(8,128)(2,1)S(1)}, bf16[16,2,64,128]{3,2,1,0:T(8,128)(2,1)S(1)}, u32[]{:S(2)}, u32[]{:S(2)}) collective-permute-start(bf16[16,2,64,128]{3,2,1,0:T(8,128)(2,1)S(1)} %all_to_all.21.refs_1_), channel_id=1, source_target_pairs={{0,2},{2,4},{4,6},{3,1},{5,3},{7,5},{6,7},{1,0},{8,10},{10,12},{12... | collective-permute-start | bytes 1572872 | tf_op jit(solution)/shard_map/ppermute | solution.py:225
  106.3 11.8 %collective-permute-start.20 = (bf16[16,2,64,128]{3,2,1,0:T(8,128)(2,1)S(1)}, bf16[16,2,64,128]{3,2,1,0:T(8,128)(2,1)S(1)}, u32[]{:S(2)}, u32[]{:S(2)}) collective-permute-start(bf16[16,2,64,128]{3,2,1,0:T(8,128)(2,1)S(1)} %collective-permute-done.16.refs_4_), channel_id=1, source_target_pairs={{2,0},{4,2},{6,4},{1,3},{3,5},{5,7},{7,6},{0,1},{10,8},{12,10},{14... | collective-permute-start | bytes 1572872 | tf_op jit(solution)/shard_map/ppermute | solution.py:226
  106.6 12.1 %collective-permute-start.19 = (bf16[16,2,64,128]{3,2,1,0:T(8,128)(2,1)S(1)}, bf16[16,2,64,128]{3,2,1,0:T(8,128)(2,1)S(1)}, u32[]{:S(2)}, u32[]{:S(2)}) collective-permute-start(bf16[16,2,64,128]{3,2,1,0:T(8,128)(2,1)S(1)} %collective-permute-done.15.refs_3_), channel_id=1, source_target_pairs={{0,2},{2,4},{4,6},{3,1},{5,3},{7,5},{6,7},{1,0},{8,10},{10,12},{12... | collective-permute-start | bytes 1572872 | tf_op jit(solution)/shard_map/ppermute | solution.py:225
  108.3 12.1 %collective-permute-start.14 = (bf16[16,2,64,128]{3,2,1,0:T(8,128)(2,1)S(1)}, bf16[16,2,64,128]{3,2,1,0:T(8,128)(2,1)S(1)}, u32[]{:S(2)}, u32[]{:S(2)}) collective-permute-start(bf16[16,2,64,128]{3,2,1,0:T(8,128)(2,1)S(1)} %all_to_all.21.refs_1_), channel_id=1, source_target_pairs={{0,1},{1,0},{2,3},{3,2},{4,5},{5,4},{6,7},{7,6},{8,9},{9,8},{10,11... | collective-permute-start | bytes 1572872 | tf_op jit(solution)/shard_map/ppermute | solution.py:220
  108.3 12.6 %collective-permute-start.18 = (bf16[16,2,64,128]{3,2,1,0:T(8,128)(2,1)S(1)}, bf16[16,2,64,128]{3,2,1,0:T(8,128)(2,1)S(1)}, u32[]{:S(2)}, u32[]{:S(2)}) collective-permute-start(bf16[16,2,64,128]{3,2,1,0:T(8,128)(2,1)S(1)} %collective-permute-done.16.refs_4_), channel_id=1, source_target_pairs={{0,1},{1,0},{2,3},{3,2},{4,5},{5,4},{6,7},{7,6},{8,9},{9,8},{10,11... | collective-permute-start | bytes 1572872 | tf_op jit(solution)/shard_map/ppermute | solution.py:220
  118.1 10.7 %collective-permute-start.24 = (bf16[16,2,64,128]{3,2,1,0:T(8,128)(2,1)S(1)}, bf16[16,2,64,128]{3,2,1,0:T(8,128)(2,1)S(1)}, u32[]{:S(2)}, u32[]{:S(2)}) collective-permute-start(bf16[16,2,64,128]{3,2,1,0:T(8,128)(2,1)S(1)} %collective-permute-done.20.refs_8_), channel_id=1, source_target_pairs={{2,0},{4,2},{6,4},{1,3},{3,5},{5,7},{7,6},{0,1},{10,8},{12,10},{14... | collective-permute-start | bytes 1572872 | tf_op jit(solution)/shard_map/ppermute | solution.py:226
  118.7 10.1 %collective-permute-start.23 = (bf16[16,2,64,128]{3,2,1,0:T(8,128)(2,1)S(1)}, bf16[16,2,64,128]{3,2,1,0:T(8,128)(2,1)S(1)}, u32[]{:S(2)}, u32[]{:S(2)}) collective-permute-start(bf16[16,2,64,128]{3,2,1,0:T(8,128)(2,1)S(1)} %collective-permute-done.19.refs_7_), channel_id=1, source_target_pairs={{0,2},{2,4},{4,6},{3,1},{5,3},{7,5},{6,7},{1,0},{8,10},{10,12},{12... | collective-permute-start | bytes 1572872 | tf_op jit(solution)/shard_map/ppermute | solution.py:225
  120.4 8.9 %collective-permute-start.17 = (bf16[16,2,64,128]{3,2,1,0:T(8,128)(2,1)S(1)}, bf16[16,2,64,128]{3,2,1,0:T(8,128)(2,1)S(1)}, u32[]{:S(2)}, u32[]{:S(2)}) collective-permute-start(bf16[16,2,64,128]{3,2,1,0:T(8,128)(2,1)S(1)} %collective-permute-done.15.refs_3_), channel_id=1, source_target_pairs={{0,1},{1,0},{2,3},{3,2},{4,5},{5,4},{6,7},{7,6},{8,9},{9,8},{10,11... | collective-permute-start | bytes 1572872 | tf_op jit(solution)/shard_map/ppermute | solution.py:220
  120.4 8.9 %collective-permute-start.22 = (bf16[16,2,64,128]{3,2,1,0:T(8,128)(2,1)S(1)}, bf16[16,2,64,128]{3,2,1,0:T(8,128)(2,1)S(1)}, u32[]{:S(2)}, u32[]{:S(2)}) collective-permute-start(bf16[16,2,64,128]{3,2,1,0:T(8,128)(2,1)S(1)} %collective-permute-done.20.refs_8_), channel_id=1, source_target_pairs={{0,1},{1,0},{2,3},{3,2},{4,5},{5,4},{6,7},{7,6},{8,9},{9,8},{10,11... | collective-permute-start | bytes 1572872 | tf_op jit(solution)/shard_map/ppermute | solution.py:220
  120.9 8.4 %collective-permute-start.21 = (bf16[16,2,64,128]{3,2,1,0:T(8,128)(2,1)S(1)}, bf16[16,2,64,128]{3,2,1,0:T(8,128)(2,1)S(1)}, u32[]{:S(2)}, u32[]{:S(2)}) collective-permute-start(bf16[16,2,64,128]{3,2,1,0:T(8,128)(2,1)S(1)} %collective-permute-done.19.refs_7_), channel_id=1, source_target_pairs={{0,1},{1,0},{2,3},{3,2},{4,5},{5,4},{6,7},{7,6},{8,9},{9,8},{10,11... | collective-permute-start | bytes 1572872 | tf_op jit(solution)/shard_map/ppermute | solution.py:220
  128.8 1.9 %collective-permute-start.26 = (bf16[16,2,64,128]{3,2,1,0:T(8,128)(2,1)S(1)}, bf16[16,2,64,128]{3,2,1,0:T(8,128)(2,1)S(1)}, u32[]{:S(2)}, u32[]{:S(2)}) collective-permute-start(bf16[16,2,64,128]{3,2,1,0:T(8,128)(2,1)S(1)} %collective-permute-done.24.refs_12_), channel_id=1, source_target_pairs={{0,1},{1,0},{2,3},{3,2},{4,5},{5,4},{6,7},{7,6},{8,9},{9,8},{10,11... | collective-permute-start | bytes 1572872 | tf_op jit(solution)/shard_map/ppermute | solution.py:220
  128.8 2.7 %collective-permute-start.25 = (bf16[16,2,64,128]{3,2,1,0:T(8,128)(2,1)S(1)}, bf16[16,2,64,128]{3,2,1,0:T(8,128)(2,1)S(1)}, u32[]{:S(2)}, u32[]{:S(2)}) collective-permute-start(bf16[16,2,64,128]{3,2,1,0:T(8,128)(2,1)S(1)} %collective-permute-done.23.refs_11_), channel_id=1, source_target_pairs={{0,1},{1,0},{2,3},{3,2},{4,5},{5,4},{6,7},{7,6},{8,9},{9,8},{10,11... | collective-permute-start | bytes 1572872 | tf_op jit(solution)/shard_map/ppermute | solution.py:220
  153.3 9.9 %collective-permute-start.27 = (bf16[7,64,128]{2,1,0:T(8,128)(2,1)S(1)}, bf16[7,64,128]{2,1,0:T(8,128)(2,1)S(1)}, u32[]{:S(2)}, u32[]{:S(2)}) collective-permute-start(bf16[7,64,128]{2,1,0:T(8,128)(2,1)S(1)} %slice.9), channel_id=1, source_target_pairs={{0,128},{128,0},{1,129},{129,1},{2,130},{130,2},{3,131},{131,3},{4... | collective-permute-start | bytes 344072 | tf_op jit(solution)/shard_map/ppermute | solution.py:186
  (5 other events, 114.2 us)

commit v3 on v2

--- a/solution.py
+++ b/solution.py
@@ -26,55 +26,43 @@
     return (residual.astype(jnp.float32) + 0.5 * branch).astype(jnp.bfloat16)
 
 
-def graph_kernel(layer, chips, blocked, near, *refs):
-    count = 4 * chips - 2
-    cols = refs[0]
-    pieces = refs[1 : 1 + count]
-    weights, gain, up, down, out, state, summed, sem = refs[1 + count :]
+def graph_kernel(layer, chips, blocked, *refs):
+    cols, mate = refs[:2]
+    snaps, row_tiles, k_count = cols.shape
+    owns = refs[2 : 2 + snaps]
+    moved = refs[2 + snaps : 2 + snaps + 2 * snaps * (chips - 1)]
+    rest = refs[2 + snaps + 2 * snaps * (chips - 1) :]
+    joined = rest[: chips - 1]
+    weights, gain, up, down, out, state, summed = rest[chips - 1 :]
     z, c = lax.axis_index("zl"), lax.axis_index("co")
-    snaps, row_tiles, k_count = cols.shape
     span, _, part, tile = out.shape
     per_tile = tile // part
 
-    def fetch(piece, t, slot):
-        return pltpu.make_async_copy(
-            piece.at[:, t] if blocked else piece.at[t],
-            state.at[t, pl.ds(slot * span, span)],
-            sem.at[t, slot],
-        )
-
-    def place_piece(piece, slot):
-        for t in range(snaps):
-            if near:
-                state[t, pl.ds(slot * span, span)] = piece[:, t] if blocked else piece[t]
-            else:
-                fetch(piece, t, slot).start()
-
-    if near:
-        for t in range(snaps):
-            fetch(pieces[0], t, 2 * z + c).start()
-    else:
-        place_piece(pieces[0], 2 * z + c)
-    place_piece(pieces[1], 2 * z + 1 - c)
+    def place(t, slot, value):
+        state[t, pl.ds(slot * span, span)] = value
+
+    for t in range(snaps):
+        place(t, 2 * z + c, owns[t][...])
+        place(t, 2 * z + 1 - c, mate[:, t] if blocked else mate[t])
     for step in range(1, chips):
-        ahead, behind, ahead_mate, behind_mate = pieces[4 * step - 2 : 4 * step + 2]
+        ahead = moved[2 * snaps * (step - 1) : 2 * snaps * (step - 1) + snaps]
+        behind = moved[2 * snaps * (step - 1) + snaps : 2 * snaps * step]
         shift = step * (1 - 2 * c)
 
-        def place_pair(mine, other, chip):
-            @pl.when(jnp.logical_and(chip >= 0, chip < chips))
-            def _():
-                place_piece(mine, 2 * chip + c)
-                place_piece(other, 2 * chip + 1 - c)
-
-        place_pair(ahead, behind_mate, z - shift)
-        place_pair(behind, ahead_mate, z + shift)
-
-    for t in range(snaps):
-        if near:
-            fetch(pieces[0], t, 2 * z + c).wait()
-        else:
-            for slot in range(2 * chips):
-                fetch(pieces[0], t, slot).wait()
+        @pl.when(jnp.logical_and(z - shift >= 0, z - shift < chips))
+        def _():
+            for t in range(snaps):
+                other = joined[step - 1][snaps + t]
+                place(t, 2 * (z - shift) + c, ahead[t][...])
+                place(t, 2 * (z - shift) + 1 - c, other)
+
+        @pl.when(jnp.logical_and(z + shift >= 0, z + shift < chips))
+        def _():
+            for t in range(snaps):
+                other = joined[step - 1][t]
+                place(t, 2 * (z + shift) + c, behind[t][...])
+                place(t, 2 * (z + shift) + 1 - c, other)
+
     chunk = 512
     blocks = chunk // part
 
@@ -103,29 +91,39 @@
             out[pl.ds(q * blocks, blocks), t] = done.reshape(blocks, part, tile)
 
 
-def graph_stage(layer, cols, pieces, weights, gain, up, down):
+def graph_stage(layer, cols, chips, pieces, weights, gain, up, down):
     snaps, row_tiles, _ = cols.shape
-    chips = (len(pieces) + 2) // 4
-    part, width = pieces[0].shape[2:]
-    span = row_tiles * width // part
-    any_spec = pl.BlockSpec(memory_space=pl.ANY)
+    span, part, width = pieces[1].shape
     smem = pl.BlockSpec(memory_space=pltpu.SMEM)
     vmem = pl.BlockSpec(memory_space=pltpu.VMEM)
     return pl.pallas_call(
-        functools.partial(graph_kernel, layer, chips, layer > 0, True),
+        functools.partial(graph_kernel, layer, chips, layer > 0),
         out_shape=jax.ShapeDtypeStruct((span, snaps, part, width), jnp.bfloat16),
-        in_specs=[smem, any_spec]
-        + [vmem] * (len(pieces) - 1)
-        + [vmem] * 4,
+        in_specs=[smem] + [vmem] * (len(pieces) + 4),
         out_specs=vmem,
         scratch_shapes=[
             pltpu.VMEM((snaps, 2 * chips * span, part, width), jnp.bfloat16),
             pltpu.VMEM((row_tiles * width, width), jnp.float32),
-            pltpu.SemaphoreType.DMA((snaps, 2 * chips)),
         ],
         compiler_params=pltpu.CompilerParams(vmem_limit_bytes=12 << 20),
         name="graph",
     )(cols, *pieces, weights, gain, up, down)
+
+
+def join(values):
+    def kernel(*refs):
+        for index, value in enumerate(refs[:-1]):
+            refs[-1][index] = value[...]
+
+    vmem = pl.BlockSpec(memory_space=pltpu.VMEM)
+    return pl.pallas_call(
+        kernel,
+        out_shape=jax.ShapeDtypeStruct((len(values),) + values[0].shape, values[0].dtype),
+        in_specs=[vmem] * len(values),
+        out_specs=vmem,
+        compiler_params=pltpu.CompilerParams(vmem_limit_bytes=1 << 20),
+        name="join",
+    )(*values)
 
 
 def tie(value, other):
@@ -147,7 +145,8 @@
 def late_kernel(layer, own, lags, gain, up, down, out):
     before = lags.shape[1] - 1
     rows, width = own.shape[1:]
-    for q in range(1, own.shape[0] // GROUP):
+    @pl.loop(1, own.shape[0] // GROUP)
+    def _(q):
         mixed = jnp.zeros((GROUP, rows, width), jnp.float32)
         for m in range(before + 1):
             part = own[pl.ds(q * GROUP - m, GROUP)].astype(jnp.float32)
@@ -214,18 +213,26 @@
     return forward, [(b, a) for a, b in forward]
 
 
-def gather_line(state, beside=None):
+def gather_line(state, chunks, beside=None):
     chips = lax.axis_size("zl")
     forward, backward = line_paths(chips)
     swap = lambda v: lax.ppermute(v, "co", [(0, 1), (1, 0)])
-    ahead = state
-    behind = state if beside is None else tie(state, beside)
-    pieces = [state, swap(state)]
-    for _ in range(chips - 1):
-        ahead = lax.ppermute(ahead, LINE, forward)
-        behind = lax.ppermute(behind, LINE, backward)
-        pieces += [ahead, behind, swap(ahead), swap(behind)]
-    return pieces
+    mate = swap(state)
+    ahead, behind = list(chunks), list(chunks)
+    moved, joined, last = [], [], []
+    for step in range(1, chips):
+        for t in range(len(chunks)):
+            ahead[t] = lax.ppermute(ahead[t], LINE, forward)
+            behind[t] = lax.ppermute(behind[t], LINE, backward)
+        moved += ahead + behind
+        if step < chips - 1:
+            both = join(ahead + behind)
+            if beside is not None:
+                both, beside = tie(both, beside), None
+            joined.append(swap(both))
+        else:
+            last = [swap(join(ahead + behind))]
+    return [mate, *chunks, *moved, *joined, *last]
 
 
 def on_device(
@@ -252,10 +259,11 @@
         .reshape(snaps, row_tiles, width, k_count * width)
     )
     state = features.reshape(snaps, owners, part, width)
+    chunks = [state[t] for t in range(snaps)]
     for layer in range(graph_up.shape[0]):
-        pieces = gather_line(state, weights if layer == 0 else None)
+        pieces = gather_line(state, chunks, weights if layer == 0 else None)
         graph_out = graph_stage(
-            layer, tile_cols, pieces, weights, g_gain, graph_up, graph_down
+            layer, tile_cols, lax.axis_size("zl"), pieces, weights, g_gain, graph_up, graph_down
         )
         owned = lax.all_to_all(graph_out, OWNERS, 0, 0, tiled=True)
         owned = owned.reshape(owners * snaps, part, width)
@@ -263,6 +271,7 @@
         state = lax.all_to_all(
             finished.reshape(owners, snaps, part, width), OWNERS, 0, 0, tiled=True
         )
+        chunks = [state[:, t] for t in range(snaps)]
     return state.transpose(1, 0, 2, 3).reshape(snaps, vert_dev, width)
 
 

time: 180 us -> 175 us (0.972)
  waiting for transfers between devices: 67.5 us -> 48.3 us
  starting transfers between devices: 25.7 us -> 38.9 us
  blocking collectives: 66.1 us -> 64.1 us
    ppermute x12 -> x24, waiting for transfers between devices: 58 us -> 38.9 us  [the longest x12 38.7 us: gather_line(): behind[t] = lax.ppermute(behind[t], LINE, backward)]
    ppermute x12 -> x24, starting transfers between devices: 13.5 us -> 27.6 us  [the longest x12 13.9 us: gather_line(): behind[t] = lax.ppermute(behind[t], LINE, backward)]
    ppermute x2, waiting for transfers between devices: 5.41 us -> 3.55 us  [time_stage(): halo = lax.ppermute(own[-before:], 'zh', [(0, 1), (1, 0)])]
    ppermute x14 -> x8, waiting for transfers between devices: 4.04 us -> 5.84 us  [gather_line(): swap = lambda v: lax.ppermute(v, 'co', [(0, 1), (1, 0)])]
    pallas_call x2 -> x8, Pallas kernels: 8 us -> 8.14 us  [the longest x2 7.72 us: graph_stage(): pl.pallas_call(functools.partial(graph_kernel, layer, chips, layer > 0),...]
  transfers between devices with their start and end apart: 28 -> 34, of which waited for: 14 -> 18; matrix products, arithmetic and copies ran while one was open for 2% -> 2% of each run, Pallas kernels for 3% -> 4%
where the time goes in v3:
time: 175 us
  blocking collectives  64.1 us (37%)
  waiting for transfers between devices  48.3 us (28%)
  starting transfers between devices  38.9 us (22%)
  Pallas kernels  17 us (10%)
  other arithmetic  4.3 us (2%)
  local copies, waits for them, and re-layouts  2 us (1%)
    ppermute x12, waiting for transfers between devices, gather_line(): behind[t] = lax.ppermute(behind[t], LINE, backward)  38.7 us
    all_to_all x2, blocking collectives, on_device(): owned = lax.all_to_all(graph_out, OWNERS, 0, 0, tiled=True)  35 us
    all_to_all x2, blocking collectives, on_device(): lax.all_to_all(finished.reshape(owners, snaps, part, width), OWNERS, 0, 0...  29.2 us
    ppermute x12, starting transfers between devices, gather_line(): behind[t] = lax.ppermute(behind[t], LINE, backward)  13.9 us
    ppermute x12, starting transfers between devices, gather_line(): ahead[t] = lax.ppermute(ahead[t], LINE, forward)  13.7 us
    ppermute x2, starting transfers between devices, time_stage(): halo = lax.ppermute(own[-before:], 'zh', [(0, 1), (1, 0)])  9.13 us
    pallas_call x2, Pallas kernels, graph_stage(): pl.pallas_call(functools.partial(graph_kernel, layer, chips, layer > 0),...  7.72 us
    pallas_call x2, Pallas kernels, time_stage(): pl.pallas_call(functools.partial(late_kernel, layer), out_shape=out_shape...  6.66 us
  transfers between devices with their start and end apart: 34, of which 18 were waited for; matrix products, arithmetic and copies ran while one was open for 2% of the time, Pallas kernels for 4%

profile of v3, /device:TPU:32, one launch (start us, length us, event | category | flops | bytes accessed | tf_op | source)
XLA Modules:
  0.0 175.0 jit_solution(1702236125788568081)
XLA Ops:
  5.2 4.5 %collective-permute-done.3.refs_2_.refs_6_ = bf16[16,64,128]{2,1,0:T(8,128)(2,1)S(1)} collective-permute-done((bf16[16,64,128]{2,1,0:T(8,128)(2,1)S(1)}, bf16[16,64,128]{2,1,0:T(8,128)(2,1)S(1)}, u32[]{:S(2)}, u32[]{:S(2)}) %collective-permute-start.3) | collective-permute-done | bytes 262176 | tf_op jit(solution)/shard_map/ppermute | solution.py:226
  9.7 2.5 %collective-permute-start.7 = (bf16[16,64,128]{2,1,0:T(8,128)(2,1)S(1)}, bf16[16,64,128]{2,1,0:T(8,128)(2,1)S(1)}, u32[]{:S(2)}, u32[]{:S(2)}) collective-permute-start(bf16[16,64,128]{2,1,0:T(8,128)(2,1)S(1)} %collective-permute-done.3.refs_2_.refs_6_), channel_id=1, source_target_pairs={{2,0},{4,2},{6,4},{1,3},{3,5},{5,7},{7,6},{0,1},{10,8},{12,10},{14... | collective-permute-start | bytes 786440 | tf_op jit(solution)/shard_map/ppermute | solution.py:226
  12.4 2.9 %collective-permute-done.4.refs_3_.refs_7_ = bf16[16,64,128]{2,1,0:T(8,128)(2,1)S(1)} collective-permute-done((bf16[16,64,128]{2,1,0:T(8,128)(2,1)S(1)}, bf16[16,64,128]{2,1,0:T(8,128)(2,1)S(1)}, u32[]{:S(2)}, u32[]{:S(2)}) %collective-permute-start.4) | collective-permute-done | bytes 262176 | tf_op jit(solution)/shard_map/ppermute | solution.py:226
  15.3 2.5 %collective-permute-start.8 = (bf16[16,64,128]{2,1,0:T(8,128)(2,1)S(1)}, bf16[16,64,128]{2,1,0:T(8,128)(2,1)S(1)}, u32[]{:S(2)}, u32[]{:S(2)}) collective-permute-start(bf16[16,64,128]{2,1,0:T(8,128)(2,1)S(1)} %collective-permute-done.4.refs_3_.refs_7_), channel_id=1, source_target_pairs={{2,0},{4,2},{6,4},{1,3},{3,5},{5,7},{7,6},{0,1},{10,8},{12,10},{14... | collective-permute-start | bytes 786440 | tf_op jit(solution)/shard_map/ppermute | solution.py:226
  18.0 2.9 %collective-permute-done.7.refs_2_.refs_10_ = bf16[16,64,128]{2,1,0:T(8,128)(2,1)S(1)} collective-permute-done((bf16[16,64,128]{2,1,0:T(8,128)(2,1)S(1)}, bf16[16,64,128]{2,1,0:T(8,128)(2,1)S(1)}, u32[]{:S(2)}, u32[]{:S(2)}) %collective-permute-start.7) | collective-permute-done | bytes 262176 | tf_op jit(solution)/shard_map/ppermute | solution.py:226
  20.9 2.5 %collective-permute-start.11 = (bf16[16,64,128]{2,1,0:T(8,128)(2,1)S(1)}, bf16[16,64,128]{2,1,0:T(8,128)(2,1)S(1)}, u32[]{:S(2)}, u32[]{:S(2)}) collective-permute-start(bf16[16,64,128]{2,1,0:T(8,128)(2,1)S(1)} %collective-permute-done.7.refs_2_.refs_10_), channel_id=1, source_target_pairs={{2,0},{4,2},{6,4},{1,3},{3,5},{5,7},{7,6},{0,1},{10,8},{12,10},{14... | collective-permute-start | bytes 786440 | tf_op jit(solution)/shard_map/ppermute | solution.py:226
  23.6 2.9 %collective-permute-done.8.refs_3_.refs_11_ = bf16[16,64,128]{2,1,0:T(8,128)(2,1)S(1)} collective-permute-done((bf16[16,64,128]{2,1,0:T(8,128)(2,1)S(1)}, bf16[16,64,128]{2,1,0:T(8,128)(2,1)S(1)}, u32[]{:S(2)}, u32[]{:S(2)}) %collective-permute-start.8) | collective-permute-done | bytes 262176 | tf_op jit(solution)/shard_map/ppermute | solution.py:226
  26.6 2.5 %collective-permute-start.12 = (bf16[16,64,128]{2,1,0:T(8,128)(2,1)S(1)}, bf16[16,64,128]{2,1,0:T(8,128)(2,1)S(1)}, u32[]{:S(2)}, u32[]{:S(2)}) collective-permute-start(bf16[16,64,128]{2,1,0:T(8,128)(2,1)S(1)} %collective-permute-done.8.refs_3_.refs_11_), channel_id=1, source_target_pairs={{2,0},{4,2},{6,4},{1,3},{3,5},{5,7},{7,6},{0,1},{10,8},{12,10},{14... | collective-permute-start | bytes 786440 | tf_op jit(solution)/shard_map/ppermute | solution.py:226
  29.2 4.3 %copy_bitcast_fusion.refs_1_.refs_19_ = bf16[2,8,128,1024]{3,2,1,0:T(8,128)(2,1)S(1)} fusion(s32[2,8,8,128,128]{4,3,2,1,0:T(8,128)} %param.12), kind=kLoop, calls=%fused_computation | loop fusion | flops 2097152 | bytes 12582912 | tf_op jit(solution)/shard_map/reshape | solution.py:259
  34.6 3.1 %collective-permute-done.12.refs_3_.refs_15_ = bf16[16,64,128]{2,1,0:T(8,128)(2,1)S(1)} collective-permute-done((bf16[16,64,128]{2,1,0:T(8,128)(2,1)S(1)}, bf16[16,64,128]{2,1,0:T(8,128)(2,1)S(1)}, u32[]{:S(2)}, u32[]{:S(2)}) %collective-permute-start.12) | collective-permute-done | bytes 262176 | tf_op jit(solution)/shard_map/ppermute | solution.py:226
  38.5 2.9 %collective-permute-done.refs_1_ = bf16[2,16,64,128]{3,2,1,0:T(8,128)(2,1)S(1)} collective-permute-done((bf16[2,16,64,128]{3,2,1,0:T(8,128)(2,1)S(1)}, bf16[2,16,64,128]{3,2,1,0:T(8,128)(2,1)S(1)}, u32[]{:S(2)}, u32[]{:S(2)}) %collective-permute-start) | collective-permute-done | bytes 524320 | tf_op jit(solution)/shard_map/ppermute | solution.py:219
  41.5 3.9 %graph.2 = bf16[16,2,64,128]{3,2,1,0:T(8,128)(2,1)S(1)} custom-call(s32[2,8,8]{2,1,0:T(8,128)S(1)} %copy-done.5, bf16[2,16,64,128]{3,2,1,0:T(8,128)(2,1)S(1)} %collective-permute-done.refs_1_, bf16[16,64,128]{2,1,0:T(8,128)(2,1)S(1)} %bitcast.38, bf16[16,64,128]{2,1,0:T(8,128)(2,1)S(1)} %bitcast.35, ...), custom_call_target="tpu_custom_call" | custom-call | tf_op jit(solution)/shard_map/graph/pallas_call | solution.py:99
  45.4 18.9 %all_to_all.20 = bf16[16,2,64,128]{3,2,1,0:T(8,128)(2,1)S(1)} all-to-all(bf16[16,2,64,128]{3,2,1,0:T(8,128)(2,1)S(1)} %graph.2), channel_id=1, replica_groups=mesh['zh'=2,'x'=4,'y'=4,'zl'=4,'co'=2] {'x','y'}, dimensions={0} | all-to-all | bytes 1048576 | tf_op jit(solution)/shard_map/all_to_all | solution.py:268
  64.3 6.3 %collective-permute-start.16 = (bf16[7,64,128]{2,1,0:T(8,128)(2,1)S(1)}, bf16[7,64,128]{2,1,0:T(8,128)(2,1)S(1)}, u32[]{:S(2)}, u32[]{:S(2)}) collective-permute-start(bf16[7,64,128]{2,1,0:T(8,128)(2,1)S(1)} %slice.26), channel_id=1, source_target_pairs={{0,128},{128,0},{1,129},{129,1},{2,130},{130,2},{3,131},{131,3},{4... | collective-permute-start | bytes 344072 | tf_op jit(solution)/shard_map/ppermute | solution.py:185
  70.6 3.3 %late.2.later = bf16[32,64,128]{2,1,0:T(8,128)(2,1)S(1)} custom-call(bf16[32,64,128]{2,1,0:T(8,128)(2,1)S(1)} %bitcast.26, f32[2,8,128]{2,1,0:T(8,128)S(1)} %copy-done.4, f32[2,1,128]{2,1,0:T(1,128)S(1)} %bitcast.39, bf16[2,128,1024]{2,1,0:T(8,128)(2,1)S(1)} %copy-done, bf16[2,1024,128]{2,1,0:T(8,128)(2,1)S(1)} %copy-done.1), custom_call_target="tpu_custom_call" | custom-call | tf_op jit(solution)/shard_map/late/pallas_call | solution.py:189
  75.1 14.8 %all_to_all.21 = bf16[16,2,64,128]{3,2,1,0:T(8,128)(2,1)S(1)} all-to-all(bf16[16,2,64,128]{3,2,1,0:T(8,128)(2,1)S(1)} %bitcast.31), channel_id=1, replica_groups=mesh['zh'=2,'x'=4,'y'=4,'zl'=4,'co'=2] {'x','y'}, dimensions={0} | all-to-all | bytes 1048576 | tf_op jit(solution)/shard_map/all_to_all | solution.py:271
  90.1 2.4 %collective-permute-start.19 = (bf16[16,64,128]{2,1,0:T(8,128)(2,1)S(1)}, bf16[16,64,128]{2,1,0:T(8,128)(2,1)S(1)}, u32[]{:S(2)}, u32[]{:S(2)}) collective-permute-start(bf16[16,64,128]{2,1,0:T(8,128)(2,1)S(1)} %get-tuple-element.5.refs_3_), channel_id=1, source_target_pairs={{0,2},{2,4},{4,6},{3,1},{5,3},{7,5},{6,7},{1,0},{8,10},{10,12},{12... | collective-permute-start | bytes 786440 | tf_op jit(solution)/shard_map/ppermute | solution.py:225
  94.5 5.1 %collective-permute-done.21.refs_3_.refs_7_ = bf16[16,64,128]{2,1,0:T(8,128)(2,1)S(1)} collective-permute-done((bf16[16,64,128]{2,1,0:T(8,128)(2,1)S(1)}, bf16[16,64,128]{2,1,0:T(8,128)(2,1)S(1)}, u32[]{:S(2)}, u32[]{:S(2)}) %collective-permute-start.21) | collective-permute-done | bytes 262176 | tf_op jit(solution)/shard_map/ppermute | solution.py:226
  99.6 2.1 %collective-permute-start.23 = (bf16[16,64,128]{2,1,0:T(8,128)(2,1)S(1)}, bf16[16,64,128]{2,1,0:T(8,128)(2,1)S(1)}, u32[]{:S(2)}, u32[]{:S(2)}) collective-permute-start(bf16[16,64,128]{2,1,0:T(8,128)(2,1)S(1)} %collective-permute-done.19.refs_1_.refs_5_), channel_id=1, source_target_pairs={{0,2},{2,4},{4,6},{3,1},{5,3},{7,5},{6,7},{1,0},{8,10},{10,12},{12... | collective-permute-start | bytes 786440 | tf_op jit(solution)/shard_map/ppermute | solution.py:225
  101.7 3.5 %collective-permute-done.20.refs_2_.refs_6_ = bf16[16,64,128]{2,1,0:T(8,128)(2,1)S(1)} collective-permute-done((bf16[16,64,128]{2,1,0:T(8,128)(2,1)S(1)}, bf16[16,64,128]{2,1,0:T(8,128)(2,1)S(1)}, u32[]{:S(2)}, u32[]{:S(2)}) %collective-permute-start.20) | collective-permute-done | bytes 262176 | tf_op jit(solution)/shard_map/ppermute | solution.py:226
  107.4 3.5 %collective-permute-done.25.refs_3_.refs_11_ = bf16[16,64,128]{2,1,0:T(8,128)(2,1)S(1)} collective-permute-done((bf16[16,64,128]{2,1,0:T(8,128)(2,1)S(1)}, bf16[16,64,128]{2,1,0:T(8,128)(2,1)S(1)}, u32[]{:S(2)}, u32[]{:S(2)}) %collective-permute-start.25) | collective-permute-done | bytes 262176 | tf_op jit(solution)/shard_map/ppermute | solution.py:226
  110.9 2.1 %collective-permute-start.27 = (bf16[16,64,128]{2,1,0:T(8,128)(2,1)S(1)}, bf16[16,64,128]{2,1,0:T(8,128)(2,1)S(1)}, u32[]{:S(2)}, u32[]{:S(2)}) collective-permute-start(bf16[16,64,128]{2,1,0:T(8,128)(2,1)S(1)} %collective-permute-done.23.refs_1_.refs_9_), channel_id=1, source_target_pairs={{0,2},{2,4},{4,6},{3,1},{5,3},{7,5},{6,7},{1,0},{8,10},{10,12},{12... | collective-permute-start | bytes 786440 | tf_op jit(solution)/shard_map/ppermute | solution.py:225
  113.0 3.5 %collective-permute-done.24.refs_2_.refs_10_ = bf16[16,64,128]{2,1,0:T(8,128)(2,1)S(1)} collective-permute-done((bf16[16,64,128]{2,1,0:T(8,128)(2,1)S(1)}, bf16[16,64,128]{2,1,0:T(8,128)(2,1)S(1)}, u32[]{:S(2)}, u32[]{:S(2)}) %collective-permute-start.24) | collective-permute-done | bytes 262176 | tf_op jit(solution)/shard_map/ppermute | solution.py:226
  118.8 3.3 %collective-permute-done.29.refs_3_.refs_15_ = bf16[16,64,128]{2,1,0:T(8,128)(2,1)S(1)} collective-permute-done((bf16[16,64,128]{2,1,0:T(8,128)(2,1)S(1)}, bf16[16,64,128]{2,1,0:T(8,128)(2,1)S(1)}, u32[]{:S(2)}, u32[]{:S(2)}) %collective-permute-start.29) | collective-permute-done | bytes 262176 | tf_op jit(solution)/shard_map/ppermute | solution.py:226
  122.1 3.4 %collective-permute-done.28.refs_2_.refs_14_ = bf16[16,64,128]{2,1,0:T(8,128)(2,1)S(1)} collective-permute-done((bf16[16,64,128]{2,1,0:T(8,128)(2,1)S(1)}, bf16[16,64,128]{2,1,0:T(8,128)(2,1)S(1)}, u32[]{:S(2)}, u32[]{:S(2)}) %collective-permute-start.28) | collective-permute-done | bytes 262176 | tf_op jit(solution)/shard_map/ppermute | solution.py:226
  126.1 2.9 %collective-permute-done.17.refs_1_ = bf16[16,2,64,128]{3,2,1,0:T(8,128)(2,1)S(1)} collective-permute-done((bf16[16,2,64,128]{3,2,1,0:T(8,128)(2,1)S(1)}, bf16[16,2,64,128]{3,2,1,0:T(8,128)(2,1)S(1)}, u32[]{:S(2)}, u32[]{:S(2)}) %collective-permute-start.17) | collective-permute-done | bytes 524320 | tf_op jit(solution)/shard_map/ppermute | solution.py:219
  129.0 3.9 %graph.3 = bf16[16,2,64,128]{3,2,1,0:T(8,128)(2,1)S(1)} custom-call(s32[2,8,8]{2,1,0:T(8,128)S(1)} %copy-done.5, bf16[16,2,64,128]{3,2,1,0:T(8,128)(2,1)S(1)} %collective-permute-done.17.refs_1_, bf16[16,64,128]{2,1,0:T(8,128)(2,1)S(1)} %get-tuple-element.6.refs_2_, bf16[16,64,128]{2,1,0:T(8,128)(2,1)S(1)} %get-tuple-element.5.refs_3_, ...), custom_call_target="tpu_custom_call" | custom-call | tf_op jit(solution)/shard_map/graph/pallas_call | solution.py:99
  132.9 16.1 %all_to_all.22 = bf16[16,2,64,128]{3,2,1,0:T(8,128)(2,1)S(1)} all-to-all(bf16[16,2,64,128]{3,2,1,0:T(8,128)(2,1)S(1)} %graph.3), channel_id=1, replica_groups=mesh['zh'=2,'x'=4,'y'=4,'zl'=4,'co'=2] {'x','y'}, dimensions={0} | all-to-all | bytes 1048576 | tf_op jit(solution)/shard_map/all_to_all | solution.py:268
  149.1 2.8 %collective-permute-start.33 = (bf16[7,64,128]{2,1,0:T(8,128)(2,1)S(1)}, bf16[7,64,128]{2,1,0:T(8,128)(2,1)S(1)}, u32[]{:S(2)}, u32[]{:S(2)}) collective-permute-start(bf16[7,64,128]{2,1,0:T(8,128)(2,1)S(1)} %slice.29), channel_id=1, source_target_pairs={{0,128},{128,0},{1,129},{129,1},{2,130},{130,2},{3,131},{131,3},{4... | collective-permute-start | bytes 344072 | tf_op jit(solution)/shard_map/ppermute | solution.py:185
  151.9 3.3 %late.3.later = bf16[32,64,128]{2,1,0:T(8,128)(2,1)S(1)} custom-call(bf16[32,64,128]{2,1,0:T(8,128)(2,1)S(1)} %bitcast.29, f32[2,8,128]{2,1,0:T(8,128)S(1)} %copy-done.4, f32[2,1,128]{2,1,0:T(1,128)S(1)} %bitcast.41, bf16[2,128,1024]{2,1,0:T(8,128)(2,1)S(1)} %copy-done, bf16[2,1024,128]{2,1,0:T(8,128)(2,1)S(1)} %copy-done.1), custom_call_target="tpu_custom_call" | custom-call | tf_op jit(solution)/shard_map/late/pallas_call | solution.py:189
  155.2 3.5 %collective-permute-done.33.halo = bf16[7,64,128]{2,1,0:T(8,128)(2,1)S(1)} collective-permute-done((bf16[7,64,128]{2,1,0:T(8,128)(2,1)S(1)}, bf16[7,64,128]{2,1,0:T(8,128)(2,1)S(1)}, u32[]{:S(2)}, u32[]{:S(2)}) %collective-permute-start.33) | collective-permute-done | bytes 114720 | tf_op jit(solution)/shard_map/ppermute | solution.py:185
  159.9 14.3 %all_to_all.23 = bf16[16,2,64,128]{3,2,1,0:T(8,128)(2,1)S(1)} all-to-all(bf16[16,2,64,128]{3,2,1,0:T(8,128)(2,1)S(1)} %bitcast.32), channel_id=1, replica_groups=mesh['zh'=2,'x'=4,'y'=4,'zl'=4,'co'=2] {'x','y'}, dimensions={0} | all-to-all | bytes 1048576 | tf_op jit(solution)/shard_map/all_to_all | solution.py:271
  (77 shorter events, 18.2 us)
Async XLA Ops:
  1.1 8.6 %collective-permute-start.3 = (bf16[16,64,128]{2,1,0:T(8,128)(2,1)S(1)}, bf16[16,64,128]{2,1,0:T(8,128)(2,1)S(1)}, u32[]{:S(2)}, u32[]{:S(2)}) collective-permute-start(bf16[16,64,128]{2,1,0:T(8,128)(2,1)S(1)} %bitcast.36), channel_id=1, source_target_pairs={{2,0},{4,2},{6,4},{1,3},{3,5},{5,7},{7,6},{0,1},{10,8},{12,10},{14... | collective-permute-start | bytes 786440 | tf_op jit(solution)/shard_map/ppermute | solution.py:226
  3.0 9.2 %collective-permute-start.1 = (bf16[16,64,128]{2,1,0:T(8,128)(2,1)S(1)}, bf16[16,64,128]{2,1,0:T(8,128)(2,1)S(1)}, u32[]{:S(2)}, u32[]{:S(2)}) collective-permute-start(bf16[16,64,128]{2,1,0:T(8,128)(2,1)S(1)} %bitcast.37), channel_id=1, source_target_pairs={{0,2},{2,4},{4,6},{3,1},{5,3},{7,5},{6,7},{1,0},{8,10},{10,12},{12... | collective-permute-start | bytes 786440 | tf_op jit(solution)/shard_map/ppermute | solution.py:225
  3.2 12.1 %collective-permute-start.4 = (bf16[16,64,128]{2,1,0:T(8,128)(2,1)S(1)}, bf16[16,64,128]{2,1,0:T(8,128)(2,1)S(1)}, u32[]{:S(2)}, u32[]{:S(2)}) collective-permute-start(bf16[16,64,128]{2,1,0:T(8,128)(2,1)S(1)} %bitcast.33), channel_id=1, source_target_pairs={{2,0},{4,2},{6,4},{1,3},{3,5},{5,7},{7,6},{0,1},{10,8},{12,10},{14... | collective-permute-start | bytes 786440 | tf_op jit(solution)/shard_map/ppermute | solution.py:226
  5.0 12.8 %collective-permute-start.2 = (bf16[16,64,128]{2,1,0:T(8,128)(2,1)S(1)}, bf16[16,64,128]{2,1,0:T(8,128)(2,1)S(1)}, u32[]{:S(2)}, u32[]{:S(2)}) collective-permute-start(bf16[16,64,128]{2,1,0:T(8,128)(2,1)S(1)} %bitcast.34), channel_id=1, source_target_pairs={{0,2},{2,4},{4,6},{3,1},{5,3},{7,5},{6,7},{1,0},{8,10},{10,12},{12... | collective-permute-start | bytes 786440 | tf_op jit(solution)/shard_map/ppermute | solution.py:225
  9.7 11.2 %collective-permute-start.7 = (bf16[16,64,128]{2,1,0:T(8,128)(2,1)S(1)}, bf16[16,64,128]{2,1,0:T(8,128)(2,1)S(1)}, u32[]{:S(2)}, u32[]{:S(2)}) collective-permute-start(bf16[16,64,128]{2,1,0:T(8,128)(2,1)S(1)} %collective-permute-done.3.refs_2_.refs_6_), channel_id=1, source_target_pairs={{2,0},{4,2},{6,4},{1,3},{3,5},{5,7},{7,6},{0,1},{10,8},{12,10},{14... | collective-permute-start | bytes 786440 | tf_op jit(solution)/shard_map/ppermute | solution.py:226
  12.2 11.2 %collective-permute-start.5 = (bf16[16,64,128]{2,1,0:T(8,128)(2,1)S(1)}, bf16[16,64,128]{2,1,0:T(8,128)(2,1)S(1)}, u32[]{:S(2)}, u32[]{:S(2)}) collective-permute-start(bf16[16,64,128]{2,1,0:T(8,128)(2,1)S(1)} %collective-permute-done.1.refs_0_.refs_4_), channel_id=1, source_target_pairs={{0,2},{2,4},{4,6},{3,1},{5,3},{7,5},{6,7},{1,0},{8,10},{10,12},{12... | collective-permute-start | bytes 786440 | tf_op jit(solution)/shard_map/ppermute | solution.py:225
  15.3 11.2 %collective-permute-start.8 = (bf16[16,64,128]{2,1,0:T(8,128)(2,1)S(1)}, bf16[16,64,128]{2,1,0:T(8,128)(2,1)S(1)}, u32[]{:S(2)}, u32[]{:S(2)}) collective-permute-start(bf16[16,64,128]{2,1,0:T(8,128)(2,1)S(1)} %collective-permute-done.4.refs_3_.refs_7_), channel_id=1, source_target_pairs={{2,0},{4,2},{6,4},{1,3},{3,5},{5,7},{7,6},{0,1},{10,8},{12,10},{14... | collective-permute-start | bytes 786440 | tf_op jit(solution)/shard_map/ppermute | solution.py:226
  17.9 11.2 %collective-permute-start.6 = (bf16[16,64,128]{2,1,0:T(8,128)(2,1)S(1)}, bf16[16,64,128]{2,1,0:T(8,128)(2,1)S(1)}, u32[]{:S(2)}, u32[]{:S(2)}) collective-permute-start(bf16[16,64,128]{2,1,0:T(8,128)(2,1)S(1)} %collective-permute-done.2.refs_1_.refs_5_), channel_id=1, source_target_pairs={{0,2},{2,4},{4,6},{3,1},{5,3},{7,5},{6,7},{1,0},{8,10},{10,12},{12... | collective-permute-start | bytes 786440 | tf_op jit(solution)/shard_map/ppermute | solution.py:225
  20.9 12.9 %collective-permute-start.11 = (bf16[16,64,128]{2,1,0:T(8,128)(2,1)S(1)}, bf16[16,64,128]{2,1,0:T(8,128)(2,1)S(1)}, u32[]{:S(2)}, u32[]{:S(2)}) collective-permute-start(bf16[16,64,128]{2,1,0:T(8,128)(2,1)S(1)} %collective-permute-done.7.refs_2_.refs_10_), channel_id=1, source_target_pairs={{2,0},{4,2},{6,4},{1,3},{3,5},{5,7},{7,6},{0,1},{10,8},{12,10},{14... | collective-permute-start | bytes 786440 | tf_op jit(solution)/shard_map/ppermute | solution.py:226
  23.5 11.2 %collective-permute-start.9 = (bf16[16,64,128]{2,1,0:T(8,128)(2,1)S(1)}, bf16[16,64,128]{2,1,0:T(8,128)(2,1)S(1)}, u32[]{:S(2)}, u32[]{:S(2)}) collective-permute-start(bf16[16,64,128]{2,1,0:T(8,128)(2,1)S(1)} %collective-permute-done.5.refs_0_.refs_8_), channel_id=1, source_target_pairs={{0,2},{2,4},{4,6},{3,1},{5,3},{7,5},{6,7},{1,0},{8,10},{10,12},{12... | collective-permute-start | bytes 786440 | tf_op jit(solution)/shard_map/ppermute | solution.py:225
  26.6 11.2 %collective-permute-start.12 = (bf16[16,64,128]{2,1,0:T(8,128)(2,1)S(1)}, bf16[16,64,128]{2,1,0:T(8,128)(2,1)S(1)}, u32[]{:S(2)}, u32[]{:S(2)}) collective-permute-start(bf16[16,64,128]{2,1,0:T(8,128)(2,1)S(1)} %collective-permute-done.8.refs_3_.refs_11_), channel_id=1, source_target_pairs={{2,0},{4,2},{6,4},{1,3},{3,5},{5,7},{7,6},{0,1},{10,8},{12,10},{14... | collective-permute-start | bytes 786440 | tf_op jit(solution)/shard_map/ppermute | solution.py:226
  29.1 8.7 %collective-permute-start.10 = (bf16[16,64,128]{2,1,0:T(8,128)(2,1)S(1)}, bf16[16,64,128]{2,1,0:T(8,128)(2,1)S(1)}, u32[]{:S(2)}, u32[]{:S(2)}) collective-permute-start(bf16[16,64,128]{2,1,0:T(8,128)(2,1)S(1)} %collective-permute-done.6.refs_1_.refs_9_), channel_id=1, source_target_pairs={{0,2},{2,4},{4,6},{3,1},{5,3},{7,5},{6,7},{1,0},{8,10},{10,12},{12... | collective-permute-start | bytes 786440 | tf_op jit(solution)/shard_map/ppermute | solution.py:225
  33.7 7.7 %collective-permute-start.13 = (bf16[4,16,64,128]{3,2,1,0:T(8,128)(2,1)S(1)}, bf16[4,16,64,128]{3,2,1,0:T(8,128)(2,1)S(1)}, u32[]{:S(2)}, u32[]{:S(2)}) collective-permute-start(bf16[4,16,64,128]{3,2,1,0:T(8,128)(2,1)S(1)} %tie.1), channel_id=1, source_target_pairs={{0,1},{1,0},{2,3},{3,2},{4,5},{5,4},{6,7},{7,6},{8,9},{9,8},{10,11... | collective-permute-start | bytes 3145736 | tf_op jit(solution)/shard_map/ppermute | solution.py:219
  33.9 7.6 %collective-permute-start.14 = (bf16[4,16,64,128]{3,2,1,0:T(8,128)(2,1)S(1)}, bf16[4,16,64,128]{3,2,1,0:T(8,128)(2,1)S(1)}, u32[]{:S(2)}, u32[]{:S(2)}) collective-permute-start(bf16[4,16,64,128]{3,2,1,0:T(8,128)(2,1)S(1)} %join.7), channel_id=1, source_target_pairs={{0,1},{1,0},{2,3},{3,2},{4,5},{5,4},{6,7},{7,6},{8,9},{9,8},{10,11... | collective-permute-start | bytes 3145736 | tf_op jit(solution)/shard_map/ppermute | solution.py:219
  37.8 3.6 %collective-permute-start.15 = (bf16[4,16,64,128]{3,2,1,0:T(8,128)(2,1)S(1)}, bf16[4,16,64,128]{3,2,1,0:T(8,128)(2,1)S(1)}, u32[]{:S(2)}, u32[]{:S(2)}) collective-permute-start(bf16[4,16,64,128]{3,2,1,0:T(8,128)(2,1)S(1)} %join.8), channel_id=1, source_target_pairs={{0,1},{1,0},{2,3},{3,2},{4,5},{5,4},{6,7},{7,6},{8,9},{9,8},{10,11... | collective-permute-start | bytes 3145736 | tf_op jit(solution)/shard_map/ppermute | solution.py:219
  64.3 9.7 %collective-permute-start.16 = (bf16[7,64,128]{2,1,0:T(8,128)(2,1)S(1)}, bf16[7,64,128]{2,1,0:T(8,128)(2,1)S(1)}, u32[]{:S(2)}, u32[]{:S(2)}) collective-permute-start(bf16[7,64,128]{2,1,0:T(8,128)(2,1)S(1)} %slice.26), channel_id=1, source_target_pairs={{0,128},{128,0},{1,129},{129,1},{2,130},{130,2},{3,131},{131,3},{4... | collective-permute-start | bytes 344072 | tf_op jit(solution)/shard_map/ppermute | solution.py:185
  89.9 9.7 %collective-permute-start.21 = (bf16[16,64,128]{2,1,0:T(8,128)(2,1)S(1)}, bf16[16,64,128]{2,1,0:T(8,128)(2,1)S(1)}, u32[]{:S(2)}, u32[]{:S(2)}) collective-permute-start(bf16[16,64,128]{2,1,0:T(8,128)(2,1)S(1)} %get-tuple-element.5.refs_3_), channel_id=1, source_target_pairs={{2,0},{4,2},{6,4},{1,3},{3,5},{5,7},{7,6},{0,1},{10,8},{12,10},{14... | collective-permute-start | bytes 786440 | tf_op jit(solution)/shard_map/ppermute | solution.py:226
  90.1 9.5 %collective-permute-start.19 = (bf16[16,64,128]{2,1,0:T(8,128)(2,1)S(1)}, bf16[16,64,128]{2,1,0:T(8,128)(2,1)S(1)}, u32[]{:S(2)}, u32[]{:S(2)}) collective-permute-start(bf16[16,64,128]{2,1,0:T(8,128)(2,1)S(1)} %get-tuple-element.5.refs_3_), channel_id=1, source_target_pairs={{0,2},{2,4},{4,6},{3,1},{5,3},{7,5},{6,7},{1,0},{8,10},{10,12},{12... | collective-permute-start | bytes 786440 | tf_op jit(solution)/shard_map/ppermute | solution.py:225
  92.5 12.8 %collective-permute-start.20 = (bf16[16,64,128]{2,1,0:T(8,128)(2,1)S(1)}, bf16[16,64,128]{2,1,0:T(8,128)(2,1)S(1)}, u32[]{:S(2)}, u32[]{:S(2)}) collective-permute-start(bf16[16,64,128]{2,1,0:T(8,128)(2,1)S(1)} %get-tuple-element.6.refs_2_), channel_id=1, source_target_pairs={{2,0},{4,2},{6,4},{1,3},{3,5},{5,7},{7,6},{0,1},{10,8},{12,10},{14... | collective-permute-start | bytes 786440 | tf_op jit(solution)/shard_map/ppermute | solution.py:226
  92.5 12.8 %collective-permute-start.18 = (bf16[16,64,128]{2,1,0:T(8,128)(2,1)S(1)}, bf16[16,64,128]{2,1,0:T(8,128)(2,1)S(1)}, u32[]{:S(2)}, u32[]{:S(2)}) collective-permute-start(bf16[16,64,128]{2,1,0:T(8,128)(2,1)S(1)} %get-tuple-element.6.refs_2_), channel_id=1, source_target_pairs={{0,2},{2,4},{4,6},{3,1},{5,3},{7,5},{6,7},{1,0},{8,10},{10,12},{12... | collective-permute-start | bytes 786440 | tf_op jit(solution)/shard_map/ppermute | solution.py:225
  99.6 11.2 %collective-permute-start.25 = (bf16[16,64,128]{2,1,0:T(8,128)(2,1)S(1)}, bf16[16,64,128]{2,1,0:T(8,128)(2,1)S(1)}, u32[]{:S(2)}, u32[]{:S(2)}) collective-permute-start(bf16[16,64,128]{2,1,0:T(8,128)(2,1)S(1)} %collective-permute-done.21.refs_3_.refs_7_), channel_id=1, source_target_pairs={{2,0},{4,2},{6,4},{1,3},{3,5},{5,7},{7,6},{0,1},{10,8},{12,10},{14... | collective-permute-start | bytes 786440 | tf_op jit(solution)/shard_map/ppermute | solution.py:226
  99.6 11.2 %collective-permute-start.23 = (bf16[16,64,128]{2,1,0:T(8,128)(2,1)S(1)}, bf16[16,64,128]{2,1,0:T(8,128)(2,1)S(1)}, u32[]{:S(2)}, u32[]{:S(2)}) collective-permute-start(bf16[16,64,128]{2,1,0:T(8,128)(2,1)S(1)} %collective-permute-done.19.refs_1_.refs_5_), channel_id=1, source_target_pairs={{0,2},{2,4},{4,6},{3,1},{5,3},{7,5},{6,7},{1,0},{8,10},{10,12},{12... | collective-permute-start | bytes 786440 | tf_op jit(solution)/shard_map/ppermute | solution.py:225
  105.2 11.2 %collective-permute-start.24 = (bf16[16,64,128]{2,1,0:T(8,128)(2,1)S(1)}, bf16[16,64,128]{2,1,0:T(8,128)(2,1)S(1)}, u32[]{:S(2)}, u32[]{:S(2)}) collective-permute-start(bf16[16,64,128]{2,1,0:T(8,128)(2,1)S(1)} %collective-permute-done.20.refs_2_.refs_6_), channel_id=1, source_target_pairs={{2,0},{4,2},{6,4},{1,3},{3,5},{5,7},{7,6},{0,1},{10,8},{12,10},{14... | collective-permute-start | bytes 786440 | tf_op jit(solution)/shard_map/ppermute | solution.py:226
  105.2 11.2 %collective-permute-start.22 = (bf16[16,64,128]{2,1,0:T(8,128)(2,1)S(1)}, bf16[16,64,128]{2,1,0:T(8,128)(2,1)S(1)}, u32[]{:S(2)}, u32[]{:S(2)}) collective-permute-start(bf16[16,64,128]{2,1,0:T(8,128)(2,1)S(1)} %collective-permute-done.18.refs_0_.refs_4_), channel_id=1, source_target_pairs={{0,2},{2,4},{4,6},{3,1},{5,3},{7,5},{6,7},{1,0},{8,10},{10,12},{12... | collective-permute-start | bytes 786440 | tf_op jit(solution)/shard_map/ppermute | solution.py:225
  110.9 11.2 %collective-permute-start.29 = (bf16[16,64,128]{2,1,0:T(8,128)(2,1)S(1)}, bf16[16,64,128]{2,1,0:T(8,128)(2,1)S(1)}, u32[]{:S(2)}, u32[]{:S(2)}) collective-permute-start(bf16[16,64,128]{2,1,0:T(8,128)(2,1)S(1)} %collective-permute-done.25.refs_3_.refs_11_), channel_id=1, source_target_pairs={{2,0},{4,2},{6,4},{1,3},{3,5},{5,7},{7,6},{0,1},{10,8},{12,10},{14... | collective-permute-start | bytes 786440 | tf_op jit(solution)/shard_map/ppermute | solution.py:226
  110.9 11.2 %collective-permute-start.27 = (bf16[16,64,128]{2,1,0:T(8,128)(2,1)S(1)}, bf16[16,64,128]{2,1,0:T(8,128)(2,1)S(1)}, u32[]{:S(2)}, u32[]{:S(2)}) collective-permute-start(bf16[16,64,128]{2,1,0:T(8,128)(2,1)S(1)} %collective-permute-done.23.refs_1_.refs_9_), channel_id=1, source_target_pairs={{0,2},{2,4},{4,6},{3,1},{5,3},{7,5},{6,7},{1,0},{8,10},{10,12},{12... | collective-permute-start | bytes 786440 | tf_op jit(solution)/shard_map/ppermute | solution.py:225
  116.5 9.0 %collective-permute-start.28 = (bf16[16,64,128]{2,1,0:T(8,128)(2,1)S(1)}, bf16[16,64,128]{2,1,0:T(8,128)(2,1)S(1)}, u32[]{:S(2)}, u32[]{:S(2)}) collective-permute-start(bf16[16,64,128]{2,1,0:T(8,128)(2,1)S(1)} %collective-permute-done.24.refs_2_.refs_10_), channel_id=1, source_target_pairs={{2,0},{4,2},{6,4},{1,3},{3,5},{5,7},{7,6},{0,1},{10,8},{12,10},{14... | collective-permute-start | bytes 786440 | tf_op jit(solution)/shard_map/ppermute | solution.py:226
  116.5 9.0 %collective-permute-start.26 = (bf16[16,64,128]{2,1,0:T(8,128)(2,1)S(1)}, bf16[16,64,128]{2,1,0:T(8,128)(2,1)S(1)}, u32[]{:S(2)}, u32[]{:S(2)}) collective-permute-start(bf16[16,64,128]{2,1,0:T(8,128)(2,1)S(1)} %collective-permute-done.22.refs_0_.refs_8_), channel_id=1, source_target_pairs={{0,2},{2,4},{4,6},{3,1},{5,3},{7,5},{6,7},{1,0},{8,10},{10,12},{12... | collective-permute-start | bytes 786440 | tf_op jit(solution)/shard_map/ppermute | solution.py:225
  118.7 10.4 %collective-permute-start.30 = (bf16[4,16,64,128]{3,2,1,0:T(8,128)(2,1)S(1)}, bf16[4,16,64,128]{3,2,1,0:T(8,128)(2,1)S(1)}, u32[]{:S(2)}, u32[]{:S(2)}) collective-permute-start(bf16[4,16,64,128]{3,2,1,0:T(8,128)(2,1)S(1)} %join.9), channel_id=1, source_target_pairs={{0,1},{1,0},{2,3},{3,2},{4,5},{5,4},{6,7},{7,6},{8,9},{9,8},{10,11... | collective-permute-start | bytes 3145736 | tf_op jit(solution)/shard_map/ppermute | solution.py:219
  122.1 6.9 %collective-permute-start.31 = (bf16[4,16,64,128]{3,2,1,0:T(8,128)(2,1)S(1)}, bf16[4,16,64,128]{3,2,1,0:T(8,128)(2,1)S(1)}, u32[]{:S(2)}, u32[]{:S(2)}) collective-permute-start(bf16[4,16,64,128]{3,2,1,0:T(8,128)(2,1)S(1)} %join.10), channel_id=1, source_target_pairs={{0,1},{1,0},{2,3},{3,2},{4,5},{5,4},{6,7},{7,6},{8,9},{9,8},{10,11... | collective-permute-start | bytes 3145736 | tf_op jit(solution)/shard_map/ppermute | solution.py:219
  125.5 3.5 %collective-permute-start.32 = (bf16[4,16,64,128]{3,2,1,0:T(8,128)(2,1)S(1)}, bf16[4,16,64,128]{3,2,1,0:T(8,128)(2,1)S(1)}, u32[]{:S(2)}, u32[]{:S(2)}) collective-permute-start(bf16[4,16,64,128]{3,2,1,0:T(8,128)(2,1)S(1)} %join.11), channel_id=1, source_target_pairs={{0,1},{1,0},{2,3},{3,2},{4,5},{5,4},{6,7},{7,6},{8,9},{9,8},{10,11... | collective-permute-start | bytes 3145736 | tf_op jit(solution)/shard_map/ppermute | solution.py:219
  149.1 9.7 %collective-permute-start.33 = (bf16[7,64,128]{2,1,0:T(8,128)(2,1)S(1)}, bf16[7,64,128]{2,1,0:T(8,128)(2,1)S(1)}, u32[]{:S(2)}, u32[]{:S(2)}) collective-permute-start(bf16[7,64,128]{2,1,0:T(8,128)(2,1)S(1)} %slice.29), channel_id=1, source_target_pairs={{0,128},{128,0},{1,129},{129,1},{2,130},{130,2},{3,131},{131,3},{4... | collective-permute-start | bytes 344072 | tf_op jit(solution)/shard_map/ppermute | solution.py:185
  (11 other events, 158.8 us)

commit v4 on v3

--- a/solution.py
+++ b/solution.py
@@ -52,7 +52,7 @@
         @pl.when(jnp.logical_and(z - shift >= 0, z - shift < chips))
         def _():
             for t in range(snaps):
-                other = joined[step - 1][snaps + t]
+                other = joined[step - 1][t if 2 * step >= chips else snaps + t]
                 place(t, 2 * (z - shift) + c, ahead[t][...])
                 place(t, 2 * (z - shift) + 1 - c, other)
 
@@ -110,20 +110,35 @@
     )(cols, *pieces, weights, gain, up, down)
 
 
-def join(values):
+def join(ahead, behind, step, chips):
+    snaps = len(ahead)
+    one_way = 2 * step >= chips
+
     def kernel(*refs):
-        for index, value in enumerate(refs[:-1]):
-            refs[-1][index] = value[...]
-
+        out = refs[-1]
+
+        def put(first, values):
+            for index, value in enumerate(values):
+                out[first + index] = value[...]
+
+        if one_way:
+            source = lax.axis_index("zl") - step * (1 - 2 * lax.axis_index("co"))
+            from_ahead = jnp.logical_and(source >= 0, source < chips)
+            pl.when(from_ahead)(lambda: put(0, refs[:snaps]))
+            pl.when(jnp.logical_not(from_ahead))(lambda: put(0, refs[snaps:-1]))
+        else:
+            put(0, refs[:-1])
+
+    count = snaps if one_way else 2 * snaps
     vmem = pl.BlockSpec(memory_space=pltpu.VMEM)
     return pl.pallas_call(
         kernel,
-        out_shape=jax.ShapeDtypeStruct((len(values),) + values[0].shape, values[0].dtype),
-        in_specs=[vmem] * len(values),
+        out_shape=jax.ShapeDtypeStruct((count,) + ahead[0].shape, ahead[0].dtype),
+        in_specs=[vmem] * (2 * snaps),
         out_specs=vmem,
         compiler_params=pltpu.CompilerParams(vmem_limit_bytes=1 << 20),
         name="join",
-    )(*values)
+    )(*ahead, *behind)
 
 
 def tie(value, other):
@@ -226,12 +241,12 @@
             behind[t] = lax.ppermute(behind[t], LINE, backward)
         moved += ahead + behind
         if step < chips - 1:
-            both = join(ahead + behind)
+            both = join(ahead, behind, step, chips)
             if beside is not None:
                 both, beside = tie(both, beside), None
             joined.append(swap(both))
         else:
-            last = [swap(join(ahead + behind))]
+            last = [swap(join(ahead, behind, step, chips))]
     return [mate, *chunks, *moved, *joined, *last]
 
 

time: 175 us -> 174 us (level)
  starting transfers between devices: 38.9 us -> 41.6 us
  blocking collectives: 64.1 us -> 61.5 us
    ppermute x12, waiting for transfers between devices: 0.28 us -> 30.7 us  [gather_line(): ahead[t] = lax.ppermute(ahead[t], LINE, forward)]
    ppermute x12, waiting for transfers between devices: 38.7 us -> 10.3 us  [gather_line(): behind[t] = lax.ppermute(behind[t], LINE, backward)]
    ppermute x12, starting transfers between devices: 13.7 us -> 25 us  [gather_line(): ahead[t] = lax.ppermute(ahead[t], LINE, forward)]
    ppermute x12, starting transfers between devices: 13.9 us -> 3.74 us  [gather_line(): behind[t] = lax.ppermute(behind[t], LINE, backward)]
    ppermute x2, starting transfers between devices: 9.13 us -> 11.6 us  [time_stage(): halo = lax.ppermute(own[-before:], 'zh', [(0, 1), (1, 0)])]
    ppermute x8, waiting for transfers between devices: 5.84 us -> 3.61 us  [gather_line(): swap = lambda v: lax.ppermute(v, 'co', [(0, 1), (1, 0)])]
    all_to_all x2, blocking collectives: 35 us -> 33.1 us  [on_device(): owned = lax.all_to_all(graph_out, OWNERS, 0, 0, tiled=True)]
  transfers between devices with their start and end apart: 34 -> 34, of which waited for: 18 -> 20; matrix products, arithmetic and copies ran while one was open for 2% -> 2% of each run, Pallas kernels for 4% -> 4%
where the time goes in v4:
time: 174 us
  blocking collectives  61.5 us (35%)
  waiting for transfers between devices  47 us (27%)
  starting transfers between devices  41.6 us (24%)
  Pallas kernels  16.9 us (10%)
  other arithmetic  4.3 us (2%)
  local copies, waits for them, and re-layouts  2 us (1%)
    all_to_all x2, blocking collectives, on_device(): owned = lax.all_to_all(graph_out, OWNERS, 0, 0, tiled=True)  33.1 us
    ppermute x12, waiting for transfers between devices, gather_line(): ahead[t] = lax.ppermute(ahead[t], LINE, forward)  30.7 us
    all_to_all x2, blocking collectives, on_device(): lax.all_to_all(finished.reshape(owners, snaps, part, width), OWNERS, 0, 0...  28.5 us
    ppermute x12, starting transfers between devices, gather_line(): ahead[t] = lax.ppermute(ahead[t], LINE, forward)  25 us
    ppermute x2, starting transfers between devices, time_stage(): halo = lax.ppermute(own[-before:], 'zh', [(0, 1), (1, 0)])  11.6 us
    ppermute x12, waiting for transfers between devices, gather_line(): behind[t] = lax.ppermute(behind[t], LINE, backward)  10.3 us
    pallas_call x2, Pallas kernels, graph_stage(): pl.pallas_call(functools.partial(graph_kernel, layer, chips, layer > 0),...  7.71 us
    pallas_call x2, Pallas kernels, time_stage(): pl.pallas_call(functools.partial(late_kernel, layer), out_shape=out_shape...  6.67 us
  transfers between devices with their start and end apart: 34, of which 20 were waited for; matrix products, arithmetic and copies ran while one was open for 2% of the time, Pallas kernels for 4%

profile of v4, /device:TPU:32, one launch (start us, length us, event | category | flops | bytes accessed | tf_op | source)
XLA Modules:
  0.0 173.6 jit_solution(7304047333059733095)
XLA Ops:
  1.1 2.0 %collective-permute-start.1 = (bf16[16,64,128]{2,1,0:T(8,128)(2,1)S(1)}, bf16[16,64,128]{2,1,0:T(8,128)(2,1)S(1)}, u32[]{:S(2)}, u32[]{:S(2)}) collective-permute-start(bf16[16,64,128]{2,1,0:T(8,128)(2,1)S(1)} %bitcast.36), channel_id=1, source_target_pairs={{0,2},{2,4},{4,6},{3,1},{5,3},{7,5},{6,7},{1,0},{8,10},{10,12},{12... | collective-permute-start | bytes 786440 | tf_op jit(solution)/shard_map/ppermute | solution.py:240
  5.2 4.3 %copy_bitcast_fusion.refs_1_.refs_19_ = bf16[2,8,128,1024]{3,2,1,0:T(8,128)(2,1)S(1)} fusion(s32[2,8,8,128,128]{4,3,2,1,0:T(8,128)} %param.12), kind=kLoop, calls=%fused_computation | loop fusion | flops 2097152 | bytes 12582912 | tf_op jit(solution)/shard_map/reshape | solution.py:274
  10.2 2.0 %collective-permute-start.5 = (bf16[16,64,128]{2,1,0:T(8,128)(2,1)S(1)}, bf16[16,64,128]{2,1,0:T(8,128)(2,1)S(1)}, u32[]{:S(2)}, u32[]{:S(2)}) collective-permute-start(bf16[16,64,128]{2,1,0:T(8,128)(2,1)S(1)} %collective-permute-done.1.refs_0_.refs_4_), channel_id=1, source_target_pairs={{0,2},{2,4},{4,6},{3,1},{5,3},{7,5},{6,7},{1,0},{8,10},{10,12},{12... | collective-permute-start | bytes 786440 | tf_op jit(solution)/shard_map/ppermute | solution.py:240
  12.2 3.3 %collective-permute-done.2.refs_1_.refs_5_ = bf16[16,64,128]{2,1,0:T(8,128)(2,1)S(1)} collective-permute-done((bf16[16,64,128]{2,1,0:T(8,128)(2,1)S(1)}, bf16[16,64,128]{2,1,0:T(8,128)(2,1)S(1)}, u32[]{:S(2)}, u32[]{:S(2)}) %collective-permute-start.2) | collective-permute-done | bytes 262176 | tf_op jit(solution)/shard_map/ppermute | solution.py:240
  18.3 2.0 %collective-permute-done.5.refs_0_.refs_8_ = bf16[16,64,128]{2,1,0:T(8,128)(2,1)S(1)} collective-permute-done((bf16[16,64,128]{2,1,0:T(8,128)(2,1)S(1)}, bf16[16,64,128]{2,1,0:T(8,128)(2,1)S(1)}, u32[]{:S(2)}, u32[]{:S(2)}) %collective-permute-start.5) | collective-permute-done | bytes 262176 | tf_op jit(solution)/shard_map/ppermute | solution.py:240
  20.2 2.3 %collective-permute-start.9 = (bf16[16,64,128]{2,1,0:T(8,128)(2,1)S(1)}, bf16[16,64,128]{2,1,0:T(8,128)(2,1)S(1)}, u32[]{:S(2)}, u32[]{:S(2)}) collective-permute-start(bf16[16,64,128]{2,1,0:T(8,128)(2,1)S(1)} %collective-permute-done.5.refs_0_.refs_8_), channel_id=1, source_target_pairs={{0,2},{2,4},{4,6},{3,1},{5,3},{7,5},{6,7},{1,0},{8,10},{10,12},{12... | collective-permute-start | bytes 786440 | tf_op jit(solution)/shard_map/ppermute | solution.py:240
  22.5 3.4 %collective-permute-done.6.refs_1_.refs_9_ = bf16[16,64,128]{2,1,0:T(8,128)(2,1)S(1)} collective-permute-done((bf16[16,64,128]{2,1,0:T(8,128)(2,1)S(1)}, bf16[16,64,128]{2,1,0:T(8,128)(2,1)S(1)}, u32[]{:S(2)}, u32[]{:S(2)}) %collective-permute-start.6) | collective-permute-done | bytes 262176 | tf_op jit(solution)/shard_map/ppermute | solution.py:240
  25.9 2.3 %collective-permute-start.10 = (bf16[16,64,128]{2,1,0:T(8,128)(2,1)S(1)}, bf16[16,64,128]{2,1,0:T(8,128)(2,1)S(1)}, u32[]{:S(2)}, u32[]{:S(2)}) collective-permute-start(bf16[16,64,128]{2,1,0:T(8,128)(2,1)S(1)} %collective-permute-done.6.refs_1_.refs_9_), channel_id=1, source_target_pairs={{0,2},{2,4},{4,6},{3,1},{5,3},{7,5},{6,7},{1,0},{8,10},{10,12},{12... | collective-permute-start | bytes 786440 | tf_op jit(solution)/shard_map/ppermute | solution.py:240
  28.1 2.8 %collective-permute-done.8.refs_3_.refs_11_ = bf16[16,64,128]{2,1,0:T(8,128)(2,1)S(1)} collective-permute-done((bf16[16,64,128]{2,1,0:T(8,128)(2,1)S(1)}, bf16[16,64,128]{2,1,0:T(8,128)(2,1)S(1)}, u32[]{:S(2)}, u32[]{:S(2)}) %collective-permute-start.8) | collective-permute-done | bytes 262176 | tf_op jit(solution)/shard_map/ppermute | solution.py:241
  32.4 4.7 %collective-permute-done.10.refs_1_.refs_13_ = bf16[16,64,128]{2,1,0:T(8,128)(2,1)S(1)} collective-permute-done((bf16[16,64,128]{2,1,0:T(8,128)(2,1)S(1)}, bf16[16,64,128]{2,1,0:T(8,128)(2,1)S(1)}, u32[]{:S(2)}, u32[]{:S(2)}) %collective-permute-start.10) | collective-permute-done | bytes 262176 | tf_op jit(solution)/shard_map/ppermute | solution.py:240
  39.8 3.9 %graph.2 = bf16[16,2,64,128]{3,2,1,0:T(8,128)(2,1)S(1)} custom-call(s32[2,8,8]{2,1,0:T(8,128)S(1)} %copy-done.5, bf16[2,16,64,128]{3,2,1,0:T(8,128)(2,1)S(1)} %collective-permute-done.refs_1_, bf16[16,64,128]{2,1,0:T(8,128)(2,1)S(1)} %bitcast.38, bf16[16,64,128]{2,1,0:T(8,128)(2,1)S(1)} %bitcast.35, ...), custom_call_target="tpu_custom_call" | custom-call | tf_op jit(solution)/shard_map/graph/pallas_call | solution.py:99
  43.7 18.4 %all_to_all.20 = bf16[16,2,64,128]{3,2,1,0:T(8,128)(2,1)S(1)} all-to-all(bf16[16,2,64,128]{3,2,1,0:T(8,128)(2,1)S(1)} %graph.2), channel_id=1, replica_groups=mesh['zh'=2,'x'=4,'y'=4,'zl'=4,'co'=2] {'x','y'}, dimensions={0} | all-to-all | bytes 1048576 | tf_op jit(solution)/shard_map/all_to_all | solution.py:283
  62.1 6.6 %collective-permute-start.16 = (bf16[7,64,128]{2,1,0:T(8,128)(2,1)S(1)}, bf16[7,64,128]{2,1,0:T(8,128)(2,1)S(1)}, u32[]{:S(2)}, u32[]{:S(2)}) collective-permute-start(bf16[7,64,128]{2,1,0:T(8,128)(2,1)S(1)} %slice.26), channel_id=1, source_target_pairs={{0,128},{128,0},{1,129},{129,1},{2,130},{130,2},{3,131},{131,3},{4... | collective-permute-start | bytes 344072 | tf_op jit(solution)/shard_map/ppermute | solution.py:200
  68.7 3.3 %late.2.later = bf16[32,64,128]{2,1,0:T(8,128)(2,1)S(1)} custom-call(bf16[32,64,128]{2,1,0:T(8,128)(2,1)S(1)} %bitcast.26, f32[2,8,128]{2,1,0:T(8,128)S(1)} %copy-done.4, f32[2,1,128]{2,1,0:T(1,128)S(1)} %bitcast.39, bf16[2,128,1024]{2,1,0:T(8,128)(2,1)S(1)} %copy-done, bf16[2,1024,128]{2,1,0:T(8,128)(2,1)S(1)} %copy-done.1), custom_call_target="tpu_custom_call" | custom-call | tf_op jit(solution)/shard_map/late/pallas_call | solution.py:204
  73.9 13.8 %all_to_all.21 = bf16[16,2,64,128]{3,2,1,0:T(8,128)(2,1)S(1)} all-to-all(bf16[16,2,64,128]{3,2,1,0:T(8,128)(2,1)S(1)} %bitcast.31), channel_id=1, replica_groups=mesh['zh'=2,'x'=4,'y'=4,'zl'=4,'co'=2] {'x','y'}, dimensions={0} | all-to-all | bytes 1048576 | tf_op jit(solution)/shard_map/all_to_all | solution.py:286
  87.7 2.7 %collective-permute-start.18 = (bf16[16,64,128]{2,1,0:T(8,128)(2,1)S(1)}, bf16[16,64,128]{2,1,0:T(8,128)(2,1)S(1)}, u32[]{:S(2)}, u32[]{:S(2)}) collective-permute-start(bf16[16,64,128]{2,1,0:T(8,128)(2,1)S(1)} %get-tuple-element.6.refs_2_), channel_id=1, source_target_pairs={{0,2},{2,4},{4,6},{3,1},{5,3},{7,5},{6,7},{1,0},{8,10},{10,12},{12... | collective-permute-start | bytes 786440 | tf_op jit(solution)/shard_map/ppermute | solution.py:240
  92.5 4.7 %collective-permute-done.18.refs_0_.refs_4_ = bf16[16,64,128]{2,1,0:T(8,128)(2,1)S(1)} collective-permute-done((bf16[16,64,128]{2,1,0:T(8,128)(2,1)S(1)}, bf16[16,64,128]{2,1,0:T(8,128)(2,1)S(1)}, u32[]{:S(2)}, u32[]{:S(2)}) %collective-permute-start.18) | collective-permute-done | bytes 262176 | tf_op jit(solution)/shard_map/ppermute | solution.py:240
  97.2 2.5 %collective-permute-start.22 = (bf16[16,64,128]{2,1,0:T(8,128)(2,1)S(1)}, bf16[16,64,128]{2,1,0:T(8,128)(2,1)S(1)}, u32[]{:S(2)}, u32[]{:S(2)}) collective-permute-start(bf16[16,64,128]{2,1,0:T(8,128)(2,1)S(1)} %collective-permute-done.18.refs_0_.refs_4_), channel_id=1, source_target_pairs={{0,2},{2,4},{4,6},{3,1},{5,3},{7,5},{6,7},{1,0},{8,10},{10,12},{12... | collective-permute-start | bytes 786440 | tf_op jit(solution)/shard_map/ppermute | solution.py:240
  99.7 3.1 %collective-permute-done.19.refs_1_.refs_5_ = bf16[16,64,128]{2,1,0:T(8,128)(2,1)S(1)} collective-permute-done((bf16[16,64,128]{2,1,0:T(8,128)(2,1)S(1)}, bf16[16,64,128]{2,1,0:T(8,128)(2,1)S(1)}, u32[]{:S(2)}, u32[]{:S(2)}) %collective-permute-start.19) | collective-permute-done | bytes 262176 | tf_op jit(solution)/shard_map/ppermute | solution.py:240
  102.8 2.5 %collective-permute-start.23 = (bf16[16,64,128]{2,1,0:T(8,128)(2,1)S(1)}, bf16[16,64,128]{2,1,0:T(8,128)(2,1)S(1)}, u32[]{:S(2)}, u32[]{:S(2)}) collective-permute-start(bf16[16,64,128]{2,1,0:T(8,128)(2,1)S(1)} %collective-permute-done.19.refs_1_.refs_5_), channel_id=1, source_target_pairs={{0,2},{2,4},{4,6},{3,1},{5,3},{7,5},{6,7},{1,0},{8,10},{10,12},{12... | collective-permute-start | bytes 786440 | tf_op jit(solution)/shard_map/ppermute | solution.py:240
  105.6 2.8 %collective-permute-done.22.refs_0_.refs_8_ = bf16[16,64,128]{2,1,0:T(8,128)(2,1)S(1)} collective-permute-done((bf16[16,64,128]{2,1,0:T(8,128)(2,1)S(1)}, bf16[16,64,128]{2,1,0:T(8,128)(2,1)S(1)}, u32[]{:S(2)}, u32[]{:S(2)}) %collective-permute-start.22) | collective-permute-done | bytes 262176 | tf_op jit(solution)/shard_map/ppermute | solution.py:240
  108.4 2.5 %collective-permute-start.26 = (bf16[16,64,128]{2,1,0:T(8,128)(2,1)S(1)}, bf16[16,64,128]{2,1,0:T(8,128)(2,1)S(1)}, u32[]{:S(2)}, u32[]{:S(2)}) collective-permute-start(bf16[16,64,128]{2,1,0:T(8,128)(2,1)S(1)} %collective-permute-done.22.refs_0_.refs_8_), channel_id=1, source_target_pairs={{0,2},{2,4},{4,6},{3,1},{5,3},{7,5},{6,7},{1,0},{8,10},{10,12},{12... | collective-permute-start | bytes 786440 | tf_op jit(solution)/shard_map/ppermute | solution.py:240
  110.9 2.2 %collective-permute-done.23.refs_1_.refs_9_ = bf16[16,64,128]{2,1,0:T(8,128)(2,1)S(1)} collective-permute-done((bf16[16,64,128]{2,1,0:T(8,128)(2,1)S(1)}, bf16[16,64,128]{2,1,0:T(8,128)(2,1)S(1)}, u32[]{:S(2)}, u32[]{:S(2)}) %collective-permute-start.23) | collective-permute-done | bytes 262176 | tf_op jit(solution)/shard_map/ppermute | solution.py:240
  113.1 2.5 %collective-permute-start.27 = (bf16[16,64,128]{2,1,0:T(8,128)(2,1)S(1)}, bf16[16,64,128]{2,1,0:T(8,128)(2,1)S(1)}, u32[]{:S(2)}, u32[]{:S(2)}) collective-permute-start(bf16[16,64,128]{2,1,0:T(8,128)(2,1)S(1)} %collective-permute-done.23.refs_1_.refs_9_), channel_id=1, source_target_pairs={{0,2},{2,4},{4,6},{3,1},{5,3},{7,5},{6,7},{1,0},{8,10},{10,12},{12... | collective-permute-start | bytes 786440 | tf_op jit(solution)/shard_map/ppermute | solution.py:240
  115.6 4.4 %collective-permute-done.25.refs_3_.refs_11_ = bf16[16,64,128]{2,1,0:T(8,128)(2,1)S(1)} collective-permute-done((bf16[16,64,128]{2,1,0:T(8,128)(2,1)S(1)}, bf16[16,64,128]{2,1,0:T(8,128)(2,1)S(1)}, u32[]{:S(2)}, u32[]{:S(2)}) %collective-permute-start.25) | collective-permute-done | bytes 262176 | tf_op jit(solution)/shard_map/ppermute | solution.py:241
  120.1 3.8 %collective-permute-done.27.refs_1_.refs_13_ = bf16[16,64,128]{2,1,0:T(8,128)(2,1)S(1)} collective-permute-done((bf16[16,64,128]{2,1,0:T(8,128)(2,1)S(1)}, bf16[16,64,128]{2,1,0:T(8,128)(2,1)S(1)}, u32[]{:S(2)}, u32[]{:S(2)}) %collective-permute-start.27) | collective-permute-done | bytes 262176 | tf_op jit(solution)/shard_map/ppermute | solution.py:240
  123.9 2.4 %collective-permute-done.29.refs_3_.refs_15_ = bf16[16,64,128]{2,1,0:T(8,128)(2,1)S(1)} collective-permute-done((bf16[16,64,128]{2,1,0:T(8,128)(2,1)S(1)}, bf16[16,64,128]{2,1,0:T(8,128)(2,1)S(1)}, u32[]{:S(2)}, u32[]{:S(2)}) %collective-permute-start.29) | collective-permute-done | bytes 262176 | tf_op jit(solution)/shard_map/ppermute | solution.py:241
  128.4 3.8 %graph.3 = bf16[16,2,64,128]{3,2,1,0:T(8,128)(2,1)S(1)} custom-call(s32[2,8,8]{2,1,0:T(8,128)S(1)} %copy-done.5, bf16[16,2,64,128]{3,2,1,0:T(8,128)(2,1)S(1)} %collective-permute-done.17.refs_1_, bf16[16,64,128]{2,1,0:T(8,128)(2,1)S(1)} %get-tuple-element.6.refs_2_, bf16[16,64,128]{2,1,0:T(8,128)(2,1)S(1)} %get-tuple-element.5.refs_3_, ...), custom_call_target="tpu_custom_call" | custom-call | tf_op jit(solution)/shard_map/graph/pallas_call | solution.py:99
  132.3 14.7 %all_to_all.22 = bf16[16,2,64,128]{3,2,1,0:T(8,128)(2,1)S(1)} all-to-all(bf16[16,2,64,128]{3,2,1,0:T(8,128)(2,1)S(1)} %graph.3), channel_id=1, replica_groups=mesh['zh'=2,'x'=4,'y'=4,'zl'=4,'co'=2] {'x','y'}, dimensions={0} | all-to-all | bytes 1048576 | tf_op jit(solution)/shard_map/all_to_all | solution.py:283
  147.0 5.0 %collective-permute-start.33 = (bf16[7,64,128]{2,1,0:T(8,128)(2,1)S(1)}, bf16[7,64,128]{2,1,0:T(8,128)(2,1)S(1)}, u32[]{:S(2)}, u32[]{:S(2)}) collective-permute-start(bf16[7,64,128]{2,1,0:T(8,128)(2,1)S(1)} %slice.29), channel_id=1, source_target_pairs={{0,128},{128,0},{1,129},{129,1},{2,130},{130,2},{3,131},{131,3},{4... | collective-permute-start | bytes 344072 | tf_op jit(solution)/shard_map/ppermute | solution.py:200
  152.0 3.3 %late.3.later = bf16[32,64,128]{2,1,0:T(8,128)(2,1)S(1)} custom-call(bf16[32,64,128]{2,1,0:T(8,128)(2,1)S(1)} %bitcast.29, f32[2,8,128]{2,1,0:T(8,128)S(1)} %copy-done.4, f32[2,1,128]{2,1,0:T(1,128)S(1)} %bitcast.41, bf16[2,128,1024]{2,1,0:T(8,128)(2,1)S(1)} %copy-done, bf16[2,1024,128]{2,1,0:T(8,128)(2,1)S(1)} %copy-done.1), custom_call_target="tpu_custom_call" | custom-call | tf_op jit(solution)/shard_map/late/pallas_call | solution.py:204
  158.1 14.7 %all_to_all.23 = bf16[16,2,64,128]{3,2,1,0:T(8,128)(2,1)S(1)} all-to-all(bf16[16,2,64,128]{3,2,1,0:T(8,128)(2,1)S(1)} %bitcast.32), channel_id=1, replica_groups=mesh['zh'=2,'x'=4,'y'=4,'zl'=4,'co'=2] {'x','y'}, dimensions={0} | all-to-all | bytes 1048576 | tf_op jit(solution)/shard_map/all_to_all | solution.py:286
  (77 shorter events, 20.6 us)
Async XLA Ops:
  1.1 9.2 %collective-permute-start.1 = (bf16[16,64,128]{2,1,0:T(8,128)(2,1)S(1)}, bf16[16,64,128]{2,1,0:T(8,128)(2,1)S(1)}, u32[]{:S(2)}, u32[]{:S(2)}) collective-permute-start(bf16[16,64,128]{2,1,0:T(8,128)(2,1)S(1)} %bitcast.36), channel_id=1, source_target_pairs={{0,2},{2,4},{4,6},{3,1},{5,3},{7,5},{6,7},{1,0},{8,10},{10,12},{12... | collective-permute-start | bytes 786440 | tf_op jit(solution)/shard_map/ppermute | solution.py:240
  3.1 13.8 %collective-permute-start.3 = (bf16[16,64,128]{2,1,0:T(8,128)(2,1)S(1)}, bf16[16,64,128]{2,1,0:T(8,128)(2,1)S(1)}, u32[]{:S(2)}, u32[]{:S(2)}) collective-permute-start(bf16[16,64,128]{2,1,0:T(8,128)(2,1)S(1)} %bitcast.37), channel_id=1, source_target_pairs={{2,0},{4,2},{6,4},{1,3},{3,5},{5,7},{7,6},{0,1},{10,8},{12,10},{14... | collective-permute-start | bytes 786440 | tf_op jit(solution)/shard_map/ppermute | solution.py:241
  3.2 12.4 %collective-permute-start.2 = (bf16[16,64,128]{2,1,0:T(8,128)(2,1)S(1)}, bf16[16,64,128]{2,1,0:T(8,128)(2,1)S(1)}, u32[]{:S(2)}, u32[]{:S(2)}) collective-permute-start(bf16[16,64,128]{2,1,0:T(8,128)(2,1)S(1)} %bitcast.33), channel_id=1, source_target_pairs={{0,2},{2,4},{4,6},{3,1},{5,3},{7,5},{6,7},{1,0},{8,10},{10,12},{12... | collective-permute-start | bytes 786440 | tf_op jit(solution)/shard_map/ppermute | solution.py:240
  5.1 12.8 %collective-permute-start.4 = (bf16[16,64,128]{2,1,0:T(8,128)(2,1)S(1)}, bf16[16,64,128]{2,1,0:T(8,128)(2,1)S(1)}, u32[]{:S(2)}, u32[]{:S(2)}) collective-permute-start(bf16[16,64,128]{2,1,0:T(8,128)(2,1)S(1)} %bitcast.34), channel_id=1, source_target_pairs={{2,0},{4,2},{6,4},{1,3},{3,5},{5,7},{7,6},{0,1},{10,8},{12,10},{14... | collective-permute-start | bytes 786440 | tf_op jit(solution)/shard_map/ppermute | solution.py:241
  10.2 10.0 %collective-permute-start.5 = (bf16[16,64,128]{2,1,0:T(8,128)(2,1)S(1)}, bf16[16,64,128]{2,1,0:T(8,128)(2,1)S(1)}, u32[]{:S(2)}, u32[]{:S(2)}) collective-permute-start(bf16[16,64,128]{2,1,0:T(8,128)(2,1)S(1)} %collective-permute-done.1.refs_0_.refs_4_), channel_id=1, source_target_pairs={{0,2},{2,4},{4,6},{3,1},{5,3},{7,5},{6,7},{1,0},{8,10},{10,12},{12... | collective-permute-start | bytes 786440 | tf_op jit(solution)/shard_map/ppermute | solution.py:240
  15.6 10.3 %collective-permute-start.6 = (bf16[16,64,128]{2,1,0:T(8,128)(2,1)S(1)}, bf16[16,64,128]{2,1,0:T(8,128)(2,1)S(1)}, u32[]{:S(2)}, u32[]{:S(2)}) collective-permute-start(bf16[16,64,128]{2,1,0:T(8,128)(2,1)S(1)} %collective-permute-done.2.refs_1_.refs_5_), channel_id=1, source_target_pairs={{0,2},{2,4},{4,6},{3,1},{5,3},{7,5},{6,7},{1,0},{8,10},{10,12},{12... | collective-permute-start | bytes 786440 | tf_op jit(solution)/shard_map/ppermute | solution.py:240
  16.9 11.2 %collective-permute-start.7 = (bf16[16,64,128]{2,1,0:T(8,128)(2,1)S(1)}, bf16[16,64,128]{2,1,0:T(8,128)(2,1)S(1)}, u32[]{:S(2)}, u32[]{:S(2)}) collective-permute-start(bf16[16,64,128]{2,1,0:T(8,128)(2,1)S(1)} %collective-permute-done.3.refs_2_.refs_6_), channel_id=1, source_target_pairs={{2,0},{4,2},{6,4},{1,3},{3,5},{5,7},{7,6},{0,1},{10,8},{12,10},{14... | collective-permute-start | bytes 786440 | tf_op jit(solution)/shard_map/ppermute | solution.py:241
  17.9 13.0 %collective-permute-start.8 = (bf16[16,64,128]{2,1,0:T(8,128)(2,1)S(1)}, bf16[16,64,128]{2,1,0:T(8,128)(2,1)S(1)}, u32[]{:S(2)}, u32[]{:S(2)}) collective-permute-start(bf16[16,64,128]{2,1,0:T(8,128)(2,1)S(1)} %collective-permute-done.4.refs_3_.refs_7_), channel_id=1, source_target_pairs={{2,0},{4,2},{6,4},{1,3},{3,5},{5,7},{7,6},{0,1},{10,8},{12,10},{14... | collective-permute-start | bytes 786440 | tf_op jit(solution)/shard_map/ppermute | solution.py:241
  18.2 20.8 %collective-permute-start.13 = (bf16[4,16,64,128]{3,2,1,0:T(8,128)(2,1)S(1)}, bf16[4,16,64,128]{3,2,1,0:T(8,128)(2,1)S(1)}, u32[]{:S(2)}, u32[]{:S(2)}) collective-permute-start(bf16[4,16,64,128]{3,2,1,0:T(8,128)(2,1)S(1)} %tie.1), channel_id=1, source_target_pairs={{0,1},{1,0},{2,3},{3,2},{4,5},{5,4},{6,7},{7,6},{8,9},{9,8},{10,11... | collective-permute-start | bytes 3145736 | tf_op jit(solution)/shard_map/ppermute | solution.py:234
  20.2 11.8 %collective-permute-start.9 = (bf16[16,64,128]{2,1,0:T(8,128)(2,1)S(1)}, bf16[16,64,128]{2,1,0:T(8,128)(2,1)S(1)}, u32[]{:S(2)}, u32[]{:S(2)}) collective-permute-start(bf16[16,64,128]{2,1,0:T(8,128)(2,1)S(1)} %collective-permute-done.5.refs_0_.refs_8_), channel_id=1, source_target_pairs={{0,2},{2,4},{4,6},{3,1},{5,3},{7,5},{6,7},{1,0},{8,10},{10,12},{12... | collective-permute-start | bytes 786440 | tf_op jit(solution)/shard_map/ppermute | solution.py:240
  25.9 11.2 %collective-permute-start.10 = (bf16[16,64,128]{2,1,0:T(8,128)(2,1)S(1)}, bf16[16,64,128]{2,1,0:T(8,128)(2,1)S(1)}, u32[]{:S(2)}, u32[]{:S(2)}) collective-permute-start(bf16[16,64,128]{2,1,0:T(8,128)(2,1)S(1)} %collective-permute-done.6.refs_1_.refs_9_), channel_id=1, source_target_pairs={{0,2},{2,4},{4,6},{3,1},{5,3},{7,5},{6,7},{1,0},{8,10},{10,12},{12... | collective-permute-start | bytes 786440 | tf_op jit(solution)/shard_map/ppermute | solution.py:240
  28.1 9.0 %collective-permute-start.11 = (bf16[16,64,128]{2,1,0:T(8,128)(2,1)S(1)}, bf16[16,64,128]{2,1,0:T(8,128)(2,1)S(1)}, u32[]{:S(2)}, u32[]{:S(2)}) collective-permute-start(bf16[16,64,128]{2,1,0:T(8,128)(2,1)S(1)} %collective-permute-done.7.refs_2_.refs_10_), channel_id=1, source_target_pairs={{2,0},{4,2},{6,4},{1,3},{3,5},{5,7},{7,6},{0,1},{10,8},{12,10},{14... | collective-permute-start | bytes 786440 | tf_op jit(solution)/shard_map/ppermute | solution.py:241
  30.9 6.6 %collective-permute-start.12 = (bf16[16,64,128]{2,1,0:T(8,128)(2,1)S(1)}, bf16[16,64,128]{2,1,0:T(8,128)(2,1)S(1)}, u32[]{:S(2)}, u32[]{:S(2)}) collective-permute-start(bf16[16,64,128]{2,1,0:T(8,128)(2,1)S(1)} %collective-permute-done.8.refs_3_.refs_11_), channel_id=1, source_target_pairs={{2,0},{4,2},{6,4},{1,3},{3,5},{5,7},{7,6},{0,1},{10,8},{12,10},{14... | collective-permute-start | bytes 786440 | tf_op jit(solution)/shard_map/ppermute | solution.py:241
  32.1 5.9 %collective-permute-start = (bf16[2,16,64,128]{3,2,1,0:T(8,128)(2,1)S(1)}, bf16[2,16,64,128]{3,2,1,0:T(8,128)(2,1)S(1)}, u32[]{:S(2)}, u32[]{:S(2)}) collective-permute-start(bf16[2,16,64,128]{3,2,1,0:T(8,128)(2,1)S(1)} %bitcast.46), channel_id=1, source_target_pairs={{0,1},{1,0},{2,3},{3,2},{4,5},{5,4},{6,7},{7,6},{8,9},{9,8},{10,11... | collective-permute-start | bytes 1572872 | tf_op jit(solution)/shard_map/ppermute | solution.py:234
  37.5 2.3 %collective-permute-start.15 = (bf16[2,16,64,128]{3,2,1,0:T(8,128)(2,1)S(1)}, bf16[2,16,64,128]{3,2,1,0:T(8,128)(2,1)S(1)}, u32[]{:S(2)}, u32[]{:S(2)}) collective-permute-start(bf16[2,16,64,128]{3,2,1,0:T(8,128)(2,1)S(1)} %join.8), channel_id=1, source_target_pairs={{0,1},{1,0},{2,3},{3,2},{4,5},{5,4},{6,7},{7,6},{8,9},{9,8},{10,11... | collective-permute-start | bytes 1572872 | tf_op jit(solution)/shard_map/ppermute | solution.py:234
  62.1 10.7 %collective-permute-start.16 = (bf16[7,64,128]{2,1,0:T(8,128)(2,1)S(1)}, bf16[7,64,128]{2,1,0:T(8,128)(2,1)S(1)}, u32[]{:S(2)}, u32[]{:S(2)}) collective-permute-start(bf16[7,64,128]{2,1,0:T(8,128)(2,1)S(1)} %slice.26), channel_id=1, source_target_pairs={{0,128},{128,0},{1,129},{129,1},{2,130},{130,2},{3,131},{131,3},{4... | collective-permute-start | bytes 344072 | tf_op jit(solution)/shard_map/ppermute | solution.py:200
  87.7 9.4 %collective-permute-start.18 = (bf16[16,64,128]{2,1,0:T(8,128)(2,1)S(1)}, bf16[16,64,128]{2,1,0:T(8,128)(2,1)S(1)}, u32[]{:S(2)}, u32[]{:S(2)}) collective-permute-start(bf16[16,64,128]{2,1,0:T(8,128)(2,1)S(1)} %get-tuple-element.6.refs_2_), channel_id=1, source_target_pairs={{0,2},{2,4},{4,6},{3,1},{5,3},{7,5},{6,7},{1,0},{8,10},{10,12},{12... | collective-permute-start | bytes 786440 | tf_op jit(solution)/shard_map/ppermute | solution.py:240
  90.4 12.4 %collective-permute-start.19 = (bf16[16,64,128]{2,1,0:T(8,128)(2,1)S(1)}, bf16[16,64,128]{2,1,0:T(8,128)(2,1)S(1)}, u32[]{:S(2)}, u32[]{:S(2)}) collective-permute-start(bf16[16,64,128]{2,1,0:T(8,128)(2,1)S(1)} %get-tuple-element.5.refs_3_), channel_id=1, source_target_pairs={{0,2},{2,4},{4,6},{3,1},{5,3},{7,5},{6,7},{1,0},{8,10},{10,12},{12... | collective-permute-start | bytes 786440 | tf_op jit(solution)/shard_map/ppermute | solution.py:240
  91.1 14.2 %collective-permute-start.20 = (bf16[16,64,128]{2,1,0:T(8,128)(2,1)S(1)}, bf16[16,64,128]{2,1,0:T(8,128)(2,1)S(1)}, u32[]{:S(2)}, u32[]{:S(2)}) collective-permute-start(bf16[16,64,128]{2,1,0:T(8,128)(2,1)S(1)} %get-tuple-element.6.refs_2_), channel_id=1, source_target_pairs={{2,0},{4,2},{6,4},{1,3},{3,5},{5,7},{7,6},{0,1},{10,8},{12,10},{14... | collective-permute-start | bytes 786440 | tf_op jit(solution)/shard_map/ppermute | solution.py:241
  92.4 12.8 %collective-permute-start.21 = (bf16[16,64,128]{2,1,0:T(8,128)(2,1)S(1)}, bf16[16,64,128]{2,1,0:T(8,128)(2,1)S(1)}, u32[]{:S(2)}, u32[]{:S(2)}) collective-permute-start(bf16[16,64,128]{2,1,0:T(8,128)(2,1)S(1)} %get-tuple-element.5.refs_3_), channel_id=1, source_target_pairs={{2,0},{4,2},{6,4},{1,3},{3,5},{5,7},{7,6},{0,1},{10,8},{12,10},{14... | collective-permute-start | bytes 786440 | tf_op jit(solution)/shard_map/ppermute | solution.py:241
  97.2 11.2 %collective-permute-start.22 = (bf16[16,64,128]{2,1,0:T(8,128)(2,1)S(1)}, bf16[16,64,128]{2,1,0:T(8,128)(2,1)S(1)}, u32[]{:S(2)}, u32[]{:S(2)}) collective-permute-start(bf16[16,64,128]{2,1,0:T(8,128)(2,1)S(1)} %collective-permute-done.18.refs_0_.refs_4_), channel_id=1, source_target_pairs={{0,2},{2,4},{4,6},{3,1},{5,3},{7,5},{6,7},{1,0},{8,10},{10,12},{12... | collective-permute-start | bytes 786440 | tf_op jit(solution)/shard_map/ppermute | solution.py:240
  102.8 10.3 %collective-permute-start.23 = (bf16[16,64,128]{2,1,0:T(8,128)(2,1)S(1)}, bf16[16,64,128]{2,1,0:T(8,128)(2,1)S(1)}, u32[]{:S(2)}, u32[]{:S(2)}) collective-permute-start(bf16[16,64,128]{2,1,0:T(8,128)(2,1)S(1)} %collective-permute-done.19.refs_1_.refs_5_), channel_id=1, source_target_pairs={{0,2},{2,4},{4,6},{3,1},{5,3},{7,5},{6,7},{1,0},{8,10},{10,12},{12... | collective-permute-start | bytes 786440 | tf_op jit(solution)/shard_map/ppermute | solution.py:240
  105.3 10.3 %collective-permute-start.24 = (bf16[16,64,128]{2,1,0:T(8,128)(2,1)S(1)}, bf16[16,64,128]{2,1,0:T(8,128)(2,1)S(1)}, u32[]{:S(2)}, u32[]{:S(2)}) collective-permute-start(bf16[16,64,128]{2,1,0:T(8,128)(2,1)S(1)} %collective-permute-done.20.refs_2_.refs_6_), channel_id=1, source_target_pairs={{2,0},{4,2},{6,4},{1,3},{3,5},{5,7},{7,6},{0,1},{10,8},{12,10},{14... | collective-permute-start | bytes 786440 | tf_op jit(solution)/shard_map/ppermute | solution.py:241
  105.3 14.7 %collective-permute-start.25 = (bf16[16,64,128]{2,1,0:T(8,128)(2,1)S(1)}, bf16[16,64,128]{2,1,0:T(8,128)(2,1)S(1)}, u32[]{:S(2)}, u32[]{:S(2)}) collective-permute-start(bf16[16,64,128]{2,1,0:T(8,128)(2,1)S(1)} %collective-permute-done.21.refs_3_.refs_7_), channel_id=1, source_target_pairs={{2,0},{4,2},{6,4},{1,3},{3,5},{5,7},{7,6},{0,1},{10,8},{12,10},{14... | collective-permute-start | bytes 786440 | tf_op jit(solution)/shard_map/ppermute | solution.py:241
  105.5 21.1 %collective-permute-start.30 = (bf16[4,16,64,128]{3,2,1,0:T(8,128)(2,1)S(1)}, bf16[4,16,64,128]{3,2,1,0:T(8,128)(2,1)S(1)}, u32[]{:S(2)}, u32[]{:S(2)}) collective-permute-start(bf16[4,16,64,128]{3,2,1,0:T(8,128)(2,1)S(1)} %join.9), channel_id=1, source_target_pairs={{0,1},{1,0},{2,3},{3,2},{4,5},{5,4},{6,7},{7,6},{8,9},{9,8},{10,11... | collective-permute-start | bytes 3145736 | tf_op jit(solution)/shard_map/ppermute | solution.py:234
  108.4 11.6 %collective-permute-start.26 = (bf16[16,64,128]{2,1,0:T(8,128)(2,1)S(1)}, bf16[16,64,128]{2,1,0:T(8,128)(2,1)S(1)}, u32[]{:S(2)}, u32[]{:S(2)}) collective-permute-start(bf16[16,64,128]{2,1,0:T(8,128)(2,1)S(1)} %collective-permute-done.22.refs_0_.refs_8_), channel_id=1, source_target_pairs={{0,2},{2,4},{4,6},{3,1},{5,3},{7,5},{6,7},{1,0},{8,10},{10,12},{12... | collective-permute-start | bytes 786440 | tf_op jit(solution)/shard_map/ppermute | solution.py:240
  113.1 10.8 %collective-permute-start.27 = (bf16[16,64,128]{2,1,0:T(8,128)(2,1)S(1)}, bf16[16,64,128]{2,1,0:T(8,128)(2,1)S(1)}, u32[]{:S(2)}, u32[]{:S(2)}) collective-permute-start(bf16[16,64,128]{2,1,0:T(8,128)(2,1)S(1)} %collective-permute-done.23.refs_1_.refs_9_), channel_id=1, source_target_pairs={{0,2},{2,4},{4,6},{3,1},{5,3},{7,5},{6,7},{1,0},{8,10},{10,12},{12... | collective-permute-start | bytes 786440 | tf_op jit(solution)/shard_map/ppermute | solution.py:240
  115.6 8.4 %collective-permute-start.28 = (bf16[16,64,128]{2,1,0:T(8,128)(2,1)S(1)}, bf16[16,64,128]{2,1,0:T(8,128)(2,1)S(1)}, u32[]{:S(2)}, u32[]{:S(2)}) collective-permute-start(bf16[16,64,128]{2,1,0:T(8,128)(2,1)S(1)} %collective-permute-done.24.refs_2_.refs_10_), channel_id=1, source_target_pairs={{2,0},{4,2},{6,4},{1,3},{3,5},{5,7},{7,6},{0,1},{10,8},{12,10},{14... | collective-permute-start | bytes 786440 | tf_op jit(solution)/shard_map/ppermute | solution.py:241
  120.0 6.4 %collective-permute-start.29 = (bf16[16,64,128]{2,1,0:T(8,128)(2,1)S(1)}, bf16[16,64,128]{2,1,0:T(8,128)(2,1)S(1)}, u32[]{:S(2)}, u32[]{:S(2)}) collective-permute-start(bf16[16,64,128]{2,1,0:T(8,128)(2,1)S(1)} %collective-permute-done.25.refs_3_.refs_11_), channel_id=1, source_target_pairs={{2,0},{4,2},{6,4},{1,3},{3,5},{5,7},{7,6},{0,1},{10,8},{12,10},{14... | collective-permute-start | bytes 786440 | tf_op jit(solution)/shard_map/ppermute | solution.py:241
  120.0 6.5 %collective-permute-start.17 = (bf16[16,2,64,128]{3,2,1,0:T(8,128)(2,1)S(1)}, bf16[16,2,64,128]{3,2,1,0:T(8,128)(2,1)S(1)}, u32[]{:S(2)}, u32[]{:S(2)}) collective-permute-start(bf16[16,2,64,128]{3,2,1,0:T(8,128)(2,1)S(1)} %all_to_all.21), channel_id=1, source_target_pairs={{0,1},{1,0},{2,3},{3,2},{4,5},{5,4},{6,7},{7,6},{8,9},{9,8},{10,11... | collective-permute-start | bytes 1572872 | tf_op jit(solution)/shard_map/ppermute | solution.py:234
  123.9 2.6 %collective-permute-start.31 = (bf16[2,16,64,128]{3,2,1,0:T(8,128)(2,1)S(1)}, bf16[2,16,64,128]{3,2,1,0:T(8,128)(2,1)S(1)}, u32[]{:S(2)}, u32[]{:S(2)}) collective-permute-start(bf16[2,16,64,128]{3,2,1,0:T(8,128)(2,1)S(1)} %join.10), channel_id=1, source_target_pairs={{0,1},{1,0},{2,3},{3,2},{4,5},{5,4},{6,7},{7,6},{8,9},{9,8},{10,11... | collective-permute-start | bytes 1572872 | tf_op jit(solution)/shard_map/ppermute | solution.py:234
  147.0 10.0 %collective-permute-start.33 = (bf16[7,64,128]{2,1,0:T(8,128)(2,1)S(1)}, bf16[7,64,128]{2,1,0:T(8,128)(2,1)S(1)}, u32[]{:S(2)}, u32[]{:S(2)}) collective-permute-start(bf16[7,64,128]{2,1,0:T(8,128)(2,1)S(1)} %slice.29), channel_id=1, source_target_pairs={{0,128},{128,0},{1,129},{129,1},{2,130},{130,2},{3,131},{131,3},{4... | collective-permute-start | bytes 344072 | tf_op jit(solution)/shard_map/ppermute | solution.py:200
  (11 other events, 220.0 us)

commit v5 on v4

--- a/solution.py
+++ b/solution.py
@@ -110,7 +110,7 @@
     )(cols, *pieces, weights, gain, up, down)
 
 
-def join(ahead, behind, step, chips):
+def join(ahead, behind, step, chips, after):
     snaps = len(ahead)
     one_way = 2 * step >= chips
 
@@ -125,20 +125,20 @@
             source = lax.axis_index("zl") - step * (1 - 2 * lax.axis_index("co"))
             from_ahead = jnp.logical_and(source >= 0, source < chips)
             pl.when(from_ahead)(lambda: put(0, refs[:snaps]))
-            pl.when(jnp.logical_not(from_ahead))(lambda: put(0, refs[snaps:-1]))
+            pl.when(jnp.logical_not(from_ahead))(lambda: put(0, refs[snaps : 2 * snaps]))
         else:
-            put(0, refs[:-1])
+            put(0, refs[: 2 * snaps])
 
     count = snaps if one_way else 2 * snaps
     vmem = pl.BlockSpec(memory_space=pltpu.VMEM)
     return pl.pallas_call(
         kernel,
         out_shape=jax.ShapeDtypeStruct((count,) + ahead[0].shape, ahead[0].dtype),
-        in_specs=[vmem] * (2 * snaps),
+        in_specs=[vmem] * (2 * snaps) + [pl.BlockSpec(memory_space=pl.ANY)],
         out_specs=vmem,
         compiler_params=pltpu.CompilerParams(vmem_limit_bytes=1 << 20),
         name="join",
-    )(*ahead, *behind)
+    )(*ahead, *behind, after)
 
 
 def tie(value, other):
@@ -241,12 +241,12 @@
             behind[t] = lax.ppermute(behind[t], LINE, backward)
         moved += ahead + behind
         if step < chips - 1:
-            both = join(ahead, behind, step, chips)
+            both = join(ahead, behind, step, chips, mate)
             if beside is not None:
                 both, beside = tie(both, beside), None
             joined.append(swap(both))
         else:
-            last = [swap(join(ahead, behind, step, chips))]
+            last = [swap(join(ahead, behind, step, chips, mate))]
     return [mate, *chunks, *moved, *joined, *last]
 
 

time: 174 us -> 173 us (level)
  blocking collectives: 61.5 us -> 64.2 us
  starting transfers between devices: 41.6 us -> 38.9 us
    ppermute x12, starting transfers between devices: 25 us -> 19.7 us  [gather_line(): ahead[t] = lax.ppermute(ahead[t], LINE, forward)]
    ppermute x12, waiting for transfers between devices: 30.7 us -> 34.4 us  [gather_line(): ahead[t] = lax.ppermute(ahead[t], LINE, forward)]
    ppermute x12, starting transfers between devices: 3.74 us -> 7.23 us  [gather_line(): behind[t] = lax.ppermute(behind[t], LINE, backward)]
    ppermute x12, waiting for transfers between devices: 10.3 us -> 7.66 us  [gather_line(): behind[t] = lax.ppermute(behind[t], LINE, backward)]
    ppermute x2, waiting for transfers between devices: 2.36 us -> 0.31 us  [time_stage(): halo = lax.ppermute(own[-before:], 'zh', [(0, 1), (1, 0)])]
    all_to_all x2, blocking collectives: 28.5 us -> 30.3 us  [on_device(): lax.all_to_all(finished.reshape(owners, snaps, part, width), OWNERS, 0, 0...]
  transfers between devices with their start and end apart: 34 -> 34, of which waited for: 20 -> 20; matrix products, arithmetic and copies ran while one was open for 2% -> 3% of each run, Pallas kernels for 4% -> 4%
where the time goes in v5:
time: 173 us
  blocking collectives  64.2 us (37%)
  waiting for transfers between devices  46 us (27%)
  starting transfers between devices  38.9 us (22%)
  Pallas kernels  16.9 us (10%)
  other arithmetic  4.3 us (2%)
  local copies, waits for them, and re-layouts  2 us (1%)
    ppermute x12, waiting for transfers between devices, gather_line(): ahead[t] = lax.ppermute(ahead[t], LINE, forward)  34.4 us
    all_to_all x2, blocking collectives, on_device(): owned = lax.all_to_all(graph_out, OWNERS, 0, 0, tiled=True)  33.9 us
    all_to_all x2, blocking collectives, on_device(): lax.all_to_all(finished.reshape(owners, snaps, part, width), OWNERS, 0, 0...  30.3 us
    ppermute x12, starting transfers between devices, gather_line(): ahead[t] = lax.ppermute(ahead[t], LINE, forward)  19.7 us
    ppermute x2, starting transfers between devices, time_stage(): halo = lax.ppermute(own[-before:], 'zh', [(0, 1), (1, 0)])  11.4 us
    pallas_call x2, Pallas kernels, graph_stage(): pl.pallas_call(functools.partial(graph_kernel, layer, chips, layer > 0),...  7.71 us
    ppermute x12, waiting for transfers between devices, gather_line(): behind[t] = lax.ppermute(behind[t], LINE, backward)  7.66 us
    ppermute x12, starting transfers between devices, gather_line(): behind[t] = lax.ppermute(behind[t], LINE, backward)  7.23 us
  transfers between devices with their start and end apart: 34, of which 20 were waited for; matrix products, arithmetic and copies ran while one was open for 3% of the time, Pallas kernels for 4%

profile of v5, /device:TPU:32, one launch (start us, length us, event | category | flops | bytes accessed | tf_op | source)
XLA Modules:
  0.0 172.6 jit_solution(8701380939446085115)
XLA Ops:
  1.1 2.0 %collective-permute-start.1 = (bf16[16,64,128]{2,1,0:T(8,128)(2,1)S(1)}, bf16[16,64,128]{2,1,0:T(8,128)(2,1)S(1)}, u32[]{:S(2)}, u32[]{:S(2)}) collective-permute-start(bf16[16,64,128]{2,1,0:T(8,128)(2,1)S(1)} %bitcast.36), channel_id=1, source_target_pairs={{0,2},{2,4},{4,6},{3,1},{5,3},{7,5},{6,7},{1,0},{8,10},{10,12},{12... | collective-permute-start | bytes 786440 | tf_op jit(solution)/shard_map/ppermute | solution.py:240
  3.2 1.9 %collective-permute-start.2 = (bf16[16,64,128]{2,1,0:T(8,128)(2,1)S(1)}, bf16[16,64,128]{2,1,0:T(8,128)(2,1)S(1)}, u32[]{:S(2)}, u32[]{:S(2)}) collective-permute-start(bf16[16,64,128]{2,1,0:T(8,128)(2,1)S(1)} %bitcast.33), channel_id=1, source_target_pairs={{0,2},{2,4},{4,6},{3,1},{5,3},{7,5},{6,7},{1,0},{8,10},{10,12},{12... | collective-permute-start | bytes 786440 | tf_op jit(solution)/shard_map/ppermute | solution.py:240
  5.2 4.3 %copy_bitcast_fusion.refs_1_.refs_19_ = bf16[2,8,128,1024]{3,2,1,0:T(8,128)(2,1)S(1)} fusion(s32[2,8,8,128,128]{4,3,2,1,0:T(8,128)} %param.12), kind=kLoop, calls=%fused_computation | loop fusion | flops 2097152 | bytes 12582912 | tf_op jit(solution)/shard_map/reshape | solution.py:274
  10.2 2.0 %collective-permute-start.5 = (bf16[16,64,128]{2,1,0:T(8,128)(2,1)S(1)}, bf16[16,64,128]{2,1,0:T(8,128)(2,1)S(1)}, u32[]{:S(2)}, u32[]{:S(2)}) collective-permute-start(bf16[16,64,128]{2,1,0:T(8,128)(2,1)S(1)} %collective-permute-done.1.refs_0_.refs_4_), channel_id=1, source_target_pairs={{0,2},{2,4},{4,6},{3,1},{5,3},{7,5},{6,7},{1,0},{8,10},{10,12},{12... | collective-permute-start | bytes 786440 | tf_op jit(solution)/shard_map/ppermute | solution.py:240
  12.2 3.3 %collective-permute-done.2.refs_1_.refs_5_ = bf16[16,64,128]{2,1,0:T(8,128)(2,1)S(1)} collective-permute-done((bf16[16,64,128]{2,1,0:T(8,128)(2,1)S(1)}, bf16[16,64,128]{2,1,0:T(8,128)(2,1)S(1)}, u32[]{:S(2)}, u32[]{:S(2)}) %collective-permute-start.2) | collective-permute-done | bytes 262176 | tf_op jit(solution)/shard_map/ppermute | solution.py:240
  18.0 2.3 %collective-permute-done.5.refs_0_.refs_8_ = bf16[16,64,128]{2,1,0:T(8,128)(2,1)S(1)} collective-permute-done((bf16[16,64,128]{2,1,0:T(8,128)(2,1)S(1)}, bf16[16,64,128]{2,1,0:T(8,128)(2,1)S(1)}, u32[]{:S(2)}, u32[]{:S(2)}) %collective-permute-start.5) | collective-permute-done | bytes 262176 | tf_op jit(solution)/shard_map/ppermute | solution.py:240
  20.2 2.3 %collective-permute-start.9 = (bf16[16,64,128]{2,1,0:T(8,128)(2,1)S(1)}, bf16[16,64,128]{2,1,0:T(8,128)(2,1)S(1)}, u32[]{:S(2)}, u32[]{:S(2)}) collective-permute-start(bf16[16,64,128]{2,1,0:T(8,128)(2,1)S(1)} %collective-permute-done.5.refs_0_.refs_8_), channel_id=1, source_target_pairs={{0,2},{2,4},{4,6},{3,1},{5,3},{7,5},{6,7},{1,0},{8,10},{10,12},{12... | collective-permute-start | bytes 786440 | tf_op jit(solution)/shard_map/ppermute | solution.py:240
  22.5 3.4 %collective-permute-done.6.refs_1_.refs_9_ = bf16[16,64,128]{2,1,0:T(8,128)(2,1)S(1)} collective-permute-done((bf16[16,64,128]{2,1,0:T(8,128)(2,1)S(1)}, bf16[16,64,128]{2,1,0:T(8,128)(2,1)S(1)}, u32[]{:S(2)}, u32[]{:S(2)}) %collective-permute-start.6) | collective-permute-done | bytes 262176 | tf_op jit(solution)/shard_map/ppermute | solution.py:240
  25.9 2.3 %collective-permute-start.10 = (bf16[16,64,128]{2,1,0:T(8,128)(2,1)S(1)}, bf16[16,64,128]{2,1,0:T(8,128)(2,1)S(1)}, u32[]{:S(2)}, u32[]{:S(2)}) collective-permute-start(bf16[16,64,128]{2,1,0:T(8,128)(2,1)S(1)} %collective-permute-done.6.refs_1_.refs_9_), channel_id=1, source_target_pairs={{0,2},{2,4},{4,6},{3,1},{5,3},{7,5},{6,7},{1,0},{8,10},{10,12},{12... | collective-permute-start | bytes 786440 | tf_op jit(solution)/shard_map/ppermute | solution.py:240
  28.1 3.1 %collective-permute-done.8.refs_3_.refs_11_ = bf16[16,64,128]{2,1,0:T(8,128)(2,1)S(1)} collective-permute-done((bf16[16,64,128]{2,1,0:T(8,128)(2,1)S(1)}, bf16[16,64,128]{2,1,0:T(8,128)(2,1)S(1)}, u32[]{:S(2)}, u32[]{:S(2)}) %collective-permute-start.8) | collective-permute-done | bytes 262176 | tf_op jit(solution)/shard_map/ppermute | solution.py:241
  32.4 4.7 %collective-permute-done.10.refs_1_.refs_13_ = bf16[16,64,128]{2,1,0:T(8,128)(2,1)S(1)} collective-permute-done((bf16[16,64,128]{2,1,0:T(8,128)(2,1)S(1)}, bf16[16,64,128]{2,1,0:T(8,128)(2,1)S(1)}, u32[]{:S(2)}, u32[]{:S(2)}) %collective-permute-start.10) | collective-permute-done | bytes 262176 | tf_op jit(solution)/shard_map/ppermute | solution.py:240
  38.1 1.8 %collective-permute-done.15.refs_18_ = bf16[2,16,64,128]{3,2,1,0:T(8,128)(2,1)S(1)} collective-permute-done((bf16[2,16,64,128]{3,2,1,0:T(8,128)(2,1)S(1)}, bf16[2,16,64,128]{3,2,1,0:T(8,128)(2,1)S(1)}, u32[]{:S(2)}, u32[]{:S(2)}) %collective-permute-start.15) | collective-permute-done | bytes 524320 | tf_op jit(solution)/shard_map/ppermute | solution.py:234
  40.0 3.9 %graph.2 = bf16[16,2,64,128]{3,2,1,0:T(8,128)(2,1)S(1)} custom-call(s32[2,8,8]{2,1,0:T(8,128)S(1)} %copy-done.5, bf16[2,16,64,128]{3,2,1,0:T(8,128)(2,1)S(1)} %collective-permute-done.refs_4_.refs_1_, bf16[16,64,128]{2,1,0:T(8,128)(2,1)S(1)} %bitcast.38, bf16[16,64,128]{2,1,0:T(8,128)(2,1)S(1)} %bitcast.35, ...), custom_call_target="tpu_custom_call" | custom-call | tf_op jit(solution)/shard_map/graph/pallas_call | solution.py:99
  43.8 18.9 %all_to_all.20 = bf16[16,2,64,128]{3,2,1,0:T(8,128)(2,1)S(1)} all-to-all(bf16[16,2,64,128]{3,2,1,0:T(8,128)(2,1)S(1)} %graph.2), channel_id=1, replica_groups=mesh['zh'=2,'x'=4,'y'=4,'zl'=4,'co'=2] {'x','y'}, dimensions={0} | all-to-all | bytes 1048576 | tf_op jit(solution)/shard_map/all_to_all | solution.py:283
  62.7 6.0 %collective-permute-start.16 = (bf16[7,64,128]{2,1,0:T(8,128)(2,1)S(1)}, bf16[7,64,128]{2,1,0:T(8,128)(2,1)S(1)}, u32[]{:S(2)}, u32[]{:S(2)}) collective-permute-start(bf16[7,64,128]{2,1,0:T(8,128)(2,1)S(1)} %slice.26), channel_id=1, source_target_pairs={{0,128},{128,0},{1,129},{129,1},{2,130},{130,2},{3,131},{131,3},{4... | collective-permute-start | bytes 344072 | tf_op jit(solution)/shard_map/ppermute | solution.py:200
  68.7 3.3 %late.2.later = bf16[32,64,128]{2,1,0:T(8,128)(2,1)S(1)} custom-call(bf16[32,64,128]{2,1,0:T(8,128)(2,1)S(1)} %bitcast.26, f32[2,8,128]{2,1,0:T(8,128)S(1)} %copy-done.4, f32[2,1,128]{2,1,0:T(1,128)S(1)} %bitcast.39, bf16[2,128,1024]{2,1,0:T(8,128)(2,1)S(1)} %copy-done, bf16[2,1024,128]{2,1,0:T(8,128)(2,1)S(1)} %copy-done.1), custom_call_target="tpu_custom_call" | custom-call | tf_op jit(solution)/shard_map/late/pallas_call | solution.py:204
  73.3 15.1 %all_to_all.21 = bf16[16,2,64,128]{3,2,1,0:T(8,128)(2,1)S(1)} all-to-all(bf16[16,2,64,128]{3,2,1,0:T(8,128)(2,1)S(1)} %bitcast.31), channel_id=1, replica_groups=mesh['zh'=2,'x'=4,'y'=4,'zl'=4,'co'=2] {'x','y'}, dimensions={0} | all-to-all | bytes 1048576 | tf_op jit(solution)/shard_map/all_to_all | solution.py:286
  88.5 2.1 %collective-permute-start.18 = (bf16[16,64,128]{2,1,0:T(8,128)(2,1)S(1)}, bf16[16,64,128]{2,1,0:T(8,128)(2,1)S(1)}, u32[]{:S(2)}, u32[]{:S(2)}) collective-permute-start(bf16[16,64,128]{2,1,0:T(8,128)(2,1)S(1)} %get-tuple-element.6.refs_2_), channel_id=1, source_target_pairs={{0,2},{2,4},{4,6},{3,1},{5,3},{7,5},{6,7},{1,0},{8,10},{10,12},{12... | collective-permute-start | bytes 786440 | tf_op jit(solution)/shard_map/ppermute | solution.py:240
  90.6 1.9 %collective-permute-start.20 = (bf16[16,64,128]{2,1,0:T(8,128)(2,1)S(1)}, bf16[16,64,128]{2,1,0:T(8,128)(2,1)S(1)}, u32[]{:S(2)}, u32[]{:S(2)}) collective-permute-start(bf16[16,64,128]{2,1,0:T(8,128)(2,1)S(1)} %get-tuple-element.6.refs_2_), channel_id=1, source_target_pairs={{2,0},{4,2},{6,4},{1,3},{3,5},{5,7},{7,6},{0,1},{10,8},{12,10},{14... | collective-permute-start | bytes 786440 | tf_op jit(solution)/shard_map/ppermute | solution.py:241
  92.6 5.1 %collective-permute-done.18.refs_0_.refs_4_ = bf16[16,64,128]{2,1,0:T(8,128)(2,1)S(1)} collective-permute-done((bf16[16,64,128]{2,1,0:T(8,128)(2,1)S(1)}, bf16[16,64,128]{2,1,0:T(8,128)(2,1)S(1)}, u32[]{:S(2)}, u32[]{:S(2)}) %collective-permute-start.18) | collective-permute-done | bytes 262176 | tf_op jit(solution)/shard_map/ppermute | solution.py:240
  97.7 2.0 %collective-permute-start.22 = (bf16[16,64,128]{2,1,0:T(8,128)(2,1)S(1)}, bf16[16,64,128]{2,1,0:T(8,128)(2,1)S(1)}, u32[]{:S(2)}, u32[]{:S(2)}) collective-permute-start(bf16[16,64,128]{2,1,0:T(8,128)(2,1)S(1)} %collective-permute-done.18.refs_0_.refs_4_), channel_id=1, source_target_pairs={{0,2},{2,4},{4,6},{3,1},{5,3},{7,5},{6,7},{1,0},{8,10},{10,12},{12... | collective-permute-start | bytes 786440 | tf_op jit(solution)/shard_map/ppermute | solution.py:240
  99.7 3.4 %collective-permute-done.19.refs_1_.refs_5_ = bf16[16,64,128]{2,1,0:T(8,128)(2,1)S(1)} collective-permute-done((bf16[16,64,128]{2,1,0:T(8,128)(2,1)S(1)}, bf16[16,64,128]{2,1,0:T(8,128)(2,1)S(1)}, u32[]{:S(2)}, u32[]{:S(2)}) %collective-permute-start.19) | collective-permute-done | bytes 262176 | tf_op jit(solution)/shard_map/ppermute | solution.py:240
  103.2 1.9 %collective-permute-start.23 = (bf16[16,64,128]{2,1,0:T(8,128)(2,1)S(1)}, bf16[16,64,128]{2,1,0:T(8,128)(2,1)S(1)}, u32[]{:S(2)}, u32[]{:S(2)}) collective-permute-start(bf16[16,64,128]{2,1,0:T(8,128)(2,1)S(1)} %collective-permute-done.19.refs_1_.refs_5_), channel_id=1, source_target_pairs={{0,2},{2,4},{4,6},{3,1},{5,3},{7,5},{6,7},{1,0},{8,10},{10,12},{12... | collective-permute-start | bytes 786440 | tf_op jit(solution)/shard_map/ppermute | solution.py:240
  105.5 1.9 %collective-permute-start.25 = (bf16[16,64,128]{2,1,0:T(8,128)(2,1)S(1)}, bf16[16,64,128]{2,1,0:T(8,128)(2,1)S(1)}, u32[]{:S(2)}, u32[]{:S(2)}) collective-permute-start(bf16[16,64,128]{2,1,0:T(8,128)(2,1)S(1)} %collective-permute-done.21.refs_3_.refs_7_), channel_id=1, source_target_pairs={{2,0},{4,2},{6,4},{1,3},{3,5},{5,7},{7,6},{0,1},{10,8},{12,10},{14... | collective-permute-start | bytes 786440 | tf_op jit(solution)/shard_map/ppermute | solution.py:241
  108.7 4.7 %collective-permute-done.23.refs_1_.refs_9_ = bf16[16,64,128]{2,1,0:T(8,128)(2,1)S(1)} collective-permute-done((bf16[16,64,128]{2,1,0:T(8,128)(2,1)S(1)}, bf16[16,64,128]{2,1,0:T(8,128)(2,1)S(1)}, u32[]{:S(2)}, u32[]{:S(2)}) %collective-permute-start.23) | collective-permute-done | bytes 262176 | tf_op jit(solution)/shard_map/ppermute | solution.py:240
  115.4 2.5 %collective-permute-done.25.refs_3_.refs_11_ = bf16[16,64,128]{2,1,0:T(8,128)(2,1)S(1)} collective-permute-done((bf16[16,64,128]{2,1,0:T(8,128)(2,1)S(1)}, bf16[16,64,128]{2,1,0:T(8,128)(2,1)S(1)}, u32[]{:S(2)}, u32[]{:S(2)}) %collective-permute-start.25) | collective-permute-done | bytes 262176 | tf_op jit(solution)/shard_map/ppermute | solution.py:241
  119.0 5.6 %collective-permute-done.27.refs_1_.refs_13_ = bf16[16,64,128]{2,1,0:T(8,128)(2,1)S(1)} collective-permute-done((bf16[16,64,128]{2,1,0:T(8,128)(2,1)S(1)}, bf16[16,64,128]{2,1,0:T(8,128)(2,1)S(1)}, u32[]{:S(2)}, u32[]{:S(2)}) %collective-permute-start.27) | collective-permute-done | bytes 262176 | tf_op jit(solution)/shard_map/ppermute | solution.py:240
  127.6 3.8 %graph.3 = bf16[16,2,64,128]{3,2,1,0:T(8,128)(2,1)S(1)} custom-call(s32[2,8,8]{2,1,0:T(8,128)S(1)} %copy-done.5, bf16[16,2,64,128]{3,2,1,0:T(8,128)(2,1)S(1)} %collective-permute-done.17.refs_4_.refs_1_, bf16[16,64,128]{2,1,0:T(8,128)(2,1)S(1)} %get-tuple-element.6.refs_2_, bf16[16,64,128]{2,1,0:T(8,128)(2,1)S(1)} %get-tuple-element.5.refs_3_, ...), custom_call_target="tpu_custom_call" | custom-call | tf_op jit(solution)/shard_map/graph/pallas_call | solution.py:99
  131.5 15.0 %all_to_all.22 = bf16[16,2,64,128]{3,2,1,0:T(8,128)(2,1)S(1)} all-to-all(bf16[16,2,64,128]{3,2,1,0:T(8,128)(2,1)S(1)} %graph.3), channel_id=1, replica_groups=mesh['zh'=2,'x'=4,'y'=4,'zl'=4,'co'=2] {'x','y'}, dimensions={0} | all-to-all | bytes 1048576 | tf_op jit(solution)/shard_map/all_to_all | solution.py:283
  146.6 5.4 %collective-permute-start.33 = (bf16[7,64,128]{2,1,0:T(8,128)(2,1)S(1)}, bf16[7,64,128]{2,1,0:T(8,128)(2,1)S(1)}, u32[]{:S(2)}, u32[]{:S(2)}) collective-permute-start(bf16[7,64,128]{2,1,0:T(8,128)(2,1)S(1)} %slice.29), channel_id=1, source_target_pairs={{0,128},{128,0},{1,129},{129,1},{2,130},{130,2},{3,131},{131,3},{4... | collective-permute-start | bytes 344072 | tf_op jit(solution)/shard_map/ppermute | solution.py:200
  151.9 3.3 %late.3.later = bf16[32,64,128]{2,1,0:T(8,128)(2,1)S(1)} custom-call(bf16[32,64,128]{2,1,0:T(8,128)(2,1)S(1)} %bitcast.29, f32[2,8,128]{2,1,0:T(8,128)S(1)} %copy-done.4, f32[2,1,128]{2,1,0:T(1,128)S(1)} %bitcast.41, bf16[2,128,1024]{2,1,0:T(8,128)(2,1)S(1)} %copy-done, bf16[2,1024,128]{2,1,0:T(8,128)(2,1)S(1)} %copy-done.1), custom_call_target="tpu_custom_call" | custom-call | tf_op jit(solution)/shard_map/late/pallas_call | solution.py:204
  156.5 15.2 %all_to_all.23 = bf16[16,2,64,128]{3,2,1,0:T(8,128)(2,1)S(1)} all-to-all(bf16[16,2,64,128]{3,2,1,0:T(8,128)(2,1)S(1)} %bitcast.32), channel_id=1, replica_groups=mesh['zh'=2,'x'=4,'y'=4,'zl'=4,'co'=2] {'x','y'}, dimensions={0} | all-to-all | bytes 1048576 | tf_op jit(solution)/shard_map/all_to_all | solution.py:286
  (75 shorter events, 17.9 us)
Async XLA Ops:
  1.1 9.2 %collective-permute-start.1 = (bf16[16,64,128]{2,1,0:T(8,128)(2,1)S(1)}, bf16[16,64,128]{2,1,0:T(8,128)(2,1)S(1)}, u32[]{:S(2)}, u32[]{:S(2)}) collective-permute-start(bf16[16,64,128]{2,1,0:T(8,128)(2,1)S(1)} %bitcast.36), channel_id=1, source_target_pairs={{0,2},{2,4},{4,6},{3,1},{5,3},{7,5},{6,7},{1,0},{8,10},{10,12},{12... | collective-permute-start | bytes 786440 | tf_op jit(solution)/shard_map/ppermute | solution.py:240
  3.1 13.8 %collective-permute-start.3 = (bf16[16,64,128]{2,1,0:T(8,128)(2,1)S(1)}, bf16[16,64,128]{2,1,0:T(8,128)(2,1)S(1)}, u32[]{:S(2)}, u32[]{:S(2)}) collective-permute-start(bf16[16,64,128]{2,1,0:T(8,128)(2,1)S(1)} %bitcast.37), channel_id=1, source_target_pairs={{2,0},{4,2},{6,4},{1,3},{3,5},{5,7},{7,6},{0,1},{10,8},{12,10},{14... | collective-permute-start | bytes 786440 | tf_op jit(solution)/shard_map/ppermute | solution.py:241
  3.2 12.4 %collective-permute-start.2 = (bf16[16,64,128]{2,1,0:T(8,128)(2,1)S(1)}, bf16[16,64,128]{2,1,0:T(8,128)(2,1)S(1)}, u32[]{:S(2)}, u32[]{:S(2)}) collective-permute-start(bf16[16,64,128]{2,1,0:T(8,128)(2,1)S(1)} %bitcast.33), channel_id=1, source_target_pairs={{0,2},{2,4},{4,6},{3,1},{5,3},{7,5},{6,7},{1,0},{8,10},{10,12},{12... | collective-permute-start | bytes 786440 | tf_op jit(solution)/shard_map/ppermute | solution.py:240
  5.1 12.5 %collective-permute-start.4 = (bf16[16,64,128]{2,1,0:T(8,128)(2,1)S(1)}, bf16[16,64,128]{2,1,0:T(8,128)(2,1)S(1)}, u32[]{:S(2)}, u32[]{:S(2)}) collective-permute-start(bf16[16,64,128]{2,1,0:T(8,128)(2,1)S(1)} %bitcast.34), channel_id=1, source_target_pairs={{2,0},{4,2},{6,4},{1,3},{3,5},{5,7},{7,6},{0,1},{10,8},{12,10},{14... | collective-permute-start | bytes 786440 | tf_op jit(solution)/shard_map/ppermute | solution.py:241
  5.2 12.5 %collective-permute-start = (bf16[2,16,64,128]{3,2,1,0:T(8,128)(2,1)}, bf16[2,16,64,128]{3,2,1,0:T(8,128)(2,1)S(1)}, u32[]{:S(2)}, u32[]{:S(2)}) collective-permute-start(bf16[2,16,64,128]{3,2,1,0:T(8,128)(2,1)} %bitcast.46), channel_id=1, source_target_pairs={{0,1},{1,0},{2,3},{3,2},{4,5},{5,4},{6,7},{7,6},{8,9},{9,8},{10,11... | collective-permute-start | bytes 1572872 | tf_op jit(solution)/shard_map/ppermute | solution.py:234
  10.2 10.0 %collective-permute-start.5 = (bf16[16,64,128]{2,1,0:T(8,128)(2,1)S(1)}, bf16[16,64,128]{2,1,0:T(8,128)(2,1)S(1)}, u32[]{:S(2)}, u32[]{:S(2)}) collective-permute-start(bf16[16,64,128]{2,1,0:T(8,128)(2,1)S(1)} %collective-permute-done.1.refs_0_.refs_4_), channel_id=1, source_target_pairs={{0,2},{2,4},{4,6},{3,1},{5,3},{7,5},{6,7},{1,0},{8,10},{10,12},{12... | collective-permute-start | bytes 786440 | tf_op jit(solution)/shard_map/ppermute | solution.py:240
  15.6 10.3 %collective-permute-start.6 = (bf16[16,64,128]{2,1,0:T(8,128)(2,1)S(1)}, bf16[16,64,128]{2,1,0:T(8,128)(2,1)S(1)}, u32[]{:S(2)}, u32[]{:S(2)}) collective-permute-start(bf16[16,64,128]{2,1,0:T(8,128)(2,1)S(1)} %collective-permute-done.2.refs_1_.refs_5_), channel_id=1, source_target_pairs={{0,2},{2,4},{4,6},{3,1},{5,3},{7,5},{6,7},{1,0},{8,10},{10,12},{12... | collective-permute-start | bytes 786440 | tf_op jit(solution)/shard_map/ppermute | solution.py:240
  16.9 11.2 %collective-permute-start.7 = (bf16[16,64,128]{2,1,0:T(8,128)(2,1)S(1)}, bf16[16,64,128]{2,1,0:T(8,128)(2,1)S(1)}, u32[]{:S(2)}, u32[]{:S(2)}) collective-permute-start(bf16[16,64,128]{2,1,0:T(8,128)(2,1)S(1)} %collective-permute-done.3.refs_2_.refs_6_), channel_id=1, source_target_pairs={{2,0},{4,2},{6,4},{1,3},{3,5},{5,7},{7,6},{0,1},{10,8},{12,10},{14... | collective-permute-start | bytes 786440 | tf_op jit(solution)/shard_map/ppermute | solution.py:241
  17.6 13.6 %collective-permute-start.8 = (bf16[16,64,128]{2,1,0:T(8,128)(2,1)S(1)}, bf16[16,64,128]{2,1,0:T(8,128)(2,1)S(1)}, u32[]{:S(2)}, u32[]{:S(2)}) collective-permute-start(bf16[16,64,128]{2,1,0:T(8,128)(2,1)S(1)} %collective-permute-done.4.refs_3_.refs_7_), channel_id=1, source_target_pairs={{2,0},{4,2},{6,4},{1,3},{3,5},{5,7},{7,6},{0,1},{10,8},{12,10},{14... | collective-permute-start | bytes 786440 | tf_op jit(solution)/shard_map/ppermute | solution.py:241
  17.9 22.0 %collective-permute-start.13 = (bf16[4,16,64,128]{3,2,1,0:T(8,128)(2,1)S(1)}, bf16[4,16,64,128]{3,2,1,0:T(8,128)(2,1)S(1)}, u32[]{:S(2)}, u32[]{:S(2)}) collective-permute-start(bf16[4,16,64,128]{3,2,1,0:T(8,128)(2,1)S(1)} %tie.1), channel_id=1, source_target_pairs={{0,1},{1,0},{2,3},{3,2},{4,5},{5,4},{6,7},{7,6},{8,9},{9,8},{10,11... | collective-permute-start | bytes 3145736 | tf_op jit(solution)/shard_map/ppermute | solution.py:234
  20.2 12.1 %collective-permute-start.9 = (bf16[16,64,128]{2,1,0:T(8,128)(2,1)S(1)}, bf16[16,64,128]{2,1,0:T(8,128)(2,1)S(1)}, u32[]{:S(2)}, u32[]{:S(2)}) collective-permute-start(bf16[16,64,128]{2,1,0:T(8,128)(2,1)S(1)} %collective-permute-done.5.refs_0_.refs_8_), channel_id=1, source_target_pairs={{0,2},{2,4},{4,6},{3,1},{5,3},{7,5},{6,7},{1,0},{8,10},{10,12},{12... | collective-permute-start | bytes 786440 | tf_op jit(solution)/shard_map/ppermute | solution.py:240
  25.9 11.2 %collective-permute-start.10 = (bf16[16,64,128]{2,1,0:T(8,128)(2,1)S(1)}, bf16[16,64,128]{2,1,0:T(8,128)(2,1)S(1)}, u32[]{:S(2)}, u32[]{:S(2)}) collective-permute-start(bf16[16,64,128]{2,1,0:T(8,128)(2,1)S(1)} %collective-permute-done.6.refs_1_.refs_9_), channel_id=1, source_target_pairs={{0,2},{2,4},{4,6},{3,1},{5,3},{7,5},{6,7},{1,0},{8,10},{10,12},{12... | collective-permute-start | bytes 786440 | tf_op jit(solution)/shard_map/ppermute | solution.py:240
  28.1 9.0 %collective-permute-start.11 = (bf16[16,64,128]{2,1,0:T(8,128)(2,1)S(1)}, bf16[16,64,128]{2,1,0:T(8,128)(2,1)S(1)}, u32[]{:S(2)}, u32[]{:S(2)}) collective-permute-start(bf16[16,64,128]{2,1,0:T(8,128)(2,1)S(1)} %collective-permute-done.7.refs_2_.refs_10_), channel_id=1, source_target_pairs={{2,0},{4,2},{6,4},{1,3},{3,5},{5,7},{7,6},{0,1},{10,8},{12,10},{14... | collective-permute-start | bytes 786440 | tf_op jit(solution)/shard_map/ppermute | solution.py:241
  31.2 6.6 %collective-permute-start.12 = (bf16[16,64,128]{2,1,0:T(8,128)(2,1)S(1)}, bf16[16,64,128]{2,1,0:T(8,128)(2,1)S(1)}, u32[]{:S(2)}, u32[]{:S(2)}) collective-permute-start(bf16[16,64,128]{2,1,0:T(8,128)(2,1)S(1)} %collective-permute-done.8.refs_3_.refs_11_), channel_id=1, source_target_pairs={{2,0},{4,2},{6,4},{1,3},{3,5},{5,7},{7,6},{0,1},{10,8},{12,10},{14... | collective-permute-start | bytes 786440 | tf_op jit(solution)/shard_map/ppermute | solution.py:241
  32.3 5.8 %collective-permute-start.14 = (bf16[2,16,64,128]{3,2,1,0:T(8,128)(2,1)S(1)}, bf16[2,16,64,128]{3,2,1,0:T(8,128)(2,1)S(1)}, u32[]{:S(2)}, u32[]{:S(2)}) collective-permute-start(bf16[2,16,64,128]{3,2,1,0:T(8,128)(2,1)S(1)} %join.7), channel_id=1, source_target_pairs={{0,1},{1,0},{2,3},{3,2},{4,5},{5,4},{6,7},{7,6},{8,9},{9,8},{10,11... | collective-permute-start | bytes 1572872 | tf_op jit(solution)/shard_map/ppermute | solution.py:234
  62.7 9.5 %collective-permute-start.16 = (bf16[7,64,128]{2,1,0:T(8,128)(2,1)S(1)}, bf16[7,64,128]{2,1,0:T(8,128)(2,1)S(1)}, u32[]{:S(2)}, u32[]{:S(2)}) collective-permute-start(bf16[7,64,128]{2,1,0:T(8,128)(2,1)S(1)} %slice.26), channel_id=1, source_target_pairs={{0,128},{128,0},{1,129},{129,1},{2,130},{130,2},{3,131},{131,3},{4... | collective-permute-start | bytes 344072 | tf_op jit(solution)/shard_map/ppermute | solution.py:200
  88.4 19.0 %collective-permute-start.17 = (bf16[16,2,64,128]{3,2,1,0:T(8,128)(2,1)S(1)}, bf16[16,2,64,128]{3,2,1,0:T(8,128)(2,1)S(1)}, u32[]{:S(2)}, u32[]{:S(2)}) collective-permute-start(bf16[16,2,64,128]{3,2,1,0:T(8,128)(2,1)S(1)} %all_to_all.21), channel_id=1, source_target_pairs={{0,1},{1,0},{2,3},{3,2},{4,5},{5,4},{6,7},{7,6},{8,9},{9,8},{10,11... | collective-permute-start | bytes 1572872 | tf_op jit(solution)/shard_map/ppermute | solution.py:234
  88.5 9.3 %collective-permute-start.18 = (bf16[16,64,128]{2,1,0:T(8,128)(2,1)S(1)}, bf16[16,64,128]{2,1,0:T(8,128)(2,1)S(1)}, u32[]{:S(2)}, u32[]{:S(2)}) collective-permute-start(bf16[16,64,128]{2,1,0:T(8,128)(2,1)S(1)} %get-tuple-element.6.refs_2_), channel_id=1, source_target_pairs={{0,2},{2,4},{4,6},{3,1},{5,3},{7,5},{6,7},{1,0},{8,10},{10,12},{12... | collective-permute-start | bytes 786440 | tf_op jit(solution)/shard_map/ppermute | solution.py:240
  90.5 12.6 %collective-permute-start.19 = (bf16[16,64,128]{2,1,0:T(8,128)(2,1)S(1)}, bf16[16,64,128]{2,1,0:T(8,128)(2,1)S(1)}, u32[]{:S(2)}, u32[]{:S(2)}) collective-permute-start(bf16[16,64,128]{2,1,0:T(8,128)(2,1)S(1)} %get-tuple-element.5.refs_3_), channel_id=1, source_target_pairs={{0,2},{2,4},{4,6},{3,1},{5,3},{7,5},{6,7},{1,0},{8,10},{10,12},{12... | collective-permute-start | bytes 786440 | tf_op jit(solution)/shard_map/ppermute | solution.py:240
  90.6 14.4 %collective-permute-start.20 = (bf16[16,64,128]{2,1,0:T(8,128)(2,1)S(1)}, bf16[16,64,128]{2,1,0:T(8,128)(2,1)S(1)}, u32[]{:S(2)}, u32[]{:S(2)}) collective-permute-start(bf16[16,64,128]{2,1,0:T(8,128)(2,1)S(1)} %get-tuple-element.6.refs_2_), channel_id=1, source_target_pairs={{2,0},{4,2},{6,4},{1,3},{3,5},{5,7},{7,6},{0,1},{10,8},{12,10},{14... | collective-permute-start | bytes 786440 | tf_op jit(solution)/shard_map/ppermute | solution.py:241
  92.6 12.9 %collective-permute-start.21 = (bf16[16,64,128]{2,1,0:T(8,128)(2,1)S(1)}, bf16[16,64,128]{2,1,0:T(8,128)(2,1)S(1)}, u32[]{:S(2)}, u32[]{:S(2)}) collective-permute-start(bf16[16,64,128]{2,1,0:T(8,128)(2,1)S(1)} %get-tuple-element.5.refs_3_), channel_id=1, source_target_pairs={{2,0},{4,2},{6,4},{1,3},{3,5},{5,7},{7,6},{0,1},{10,8},{12,10},{14... | collective-permute-start | bytes 786440 | tf_op jit(solution)/shard_map/ppermute | solution.py:241
  97.7 10.1 %collective-permute-start.22 = (bf16[16,64,128]{2,1,0:T(8,128)(2,1)S(1)}, bf16[16,64,128]{2,1,0:T(8,128)(2,1)S(1)}, u32[]{:S(2)}, u32[]{:S(2)}) collective-permute-start(bf16[16,64,128]{2,1,0:T(8,128)(2,1)S(1)} %collective-permute-done.18.refs_0_.refs_4_), channel_id=1, source_target_pairs={{0,2},{2,4},{4,6},{3,1},{5,3},{7,5},{6,7},{1,0},{8,10},{10,12},{12... | collective-permute-start | bytes 786440 | tf_op jit(solution)/shard_map/ppermute | solution.py:240
  103.2 10.3 %collective-permute-start.23 = (bf16[16,64,128]{2,1,0:T(8,128)(2,1)S(1)}, bf16[16,64,128]{2,1,0:T(8,128)(2,1)S(1)}, u32[]{:S(2)}, u32[]{:S(2)}) collective-permute-start(bf16[16,64,128]{2,1,0:T(8,128)(2,1)S(1)} %collective-permute-done.19.refs_1_.refs_5_), channel_id=1, source_target_pairs={{0,2},{2,4},{4,6},{3,1},{5,3},{7,5},{6,7},{1,0},{8,10},{10,12},{12... | collective-permute-start | bytes 786440 | tf_op jit(solution)/shard_map/ppermute | solution.py:240
  105.1 9.3 %collective-permute-start.24 = (bf16[16,64,128]{2,1,0:T(8,128)(2,1)S(1)}, bf16[16,64,128]{2,1,0:T(8,128)(2,1)S(1)}, u32[]{:S(2)}, u32[]{:S(2)}) collective-permute-start(bf16[16,64,128]{2,1,0:T(8,128)(2,1)S(1)} %collective-permute-done.20.refs_2_.refs_6_), channel_id=1, source_target_pairs={{2,0},{4,2},{6,4},{1,3},{3,5},{5,7},{7,6},{0,1},{10,8},{12,10},{14... | collective-permute-start | bytes 786440 | tf_op jit(solution)/shard_map/ppermute | solution.py:241
  105.5 12.5 %collective-permute-start.25 = (bf16[16,64,128]{2,1,0:T(8,128)(2,1)S(1)}, bf16[16,64,128]{2,1,0:T(8,128)(2,1)S(1)}, u32[]{:S(2)}, u32[]{:S(2)}) collective-permute-start(bf16[16,64,128]{2,1,0:T(8,128)(2,1)S(1)} %collective-permute-done.21.refs_3_.refs_7_), channel_id=1, source_target_pairs={{2,0},{4,2},{6,4},{1,3},{3,5},{5,7},{7,6},{0,1},{10,8},{12,10},{14... | collective-permute-start | bytes 786440 | tf_op jit(solution)/shard_map/ppermute | solution.py:241
  107.5 20.1 %collective-permute-start.30 = (bf16[4,16,64,128]{3,2,1,0:T(8,128)(2,1)S(1)}, bf16[4,16,64,128]{3,2,1,0:T(8,128)(2,1)S(1)}, u32[]{:S(2)}, u32[]{:S(2)}) collective-permute-start(bf16[4,16,64,128]{3,2,1,0:T(8,128)(2,1)S(1)} %join.9), channel_id=1, source_target_pairs={{0,1},{1,0},{2,3},{3,2},{4,5},{5,4},{6,7},{7,6},{8,9},{9,8},{10,11... | collective-permute-start | bytes 3145736 | tf_op jit(solution)/shard_map/ppermute | solution.py:234
  107.8 11.2 %collective-permute-start.26 = (bf16[16,64,128]{2,1,0:T(8,128)(2,1)S(1)}, bf16[16,64,128]{2,1,0:T(8,128)(2,1)S(1)}, u32[]{:S(2)}, u32[]{:S(2)}) collective-permute-start(bf16[16,64,128]{2,1,0:T(8,128)(2,1)S(1)} %collective-permute-done.22.refs_0_.refs_8_), channel_id=1, source_target_pairs={{0,2},{2,4},{4,6},{3,1},{5,3},{7,5},{6,7},{1,0},{8,10},{10,12},{12... | collective-permute-start | bytes 786440 | tf_op jit(solution)/shard_map/ppermute | solution.py:240
  113.4 11.2 %collective-permute-start.27 = (bf16[16,64,128]{2,1,0:T(8,128)(2,1)S(1)}, bf16[16,64,128]{2,1,0:T(8,128)(2,1)S(1)}, u32[]{:S(2)}, u32[]{:S(2)}) collective-permute-start(bf16[16,64,128]{2,1,0:T(8,128)(2,1)S(1)} %collective-permute-done.23.refs_1_.refs_9_), channel_id=1, source_target_pairs={{0,2},{2,4},{4,6},{3,1},{5,3},{7,5},{6,7},{1,0},{8,10},{10,12},{12... | collective-permute-start | bytes 786440 | tf_op jit(solution)/shard_map/ppermute | solution.py:240
  114.3 10.3 %collective-permute-start.28 = (bf16[16,64,128]{2,1,0:T(8,128)(2,1)S(1)}, bf16[16,64,128]{2,1,0:T(8,128)(2,1)S(1)}, u32[]{:S(2)}, u32[]{:S(2)}) collective-permute-start(bf16[16,64,128]{2,1,0:T(8,128)(2,1)S(1)} %collective-permute-done.24.refs_2_.refs_10_), channel_id=1, source_target_pairs={{2,0},{4,2},{6,4},{1,3},{3,5},{5,7},{7,6},{0,1},{10,8},{12,10},{14... | collective-permute-start | bytes 786440 | tf_op jit(solution)/shard_map/ppermute | solution.py:241
  118.0 7.6 %collective-permute-start.29 = (bf16[16,64,128]{2,1,0:T(8,128)(2,1)S(1)}, bf16[16,64,128]{2,1,0:T(8,128)(2,1)S(1)}, u32[]{:S(2)}, u32[]{:S(2)}) collective-permute-start(bf16[16,64,128]{2,1,0:T(8,128)(2,1)S(1)} %collective-permute-done.25.refs_3_.refs_11_), channel_id=1, source_target_pairs={{2,0},{4,2},{6,4},{1,3},{3,5},{5,7},{7,6},{0,1},{10,8},{12,10},{14... | collective-permute-start | bytes 786440 | tf_op jit(solution)/shard_map/ppermute | solution.py:241
  119.0 6.8 %collective-permute-start.31 = (bf16[2,16,64,128]{3,2,1,0:T(8,128)(2,1)S(1)}, bf16[2,16,64,128]{3,2,1,0:T(8,128)(2,1)S(1)}, u32[]{:S(2)}, u32[]{:S(2)}) collective-permute-start(bf16[2,16,64,128]{3,2,1,0:T(8,128)(2,1)S(1)} %join.10), channel_id=1, source_target_pairs={{0,1},{1,0},{2,3},{3,2},{4,5},{5,4},{6,7},{7,6},{8,9},{9,8},{10,11... | collective-permute-start | bytes 1572872 | tf_op jit(solution)/shard_map/ppermute | solution.py:234
  146.6 8.9 %collective-permute-start.33 = (bf16[7,64,128]{2,1,0:T(8,128)(2,1)S(1)}, bf16[7,64,128]{2,1,0:T(8,128)(2,1)S(1)}, u32[]{:S(2)}, u32[]{:S(2)}) collective-permute-start(bf16[7,64,128]{2,1,0:T(8,128)(2,1)S(1)} %slice.29), channel_id=1, source_target_pairs={{0,128},{128,0},{1,129},{129,1},{2,130},{130,2},{3,131},{131,3},{4... | collective-permute-start | bytes 344072 | tf_op jit(solution)/shard_map/ppermute | solution.py:200
  (10 other events, 207.4 us)
